TPU v7x, 512 devices: a whole 4x4x16 slice. The times are simulated.
512 devices in a mesh: ka: 128 (over z_lo, y, x, core), pb: 4 (over z_hi).
Axes of the slice: x: 4, y: 4, z: 16 (z_hi: 4, z_lo: 4; z = z_hi * 4 + z_lo), core: 2. Of those that a mesh axis runs over, the one named last changes fastest.
Arguments:
- coupling: float32 [256, 16, 2, 64, 128], P('ka', 'pb'), may hold values from -6 to 6
- gauge: float32 [256, 64, 128], P('ka'), may hold values from -0.5 to 0.5
- kq_index: int32 [16, 256], P(None, 'ka'), may hold values from 0 to 255, as said below
- fine_coords: int32 [3, 256], replicated, may hold values from 0 to 31
- eig_right: float32 [256, 64, 128], P('ka'), may hold values from -0.5 to 0.5
- eig_left: float32 [256, 16, 64, 128], P('ka', 'pb'), may hold values from -0.5 to 0.5
- energy_k: float32 [256, 64], P('ka'), may hold values from -4 to 4
- energy_kq: float32 [256, 16, 64], P('ka', 'pb'), may hold values from -4 to 4
- occupied: int32 [256, 16, 64], P('ka', 'pb'), may hold values 0 or 1
- frequency: float32 [16, 2], P('pb'), may hold values from 0.02 to 0.12
Outputs:
- self_energy: float32 [256, 64], P('ka')
Inputs may be any that keep to these rules, and one draw needn't show every extreme that they name: kq_index[q, k] is the number of the coarse point k displaced by the q-th window point's offset on the periodic 8 x 8 x 4 grid; for each q it is a permutation of the coarse points. Among the offsets are (4, 0, 0) and (0, 0, 3).
All inputs are finite; a program needn't handle non-finite values. No bound on the sum of `occupied` on one device may be relied on, other than what follows from the above.
Results may differ from a plain program's by a relative error of at most 0.0001.
Values sent between devices are 32-bit elements; how exact they have to be, the bound alone decides.
No kernel may reach another device: no remote copies, remote signals or barrier semaphores. Data moves between devices by JAX's collectives and lax.ppermute only.
A program may use at most 64 MiB of HBM per device.

v0:
```python
import math

import jax
import jax.numpy as jnp
from jax import lax
from jax.sharding import Mesh
from jax.sharding import PartitionSpec as P

GX = 8
GY = 8
GZ = 4
FG = 32
NK = 256
KA = ("ka_0", "ka_1", "ka_2", "ka_3")


PRECISE = lax.Precision.HIGHEST
BROADEN = 0.1
THERMAL = 0.05


def sent_to_all(x, axis):
    devices = lax.axis_size(axis)
    return lax.all_to_all(jnp.broadcast_to(x[None], (devices, *x.shape)), axis, 0, 0, tiled=True)


def joined_along(parts, dim):
    parts = jnp.moveaxis(parts, 0, dim)
    lengths = parts.shape
    return parts.reshape(*lengths[:dim], lengths[dim] * lengths[dim + 1], *lengths[dim + 2 :])


def gather_axes(x, axes, dim):
    far, near = axes
    first = sent_to_all(x, far)
    parts = jnp.swapaxes(sent_to_all(first, near), 0, 1)
    return joined_along(parts.reshape(-1, *x.shape), dim)


def taken_together(x, axis):
    return sent_to_all(x, axis).sum(axis=0)


def product(left_matrix, right_matrix):
    return jnp.dot(left_matrix, right_matrix, precision=PRECISE, preferred_element_type=jnp.float32)


def mult(pattern, first, second):
    return jnp.einsum(pattern, first, second, precision=PRECISE)


def phase_tables(fine_coords):
    points = jnp.arange(NK, dtype=jnp.int32)
    along_first = points // (GY * GZ)
    along_second = points // GZ % GY
    along_third = points % GZ
    cell_first = along_first - GX // 2
    cell_second = along_second - GY // 2
    cell_third = along_third - GZ // 2
    coarse_index = (
        cell_first[:, None] * along_first[None, :] * (GY * GZ)
        + cell_second[:, None] * along_second[None, :] * (GX * GZ)
        + cell_third[:, None] * along_third[None, :] * (GX * GY)
    ) % NK
    coarse_angles = coarse_index.astype(jnp.float32) * (2.0 * math.pi / NK)
    fine_index = (
        fine_coords[0][:, None] * cell_first[None, :]
        + fine_coords[1][:, None] * cell_second[None, :]
        + fine_coords[2][:, None] * cell_third[None, :]
    ) % FG
    fine_angles = fine_index.astype(jnp.float32) * (2.0 * math.pi / FG)
    return (
        jnp.cos(coarse_angles) / NK,
        -jnp.sin(coarse_angles) / NK,
        jnp.cos(fine_angles),
        jnp.sin(fine_angles),
    )


def right_block(matrix):
    orbitals = matrix.shape[-2]
    real_part = matrix[..., :orbitals]
    imag_part = matrix[..., orbitals:]
    upper_half = jnp.concatenate([real_part, imag_part], -1)
    lower_half = jnp.concatenate([-imag_part, real_part], -1)
    return jnp.concatenate([upper_half, lower_half], -2)


def sectioned(cols_real, cols_imag, tables):
    coarse_real, coarse_imag, fine_cos, fine_sin = tables
    space_real = product(coarse_real, cols_real) - product(coarse_imag, cols_imag)
    space_imag = product(coarse_real, cols_imag) + product(coarse_imag, cols_real)
    fine_real_part = product(fine_cos, space_real) - product(fine_sin, space_imag)
    fine_imag_part = product(fine_cos, space_imag) + product(fine_sin, space_real)
    return (fine_real_part, fine_imag_part)


def self_terms(strength, energy_k, energy_kq, occupied, frequency):
    phonon = frequency[None, :, :, None, None]
    bose_factor = 1.0 / (jnp.exp(phonon / THERMAL) - 1.0)
    filled = occupied.astype(jnp.float32)[:, :, None, :, None]
    energy_gap = energy_k[:, None, None, None, :] - energy_kq[:, :, None, :, None]
    shifted_up = energy_gap + phonon
    shifted_down = energy_gap - phonon
    kernel = (bose_factor + filled) * shifted_up / (shifted_up * shifted_up + BROADEN * BROADEN)
    kernel = kernel + (bose_factor + 1.0 - filled) * shifted_down / (
        shifted_down * shifted_down + BROADEN * BROADEN
    )
    return jnp.sum(strength / (2.0 * phonon) * kernel, axis=(1, 2, 3))


def select_rows(wanted, block_rows):
    positions = jnp.arange(block_rows.shape[0], dtype=jnp.int32)
    onehot = (wanted[:, None] == positions[None, :]).astype(jnp.float32)
    return product(onehot, block_rows.reshape(block_rows.shape[0], -1))


def shards(
    coupling,
    gauge,
    kq_index,
    fine_coords,
    eig_right,
    eig_left,
    energy_k,
    energy_kq,
    occupied,
    frequency,
):
    coarse_rows = coupling.shape[0]
    qpoint_rows = coupling.shape[1]
    branches = coupling.shape[2]
    orbitals = coupling.shape[3]
    pb_count = lax.axis_size("pb")
    tables = phase_tables(fine_coords)
    fine_total = fine_coords.shape[1]
    quarter = orbitals // pb_count
    own_part = lax.dynamic_slice_in_dim(gauge, lax.axis_index("pb") * quarter, quarter, 1)
    wanted = kq_index.T.reshape(-1)
    picked = select_rows(wanted, gather_axes(own_part, (("ka_0", "ka_1", "ka_2"), "ka_3"), 0))
    shares = picked.reshape(coarse_rows, kq_index.shape[0], quarter, 2 * orbitals)
    left_gauge = lax.all_to_all(shares, "pb", split_axis=1, concat_axis=2, tiled=True)
    right_gauge = mult("kqbjc,kcd->kqbjd", coupling, right_block(gauge))
    right_real = right_gauge[..., :orbitals]
    right_imag = right_gauge[..., orbitals:]
    left_real = left_gauge[..., :orbitals]
    left_imag = left_gauge[..., orbitals:]
    wannier_real = mult("kqjm,kqbjn->kqbmn", left_real, right_real) + mult(
        "kqjm,kqbjn->kqbmn", left_imag, right_imag
    )
    wannier_imag = mult("kqjm,kqbjn->kqbmn", left_real, right_imag) - mult(
        "kqjm,kqbjn->kqbmn", left_imag, right_real
    )
    pair_major = jnp.stack([wannier_real, wannier_imag], 1).reshape(
        coarse_rows, 2, qpoint_rows, branches, orbitals * orbitals
    )
    arrived_block = lax.all_to_all(pair_major, KA, split_axis=4, concat_axis=0, tiled=True)
    columns = arrived_block.reshape(arrived_block.shape[0], 2, -1)
    fine_real_part, fine_imag_part = sectioned(columns[:, 0], columns[:, 1], tables)
    fine_cols = jnp.stack([fine_real_part, fine_imag_part], 1).reshape(
        (fine_total, 2) + arrived_block.shape[2:]
    )
    fine_coupling = lax.all_to_all(fine_cols, KA, split_axis=0, concat_axis=4, tiled=True)
    fine_rows = fine_coupling.shape[0]
    arrived_parts = fine_coupling.reshape(fine_rows, 2, qpoint_rows, branches, orbitals, orbitals)
    coupled_real = arrived_parts[:, 0]
    coupled_imag = arrived_parts[:, 1]
    vector_real = eig_right[..., :orbitals]
    vector_imag = eig_right[..., orbitals:]
    half_real = mult("fqbjc,fcd->fqbjd", coupled_real, vector_real) - mult(
        "fqbjc,fcd->fqbjd", coupled_imag, vector_imag
    )
    half_imag = mult("fqbjc,fcd->fqbjd", coupled_real, vector_imag) + mult(
        "fqbjc,fcd->fqbjd", coupled_imag, vector_real
    )
    outer_real = eig_left[..., :orbitals]
    outer_imag = eig_left[..., orbitals:]
    bloch_real = mult("fqjm,fqbjn->fqbmn", outer_real, half_real) + mult(
        "fqjm,fqbjn->fqbmn", outer_imag, half_imag
    )
    bloch_imag = mult("fqjm,fqbjn->fqbmn", outer_real, half_imag) - mult(
        "fqjm,fqbjn->fqbmn", outer_imag, half_real
    )
    strength = bloch_real * bloch_real + bloch_imag * bloch_imag
    contrib = self_terms(strength, energy_k, energy_kq, occupied, frequency)
    summed = taken_together(contrib, "pb")
    return summed / (qpoint_rows * pb_count * orbitals)


def solution(mesh):
    split = Mesh(
        mesh.devices.reshape(4, 4, 4, 2, mesh.shape["pb"]), ("ka_0", "ka_1", "ka_2", "ka_3", "pb")
    )
    return jax.shard_map(
        shards,
        mesh=split,
        in_specs=(
            P(KA, "pb", None, None, None),
            P(KA, None, None),
            P(None, KA),
            P(),
            P(KA, None, None),
            P(KA, "pb", None, None),
            P(KA, None),
            P(KA, "pb", None),
            P(KA, "pb", None),
            P("pb", None),
        ),
        out_specs=P(KA, None),
        check_vma=False,
    )
```

profile of v0, /device:TPU:1, one launch (start us, length us, event | category | flops | bytes accessed | tf_op | source)
XLA Modules:
  0.0 292.3 jit_solution(2457836625856387109)
XLA Ops:
  0.9 39.6 %all_to_all.63 = f32[64,2,16,128]{3,2,1,0:T(8,128)S(1)} all-to-all(f32[64,2,16,128]{3,2,1,0:T(8,128)S(1)} %broadcast_in_dim.6), channel_id=1, replica_groups=mesh['ka_0'=4,'ka_1'=4,'ka_2'=4,'ka_3'=2,'pb'=4] {'ka_0','ka_1','ka_2'}, dimensions={0} | all-to-all | bytes 2097152 | tf_op jit(solution)/shard_map/all_to_all | solution.py:24
  40.8 7.6 %all_to_all.64 = f32[2,64,2,16,128]{4,3,2,1,0:T(8,128)S(1)} all-to-all(f32[2,64,2,16,128]{4,3,2,1,0:T(8,128)S(1)} %broadcast_in_dim.7), channel_id=1, replica_groups=mesh['ka_0'=4,'ka_1'=4,'ka_2'=4,'ka_3'=2,'pb'=4] {'ka_3'}, dimensions={0} | all-to-all | bytes 4194304 | tf_op jit(solution)/shard_map/all_to_all | solution.py:24
  49.6 1.9 copy.118
  51.4 2.8 fusion.69
  55.0 12.3 %all-to-all-start.2 = ((f32[2,16,16,128]{3,2,0,1:T(8,128)}), f32[2,16,16,128]{3,2,0,1:T(8,128)S(1)}, u32[]{:S(2)}, u32[]{:S(2)}) async-start(f32[2,16,16,128]{3,2,0,1:T(8,128)} %copy.119), calls=%async_computation.2 | async-start | bytes 524288 | tf_op jit(solution)/shard_map/all_to_all | solution.py:142
  68.1 12.7 %all-to-all-done.2 = f32[2,16,16,128]{3,2,0,1:T(8,128)S(1)} async-done(((f32[2,16,16,128]{3,2,0,1:T(8,128)}), f32[2,16,16,128]{3,2,0,1:T(8,128)S(1)}, u32[]{:S(2)}, u32[]{:S(2)}) %all-to-all-start.2) | async-done | bytes 262176 | tf_op jit(solution)/shard_map/all_to_all | solution.py:142
  86.5 16.3 %copy.127 = f32[2,2,4,2,4096]{2,3,1,0,4:T(2,128)} copy(f32[2,2,4,2,4096]{4,3,2,0,1:T(2,128)S(1)} %pad_maximum_fusion) | data formatting | bytes 1048576 | tf_op jit(solution)/shard_map/stack | solution.py:154
  102.8 27.6 %reshape.193 = f32[128,1,1024]{2,1,0:T(1,128)} reshape(f32[4096,2,2,2,4]{4,3,2,1,0:T(2,128)} %bitcast.132) | data formatting | bytes 1048576
  130.4 13.5 %all-to-all-start.3 = ((f32[128,1,1024]{2,1,0:T(1,128)}), f32[128,1,1024]{2,1,0:T(1,128)S(1)}, u32[]{:S(2)}, u32[]{:S(2)}) async-start(f32[128,1,1024]{2,1,0:T(1,128)} %reshape.193), calls=%async_computation.3 | async-start | bytes 1048576 | tf_op jit(solution)/shard_map/all_to_all | solution.py:157
  144.0 18.0 %all-to-all-done.3 = f32[128,1,1024]{2,1,0:T(1,128)S(1)} async-done(((f32[128,1,1024]{2,1,0:T(1,128)}), f32[128,1,1024]{2,1,0:T(1,128)S(1)}, u32[]{:S(2)}, u32[]{:S(2)}) %all-to-all-start.3) | async-done | bytes 524320 | tf_op jit(solution)/shard_map/all_to_all | solution.py:157
  162.5 1.9 reduce
  164.4 27.3 %reshape.194 = f32[4096,2,2,2,4]{4,3,2,1,0:T(2,128)} reshape(f32[128,1024]{1,0:T(8,128)S(1)} %reduce) | data formatting | bytes 1048576
  191.7 22.3 %copy.154 = f32[2,2,4,2,128,32]{5,4,3,2,1,0:T(8,128)S(1)} copy(f32[2,2,4,2,128,32]{2,3,1,0,5,4:T(2,128)} %bitcast.133) | data formatting | bytes 1048576 | tf_op jit(solution)/shard_map/all_to_all | solution.py:157
  214.0 3.0 %copy.129 = f32[128,2,2,4,2,32]{5,4,3,1,0,2:T(2,128)} copy(f32[128,2,2,4,2,32]{5,0,4,3,2,1:T(8,128)S(1)} %bitcast.134) | data formatting | bytes 1048576 | tf_op jit(solution)/shard_map/all_to_all | solution.py:157
  216.9 4.3 %reshape.181 = f32[256,2,256]{2,0,1:T(8,128)S(1)} reshape(f32[128,2,2,4,2,32]{5,4,3,1,0,2:T(2,128)} %copy.129) | data formatting | bytes 1048576 | tf_op jit(solution)/shard_map/reshape | solution.py:158
  221.2 1.5 fusion.34
  222.7 1.5 fusion.35
  224.2 1.5 convolution_subtract_fusion.4
  225.7 1.5 convolution_add_fusion.4
  227.2 1.6 fusion.56
  228.8 1.6 fusion.54
  230.4 1.6 convolution_subtract_fusion.3
  232.1 1.8 convolution_add_fusion.3
  233.9 1.5 copy.130
  235.5 2.8 reshape.195
  238.3 6.4 %all-to-all-start.4 = ((f32[128,1,1024]{2,1,0:T(1,128)}), f32[128,1,1024]{2,1,0:T(1,128)S(1)}, u32[]{:S(2)}, u32[]{:S(2)}) async-start(f32[128,1,1024]{2,1,0:T(1,128)} %reshape.195), calls=%async_computation.4 | async-start | bytes 1048576 | tf_op jit(solution)/shard_map/all_to_all | solution.py:163
  245.3 17.7 %all-to-all-done.4 = f32[128,1,1024]{2,1,0:T(1,128)S(1)} async-done(((f32[128,1,1024]{2,1,0:T(1,128)}), f32[128,1,1024]{2,1,0:T(1,128)S(1)}, u32[]{:S(2)}, u32[]{:S(2)}) %all-to-all-start.4) | async-done | bytes 524320 | tf_op jit(solution)/shard_map/all_to_all | solution.py:163
  263.0 1.9 reduce.1
  264.9 1.8 reshape.196
  267.4 1.6 copy.155
  269.0 1.8 reshape.192
  276.4 14.3 %all_to_all.65 = f32[4,1,128]{2,1,0:T(1,128)S(1)} all-to-all(f32[4,1,128]{2,1,0:T(1,128)S(1)} %reshape.197), channel_id=1, replica_groups=mesh['ka_0'=4,'ka_1'=4,'ka_2'=4,'ka_3'=2,'pb'=4] {'pb'}, dimensions={0} | all-to-all | bytes 4096 | tf_op jit(solution)/shard_map/all_to_all | solution.py:24
  (69 shorter events, 18.1 us)
Async XLA Ops:
  0.0 67.4 %copy-start = (f32[2,4,2,64,128]{4,3,2,1,0:T(8,128)S(1)}, f32[2,4,2,64,128]{4,3,2,1,0:T(8,128)}, u32[]{:S(2)}) copy-start(f32[2,4,2,64,128]{4,3,2,1,0:T(8,128)} %param.10) | copy-start | bytes 1572868
  49.5 1.9 copy-start.9
  51.4 15.9 %copy-start.4 = (f32[2,64,128]{2,1,0:T(8,128)S(1)}, f32[2,64,128]{2,1,0:T(8,128)}, u32[]{:S(2)}) copy-start(f32[2,64,128]{2,1,0:T(8,128)} %param.11) | copy-start | bytes 196612
  55.0 25.8 %all-to-all-start.2 = ((f32[2,16,16,128]{3,2,0,1:T(8,128)}), f32[2,16,16,128]{3,2,0,1:T(8,128)S(1)}, u32[]{:S(2)}, u32[]{:S(2)}) async-start(f32[2,16,16,128]{3,2,0,1:T(8,128)} %copy.119), calls=%async_computation.2 | async-start | bytes 524288 | tf_op jit(solution)/shard_map/all_to_all | solution.py:142
  102.8 41.2 %copy-start.8 = (s32[3,256]{1,0:T(4,128)S(1)}, s32[3,256]{1,0:T(4,128)}, u32[]{:S(2)}) copy-start(s32[3,256]{1,0:T(4,128)} %param.13) | copy-start | bytes 9220
  130.4 31.6 %all-to-all-start.3 = ((f32[128,1,1024]{2,1,0:T(1,128)}), f32[128,1,1024]{2,1,0:T(1,128)S(1)}, u32[]{:S(2)}, u32[]{:S(2)}) async-start(f32[128,1,1024]{2,1,0:T(1,128)} %reshape.193), calls=%async_computation.3 | async-start | bytes 1048576 | tf_op jit(solution)/shard_map/all_to_all | solution.py:157
  235.4 9.3 %copy-start.7 = (f32[4,2]{0,1:T(2,128)S(1)}, f32[4,2]{0,1:T(2,128)}, u32[]{:S(2)}) copy-start(f32[4,2]{0,1:T(2,128)} %param.19) | copy-start | bytes 100
  235.4 9.6 %copy-start.6 = (s32[2,4,64]{2,1,0:T(4,128)S(1)}, s32[2,4,64]{2,1,0:T(4,128)}, u32[]{:S(2)}) copy-start(s32[2,4,64]{2,1,0:T(4,128)} %param.18) | copy-start | bytes 6148
  235.4 9.8 %copy-start.5 = (f32[2,4,64]{2,1,0:T(4,128)S(1)}, f32[2,4,64]{2,1,0:T(4,128)}, u32[]{:S(2)}) copy-start(f32[2,4,64]{2,1,0:T(4,128)} %param.17) | copy-start | bytes 6148
  235.5 9.7 %copy-start.10 = (f32[2,64]{1,0:T(2,128)S(1)}, f32[2,64]{1,0:T(2,128)}, u32[]{:S(2)}) copy-start(f32[2,64]{1,0:T(2,128)} %param.16) | copy-start | bytes 1540
  238.3 24.7 %all-to-all-start.4 = ((f32[128,1,1024]{2,1,0:T(1,128)}), f32[128,1,1024]{2,1,0:T(1,128)S(1)}, u32[]{:S(2)}, u32[]{:S(2)}) async-start(f32[128,1,1024]{2,1,0:T(1,128)} %reshape.195), calls=%async_computation.4 | async-start | bytes 1048576 | tf_op jit(solution)/shard_map/all_to_all | solution.py:163
  269.0 1.8 copy-start.3
  271.5 1.9 copy-start.2
  275.3 16.8 %copy-start.1 = (f32[2,4,2,64,128]{4,3,2,1,0:T(8,128)S(1)}, f32[2,4,2,64,128]{4,3,2,1,0:T(8,128)}, u32[]{:S(2)}) copy-start(f32[2,4,2,64,128]{4,3,2,1,0:T(8,128)} %param.10) | copy-start | bytes 1572868
where the time goes:
time: 297 us; the launch traced here: 292 us
  local copies, waits for them, and re-layouts  118 us (40%)
  blocking collectives  61.6 us (21%)
  waiting for transfers between devices  48.4 us (16%)
  starting transfers between devices  32.3 us (11%)
  matrix products  25.9 us (9%)
  other arithmetic  5.62 us (2%)
    all_to_all x3, blocking collectives, sent_to_all(): lax.all_to_all(jnp.broadcast_to(x[None], (devices, *x.shape)), axis, 0, 0...  61.6 us
    unnamed x30, local copies, waits for them, and re-layouts  60.7 us
    all_to_all x3, local copies, waits for them, and re-layouts, shards(): lax.all_to_all(pair_major, KA, split_axis=4, concat_axis=0, tiled=True)  25.8 us
    all_to_all x1, waiting for transfers between devices, shards(): lax.all_to_all(pair_major, KA, split_axis=4, concat_axis=0, tiled=True)  18 us
    all_to_all x1, waiting for transfers between devices, shards(): lax.all_to_all(fine_cols, KA, split_axis=0, concat_axis=4, tiled=True)  17.7 us
    another operation x3, local copies, waits for them, and re-layouts, shards(): jnp.stack([wannier_real, wannier_imag], 1)  16.8 us
    dot_general x9, matrix products, product(): jnp.dot(left_matrix, right_matrix, precision=PRECISE, preferred_element_t...  15.3 us
    all_to_all x1, starting transfers between devices, shards(): lax.all_to_all(pair_major, KA, split_axis=4, concat_axis=0, tiled=True)  13.5 us
  transfers between devices with their start and end apart: 3, of which 3 were waited for; matrix products, arithmetic and copies ran while one was open for 0% of the time, Pallas kernels for 0%

commit v1 on v0

v1 whole, which is shorter than its diff:
```python
import functools
import math

import jax
import jax.numpy as jnp
import numpy as np
from jax import lax
from jax.experimental import pallas as pl
from jax.experimental.pallas import tpu as pltpu
from jax.sharding import Mesh
from jax.sharding import PartitionSpec as P

FG = 32
W = 64
LANES = 128
NK = 256
BROADEN = 0.1
THERMAL = 0.05
KA = ("z", "y", "x", "core")
VMEM = pl.BlockSpec(memory_space=pltpu.VMEM)
SMEM = pl.BlockSpec(memory_space=pltpu.SMEM)
CONTRACT_ROWS = (((0,), (0,)), ((), ()))
PLAIN = (((1,), (0,)), ((), ()))


def halves(value):
    high = value.astype(jnp.bfloat16)
    low = (value - high.astype(jnp.float32)).astype(jnp.bfloat16)
    return high, low


def product(left, right, dims):
    left_high, left_low = left
    right_high, right_low = right
    dot = functools.partial(lax.dot_general, dimension_numbers=dims, preferred_element_type=jnp.float32)
    return dot(left_high, right_high) + (dot(left_high, right_low) + dot(left_low, right_high))


def right_block(matrix):
    real_part = matrix[:, :W]
    imag_part = matrix[:, W:]
    upper = jnp.concatenate([real_part, imag_part], -1)
    lower = jnp.concatenate([-imag_part, real_part], -1)
    return jnp.concatenate([upper, lower], 0)


def signs(first):
    lane = lax.broadcasted_iota(jnp.int32, (1, LANES), 1)
    return jnp.where(lane < W, first, -first)


def apply_left(left, right_pair):
    both = product(halves(left), halves(right_pair), CONTRACT_ROWS)
    sign = signs(1.0)
    return [
        both[:W, at : at + LANES] + sign * pltpu.roll(both[W:, at : at + LANES], W, 1)
        for at in (0, LANES)
    ]


def offsets_of(position, kq, qpoint):
    along_z, along_y, along_x, core = (position[i] for i in range(4))
    first = 2 * along_z + along_y // 2
    second = (along_y % 2) * 4 + along_x
    third = 2 * core
    target = kq[position[4] * 4 + qpoint, 0]
    return (
        (target // 32 - first + 8) % 8,
        (target // 4 % 8 - second + 8) % 8,
        (target % 4 - third + 4) % 4,
    )


def source_of(position, offsets):
    row = (position[1] // 2 + offsets[0]) % 2
    second = ((position[1] % 2) * 4 + position[2] + offsets[1]) % 8
    return (row * 2 + second // 4) * 4 + second % 4


def right_kernel(coupling, gauge, out):
    for k in range(2):
        block = halves(right_block(gauge[k]))
        rows = coupling[k].reshape(-1, LANES)
        result = product(halves(rows), block, PLAIN).reshape(4, 2, W, LANES)
        for q in range(4):
            out[q, 2 * k : 2 * k + 2] = result[q]


def send_kernel(position, kq, gathered, out):
    core = position[3]
    for q in range(4):
        offsets = offsets_of(position, kq, q)
        source = source_of(position, offsets)
        for l in range(2):
            third = (2 * (1 - core) + l + offsets[2]) % 4
            out[q, l] = gathered[source, third % 2]


def keep_kernel(position, kq, gathered, swapped, old, out):
    core = position[3]
    for q in range(4):
        offsets = offsets_of(position, kq, q)
        source = source_of(position, offsets)
        for l in range(2):
            third = (2 * core + l + offsets[2]) % 4
            mine = third // 2 == core

            @pl.when(mine)
            def _(q=q, l=l, third=third, source=source):
                out[q, l] = gathered[source, third % 2]

            @pl.when(jnp.logical_not(mine))
            def _(q=q, l=l):
                out[q, l] = swapped[q, l]


def left_kernel(position, kq, arrived, out):
    offsets = offsets_of(position, kq, position[0])
    carry = (position[1] // 2 + offsets[0]) // 2
    for z in range(4):
        plane = (z + carry) % 4
        for l in range(2):
            gauge = arrived[plane, 4 + l]
            pair = jnp.concatenate([arrived[z, 2 * l], arrived[z, 2 * l + 1]], -1)
            for b, wannier in enumerate(apply_left(gauge, pair)):
                for part in range(2):
                    start = (z * 2 + l) * 4 + part * 2 + b
                    out[pl.ds(start, 32, stride=32), :] = wannier[part * 32 : part * 32 + 32]


def phase_kernel(coords, tables, high, low):
    real, imag = None, None
    for axis in range(3):
        divisions = lax.broadcasted_iota(jnp.int32, (FG, NK), 0)
        onehot = (divisions == coords[axis : axis + 1, :]).astype(jnp.float32)
        factor = [
            lax.dot_general(
                onehot,
                tables[axis, part],
                CONTRACT_ROWS,
                precision=lax.Precision.HIGHEST,
                preferred_element_type=jnp.float32,
            )
            for part in range(2)
        ]
        if real is None:
            real, imag = factor
        else:
            real, imag = (
                real * factor[0] - imag * factor[1],
                real * factor[1] + imag * factor[0],
            )
    for row, part in enumerate((real, imag)):
        part_high, part_low = halves(part)
        high[row * NK : row * NK + NK] = part_high
        low[row * NK : row * NK + NK] = part_low


def fourier_kernel(high, low, columns, out):
    parts = [columns[pl.ds(c, NK, stride=4), :] for c in range(4)]
    result = product((high[...], low[...]), halves(jnp.concatenate(parts, -1)), PLAIN)
    sign = signs(-1.0)
    for c in range(4):
        at = c * LANES
        rolled = pltpu.roll(result[NK:, at : at + LANES], W, 1)
        out[pl.ds(c, NK, stride=4), :] = result[:NK, at : at + LANES] + sign * rolled


def bloch_kernel(frequency, arrived, eig_right, eig_left, energy_k, energy_kq, occupied, out):
    lane = lax.broadcasted_iota(jnp.int32, (1, LANES), 1)
    first = lane < W
    states = jnp.concatenate([energy_kq[...], occupied[...].astype(jnp.float32)], -1).T
    energies = jnp.concatenate([energy_k[0:1], energy_k[1:2]], -1)
    strengths = {}
    for f in range(2):
        rows = [
            arrived[pl.ds(q * 256 + f * 4 + part * 2 + b, 32, stride=8), :]
            for q in range(4)
            for b in range(2)
            for part in range(2)
        ]
        half = product(
            halves(jnp.concatenate(rows, 0)), halves(right_block(eig_right[f])), PLAIN
        )
        for q in range(4):
            at = q * LANES
            pair = jnp.concatenate([half[at : at + W], half[at + W : at + LANES]], -1)
            for b, bloch in enumerate(apply_left(eig_left[f, q], pair)):
                square = bloch * bloch
                strengths[f, q, b] = square + pltpu.roll(square, W, 1)
    total = jnp.zeros((W, LANES), jnp.float32)
    for q in range(4):
        energy_left = jnp.where(first, states[:W, q : q + 1], states[:W, q + 4 : q + 5])
        filled = jnp.where(first, states[W:, q : q + 1], states[W:, q + 4 : q + 5])
        gap = energies - energy_left
        for b in range(2):
            phonon = jnp.full((1, LANES), frequency[q, b], jnp.float32)
            bose = 1.0 / (jnp.exp(phonon / THERMAL) - 1.0)
            up = gap + phonon
            down = gap - phonon
            kernel = (bose + filled) * up / (up * up + BROADEN * BROADEN)
            kernel = kernel + (bose + 1.0 - filled) * down / (down * down + BROADEN * BROADEN)
            strength = jnp.where(first, strengths[0, q, b], strengths[1, q, b])
            total = total + strength / (2.0 * phonon) * kernel
    summed = jnp.sum(total, axis=0, keepdims=True) * (1.0 / 1024.0)
    out[0:1] = summed[:, :W]
    out[1:2] = summed[:, W:]


def phase_tables():
    column = np.arange(NK)
    source, z, l = column // 8, column // 2 % 4, column % 2
    y, x, core = source // 8, source // 2 % 4, source % 2
    coordinates = (2 * z + y // 2, (y % 2) * 4 + x, 2 * core + l)
    tables = np.zeros((3, 2, FG, NK), np.float64)
    for axis, (size, where) in enumerate(zip((8, 8, 4), coordinates)):
        steps = np.arange(FG)[:, None] - (FG // size) * where[None, :]
        for cell in range(-size // 2, size // 2):
            angle = 2.0 * math.pi * ((cell * steps) % FG) / FG
            tables[axis, 0] += np.cos(angle) / size
            tables[axis, 1] += np.sin(angle) / size
    return tables.astype(np.float32)


def call(kernel, shapes, specs, flops, **more):
    return pl.pallas_call(
        kernel,
        out_shape=shapes,
        in_specs=specs,
        cost_estimate=pl.CostEstimate(flops=flops, bytes_accessed=1 << 20, transcendentals=0),
        **more,
    )


def f32(*shape):
    return jax.ShapeDtypeStruct(shape, jnp.float32)


def shards(
    coupling,
    gauge,
    kq_index,
    fine_coords,
    eig_right,
    eig_left,
    energy_k,
    energy_kq,
    occupied,
    frequency,
):
    position = jnp.stack([lax.axis_index(name) for name in (*KA, "pb")])
    to_all = jnp.broadcast_to(gauge[None], (16, 2, W, LANES))
    gathered = lax.all_to_all(to_all, ("y", "x"), 0, 0, tiled=True)
    products = call(right_kernel, f32(4, 6, W, LANES), [VMEM, VMEM], 1 << 27)(coupling, gauge)
    high, low = call(
        phase_kernel,
        [jax.ShapeDtypeStruct((2 * NK, NK), jnp.bfloat16)] * 2,
        [VMEM, VMEM],
        1 << 28,
    )(fine_coords, jnp.asarray(phase_tables()))
    sent = call(send_kernel, f32(4, 2, W, LANES), [SMEM, SMEM, VMEM], 1 << 20)(
        position, kq_index, gathered
    )
    swapped = lax.ppermute(sent, "core", [(0, 1), (1, 0)])
    filled = call(
        keep_kernel,
        f32(4, 6, W, LANES),
        [SMEM, SMEM, VMEM, VMEM, pl.BlockSpec(memory_space=pl.ANY)],
        1 << 20,
        grid=(1,),
        out_specs=pl.BlockSpec((4, 2, W, LANES), lambda i: (0, 2, 0, 0)),
        input_output_aliases={4: 0},
    )(position, kq_index, gathered, swapped, products)
    arrived = lax.all_to_all(filled, "z", 0, 0, tiled=True)
    pieces = call(left_kernel, f32(1024, LANES), [SMEM, SMEM, VMEM], 1 << 27)(
        position, kq_index, arrived
    )
    columns = lax.all_to_all(
        pieces.reshape(32, 32, LANES), ("y", "x", "core"), 0, 0, tiled=True
    ).reshape(1024, LANES)
    fine = call(fourier_kernel, f32(1024, LANES), [VMEM, VMEM, VMEM], 1 << 28)(high, low, columns)
    blocks = lax.all_to_all(fine.reshape(128, 8, LANES), KA, 0, 0, tiled=True)
    terms = call(bloch_kernel, f32(2, W), [SMEM] + [VMEM] * 6, 1 << 27)(
        frequency,
        blocks.reshape(1024, LANES),
        eig_right,
        eig_left,
        energy_k,
        energy_kq.reshape(8, W),
        occupied.reshape(8, W),
    )
    return lax.psum(terms, "pb")


def solution(mesh):
    split = Mesh(mesh.devices.reshape(4, 4, 4, 2, mesh.shape["pb"]), (*KA, "pb"))
    return jax.shard_map(
        shards,
        mesh=split,
        in_specs=(
            P(KA, "pb", None, None, None),
            P(KA, None, None),
            P(None, KA),
            P(),
            P(KA, None, None),
            P(KA, "pb", None, None),
            P(KA, None),
            P(KA, "pb", None),
            P(KA, "pb", None),
            P("pb", None),
        ),
        out_specs=P(KA, None),
        check_vma=False,
    )
```

time: 297 us -> 135 us (0.45); the launches traced: 292 us -> 134 us
  local copies, waits for them, and re-layouts: 118 us -> 7.76 us
  matrix products: 25.9 us -> 0 us
  Pallas kernels: 0 us -> 19.2 us
  blocking collectives: 61.6 us -> 44.1 us
  waiting for transfers between devices: 48.4 us -> 38.5 us
  starting transfers between devices: 32.3 us -> 24.1 us
  other arithmetic: 5.62 us -> 0 us
    unnamed x30 -> x14, local copies, waits for them, and re-layouts: 60.7 us -> 5.27 us
    all_to_all x3 -> x1, blocking collectives: 61.6 us -> 25.7 us  [shards(): arrived = lax.all_to_all(filled, 'z', 0, 0, tiled=True)]
    all_to_all x5 -> x0, local copies, waits for them, and re-layouts: 26.5 us -> none  [the longest x3 25.8 us: shards(): lax.all_to_all(pair_major, KA, split_axis=4, concat_axis=0, tiled=True)]
    dot_general x22 -> x0, matrix products: 25.9 us -> none  [the longest x9 15.3 us: product(): jnp.dot(left_matrix, right_matrix, precision=PRECISE, preferred_element_t...]
    pallas_call x0 -> x7, Pallas kernels: none -> 19.2 us  [the longest x1 3.41 us: shards(): call(bloch_kernel, f32(2, W), [SMEM] + [VMEM] * 6, 1 << 27)]
    psum x0 -> x1, blocking collectives: none -> 18.4 us  [shards(): return lax.psum(terms, 'pb')]
    another operation x4 -> x1, local copies, waits for them, and re-layouts: 18.3 us -> 0.57 us  [shards(): position = jnp.stack([lax.axis_index(name) for name in (*KA, 'pb')])]
    all_to_all x3, starting transfers between devices: 32.3 us -> 18.3 us  [the longest x1 7.57 us: shards(): gathered = lax.all_to_all(to_all, ('y', 'x'), 0, 0, tiled=True)]
  transfers between devices with their start and end apart: 3 -> 4, of which waited for: 3 -> 3; matrix products, arithmetic and copies ran while one was open for 0% -> 1% of each run, Pallas kernels for 0% -> 4%
where the time goes in v1:
time: 135 us; the launch traced here: 134 us
  blocking collectives  44.1 us (33%)
  waiting for transfers between devices  38.5 us (29%)
  starting transfers between devices  24.1 us (18%)
  Pallas kernels  19.2 us (14%)
  local copies, waits for them, and re-layouts  7.76 us (6%)
    all_to_all x1, blocking collectives, shards(): arrived = lax.all_to_all(filled, 'z', 0, 0, tiled=True)  25.7 us
    psum x1, blocking collectives, shards(): return lax.psum(terms, 'pb')  18.4 us
    all_to_all x1, waiting for transfers between devices, shards(): blocks = lax.all_to_all(fine.reshape(128, 8, LANES), KA, 0, 0, tiled=True)  17.5 us
    all_to_all x1, waiting for transfers between devices, shards(): gathered = lax.all_to_all(to_all, ('y', 'x'), 0, 0, tiled=True)  12.7 us
    all_to_all x1, waiting for transfers between devices, shards(): lax.all_to_all(pieces.reshape(32, 32, LANES), ('y', 'x', 'core'), 0, 0, t...  8.31 us
    all_to_all x1, starting transfers between devices, shards(): gathered = lax.all_to_all(to_all, ('y', 'x'), 0, 0, tiled=True)  7.57 us
    all_to_all x1, starting transfers between devices, shards(): blocks = lax.all_to_all(fine.reshape(128, 8, LANES), KA, 0, 0, tiled=True)  6.04 us
    ppermute x1, starting transfers between devices, shards(): swapped = lax.ppermute(sent, 'core', [(0, 1), (1, 0)])  5.82 us
  transfers between devices with their start and end apart: 4, of which 3 were waited for; matrix products, arithmetic and copies ran while one was open for 1% of the time, Pallas kernels for 4%

profile of v1, /device:TPU:1, one launch (start us, length us, event | category | flops | bytes accessed | tf_op | source)
XLA Modules:
  0.0 133.8 jit_solution(11130193423454994434)
XLA Ops:
  0.0 1.9 %broadcast_in_dim.2 = f32[16,2,64,128]{3,2,1,0:T(8,128)} broadcast(f32[2,64,128]{2,1,0:T(8,128)} %gauge.1), dimensions={1,2,3} | broadcast | bytes 1114112 | tf_op jit(solution)/shard_map/broadcast_in_dim | solution.py:252
  1.9 7.6 %all-to-all-start = ((f32[16,2,64,128]{3,2,1,0:T(8,128)}), f32[16,2,64,128]{3,2,1,0:T(8,128)S(1)}, u32[]{:S(2)}, u32[]{:S(2)}) async-start(f32[16,2,64,128]{3,2,1,0:T(8,128)} %broadcast_in_dim.2), calls=%async_computation | async-start | bytes 2097152 | tf_op jit(solution)/shard_map/all_to_all | solution.py:253
  9.5 0.0 copy-start.4
  9.5 0.7 copy-done.4
  10.2 0.7 copy.15.kq
  10.9 0.6 stack.23.position
  11.4 12.7 %all-to-all-done.gathered = f32[16,2,64,128]{3,2,1,0:T(8,128)S(1)} async-done(((f32[16,2,64,128]{3,2,1,0:T(8,128)}), f32[16,2,64,128]{3,2,1,0:T(8,128)S(1)}, u32[]{:S(2)}, u32[]{:S(2)}) %all-to-all-start) | async-done | bytes 1048608 | tf_op jit(solution)/shard_map/all_to_all | solution.py:253
  24.1 0.0 copy-start
  24.1 1.0 copy-done
  25.1 2.1 %shard_map.110 = f32[4,2,64,128]{3,2,1,0:T(8,128)} custom-call(s32[5]{0:T(128)} %stack.23.position, s32[16,2]{1,0:T(8,128)} %copy.15.kq, f32[16,2,64,128]{3,2,1,0:T(8,128)} %copy-done), custom_call_target="tpu_custom_call" | custom-call | flops 1048576 | bytes 1048576 | tf_op jit(solution)/shard_map/pallas_call | solution.py:261
  27.2 5.8 %collective-permute-start = (f32[4,2,64,128]{3,2,1,0:T(8,128)}, f32[4,2,64,128]{3,2,1,0:T(8,128)S(1)}, u32[]{:S(2)}, u32[]{:S(2)}) collective-permute-start(f32[4,2,64,128]{3,2,1,0:T(8,128)} %shard_map.110), channel_id=1, source_target_pairs={{0,4},{4,0},{1,5},{5,1},{2,6},{6,2},{3,7},{7,3},{8,12},{12,8},{9,1... | collective-permute-start | bytes 786440 | tf_op jit(solution)/shard_map/ppermute | solution.py:264
  33.1 2.4 %shard_map.111.old = f32[4,6,64,128]{3,2,1,0:T(8,128)} custom-call(f32[2,4,2,64,128]{4,3,2,1,0:T(8,128)} %coupling.1, f32[2,64,128]{2,1,0:T(8,128)} %gauge.1), custom_call_target="tpu_custom_call" | custom-call | flops 134217728 | bytes 1048576 | tf_op jit(solution)/shard_map/pallas_call | solution.py:254
  35.5 0.0 collective-permute-done.swapped
  35.5 0.0 copy-start.3
  35.5 0.7 copy-done.3
  36.2 2.3 %shard_map.112 = f32[4,6,64,128]{3,2,1,0:T(8,128)} custom-call(s32[5]{0:T(128)} %stack.23.position, s32[16,2]{1,0:T(8,128)} %copy.15.kq, f32[16,2,64,128]{3,2,1,0:T(8,128)} %copy-done, f32[4,2,64,128]{3,2,1,0:T(8,128)} %copy-done.3, f32[4,6,64,128]{3,2,1,0:T(8,128)} %shard_map.111.old), custom_call_target="tpu_custom_call", output_to_operand_aliasing={{}: (4, {})} | custom-call | flops 1048576 | bytes 1048576 | tf_op jit(solution)/shard_map/pallas_call | solution.py:265
  38.5 25.7 %all_to_all.20.arrived = f32[4,6,64,128]{3,2,1,0:T(8,128)} all-to-all(f32[4,6,64,128]{3,2,1,0:T(8,128)} %shard_map.112), channel_id=1, replica_groups=mesh['z'=4,'y'=4,'x'=4,'core'=2,'pb'=4] {'z'}, dimensions={0} | all-to-all | bytes 1572864 | tf_op jit(solution)/shard_map/all_to_all | solution.py:274
  64.2 3.0 %shard_map.113 = f32[1024,128]{1,0:T(8,128)} custom-call(s32[5]{0:T(128)} %stack.23.position, s32[16,2]{1,0:T(8,128)} %copy.15.kq, f32[4,6,64,128]{3,2,1,0:T(8,128)} %all_to_all.20.arrived), custom_call_target="tpu_custom_call" | custom-call | flops 134217728 | bytes 1048576 | tf_op jit(solution)/shard_map/pallas_call | solution.py:275
  67.2 4.7 %all-to-all-start.2 = ((f32[32,32,128]{2,1,0:T(8,128)}), f32[32,32,128]{2,1,0:T(8,128)S(1)}, u32[]{:S(2)}, u32[]{:S(2)}) async-start(f32[32,32,128]{2,1,0:T(8,128)} %bitcast.12), calls=%async_computation.2 | async-start | bytes 1048576 | tf_op jit(solution)/shard_map/all_to_all | solution.py:278
  71.9 3.2 %shard_map.109 = (bf16[512,256]{1,0:T(8,128)(2,1)}, bf16[512,256]{1,0:T(8,128)(2,1)}) custom-call(s32[3,256]{1,0:T(4,128)} %coords.1, f32[3,2,32,256]{3,2,1,0:T(8,128)} %constant.22.clone.tables), custom_call_target="tpu_custom_call" | custom-call | flops 268435456 | bytes 1048576 | tf_op jit(solution)/shard_map/pallas_call | solution.py:255
  75.1 8.3 %all-to-all-done.2 = f32[32,32,128]{2,1,0:T(8,128)S(1)} async-done(((f32[32,32,128]{2,1,0:T(8,128)}), f32[32,32,128]{2,1,0:T(8,128)S(1)}, u32[]{:S(2)}, u32[]{:S(2)}) %all-to-all-start.2) | async-done | bytes 524320 | tf_op jit(solution)/shard_map/all_to_all | solution.py:278
  83.4 0.0 copy-start.1
  83.4 0.8 copy-done.1
  84.2 2.7 %shard_map.114 = f32[1024,128]{1,0:T(8,128)} custom-call(bf16[512,256]{1,0:T(8,128)(2,1)} %get-tuple-element.7.high, bf16[512,256]{1,0:T(8,128)(2,1)} %get-tuple-element.8.low, f32[1024,128]{1,0:T(8,128)} %bitcast.11), custom_call_target="tpu_custom_call" | custom-call | flops 268435456 | bytes 1048576 | tf_op jit(solution)/shard_map/pallas_call | solution.py:281
  86.9 0.0 copy-start.5
  86.9 6.0 %all-to-all-start.3 = ((f32[128,8,128]{2,1,0:T(8,128)}), f32[128,8,128]{2,1,0:T(8,128)S(1)}, u32[]{:S(2)}, u32[]{:S(2)}) async-start(f32[128,8,128]{2,1,0:T(8,128)} %bitcast.13), calls=%async_computation.3 | async-start | bytes 1048576 | tf_op jit(solution)/shard_map/all_to_all | solution.py:282
  93.0 0.0 copy-done.5
  93.0 0.7 copy.16.frequency
  93.7 17.5 %all-to-all-done.3 = f32[128,8,128]{2,1,0:T(8,128)S(1)} async-done(((f32[128,8,128]{2,1,0:T(8,128)}), f32[128,8,128]{2,1,0:T(8,128)S(1)}, u32[]{:S(2)}, u32[]{:S(2)}) %all-to-all-start.3) | async-done | bytes 524320 | tf_op jit(solution)/shard_map/all_to_all | solution.py:282
  111.2 0.8 copy-done.2
  112.0 3.4 %shard_map.115 = f32[2,64]{1,0:T(2,128)} custom-call(f32[4,2]{1,0:T(4,128)} %copy.16.frequency, f32[1024,128]{1,0:T(8,128)} %bitcast.14, f32[2,64,128]{2,1,0:T(8,128)} %eig_right.1, f32[2,4,64,128]{3,2,1,0:T(8,128)} %eig_left.1, f32[2,64]{1,0:T(2,128)} %energy_k.1, f32[8,64]{1,0:T(8,128)} %bitcast.15, s32[8,64]{1,0:T(8,128)} %bitcast.16), custom_call_target="tpu_custom_call" | custom-call | flops 134217728 | bytes 1048576 | tf_op jit(solution)/shard_map/pallas_call | solution.py:283
  115.4 18.4 %psum.7 = f32[2,64]{1,0:T(2,128)} all-reduce(f32[2,64]{1,0:T(2,128)} %shard_map.115), channel_id=1, replica_groups=mesh['z'=4,'y'=4,'x'=4,'core'=2,'pb'=4] {'pb'}, use_global_device_ids=true, to_apply=%region_0.0 | all-reduce | flops 128 | bytes 1024 | tf_op jit(solution)/shard_map/psum | solution.py:292
  (1 shorter events, 0.0 us)
Async XLA Ops:
  1.9 22.2 %all-to-all-start = ((f32[16,2,64,128]{3,2,1,0:T(8,128)}), f32[16,2,64,128]{3,2,1,0:T(8,128)S(1)}, u32[]{:S(2)}, u32[]{:S(2)}) async-start(f32[16,2,64,128]{3,2,1,0:T(8,128)} %broadcast_in_dim.2), calls=%async_computation | async-start | bytes 2097152 | tf_op jit(solution)/shard_map/all_to_all | solution.py:253
  9.5 0.7 copy-start.4
  24.1 1.0 copy-start
  27.2 8.2 %collective-permute-start = (f32[4,2,64,128]{3,2,1,0:T(8,128)}, f32[4,2,64,128]{3,2,1,0:T(8,128)S(1)}, u32[]{:S(2)}, u32[]{:S(2)}) collective-permute-start(f32[4,2,64,128]{3,2,1,0:T(8,128)} %shard_map.110), channel_id=1, source_target_pairs={{0,4},{4,0},{1,5},{5,1},{2,6},{6,2},{3,7},{7,3},{8,12},{12,8},{9,1... | collective-permute-start | bytes 786440 | tf_op jit(solution)/shard_map/ppermute | solution.py:264
  35.5 0.7 copy-start.3
  67.2 16.2 %all-to-all-start.2 = ((f32[32,32,128]{2,1,0:T(8,128)}), f32[32,32,128]{2,1,0:T(8,128)S(1)}, u32[]{:S(2)}, u32[]{:S(2)}) async-start(f32[32,32,128]{2,1,0:T(8,128)} %bitcast.12), calls=%async_computation.2 | async-start | bytes 1048576 | tf_op jit(solution)/shard_map/all_to_all | solution.py:278
  83.4 0.8 copy-start.1
  86.9 6.1 %copy-start.5 = (f32[4,2]{0,1:T(2,128)S(1)}, f32[4,2]{0,1:T(2,128)}, u32[]{:S(2)}) copy-start(f32[4,2]{0,1:T(2,128)} %param.20) | copy-start | bytes 100
  86.9 24.2 %all-to-all-start.3 = ((f32[128,8,128]{2,1,0:T(8,128)}), f32[128,8,128]{2,1,0:T(8,128)S(1)}, u32[]{:S(2)}, u32[]{:S(2)}) async-start(f32[128,8,128]{2,1,0:T(8,128)} %bitcast.13), calls=%async_computation.3 | async-start | bytes 1048576 | tf_op jit(solution)/shard_map/all_to_all | solution.py:282
  111.2 0.8 copy-start.2

commit v2 on v1

--- a/solution.py
+++ b/solution.py
@@ -77,62 +77,57 @@
     return (row * 2 + second // 4) * 4 + second % 4
 
 
-def right_kernel(coupling, gauge, out):
+def right_kernel(position, coupling, gauge, *outs):
     for k in range(2):
         block = halves(right_block(gauge[k]))
-        rows = coupling[k].reshape(-1, LANES)
-        result = product(halves(rows), block, PLAIN).reshape(4, 2, W, LANES)
-        for q in range(4):
-            out[q, 2 * k : 2 * k + 2] = result[q]
-
-
-def send_kernel(position, kq, gathered, out):
+        for shift, out in enumerate(outs):
+            rows = coupling[k, (position[0] + shift) % 4].reshape(-1, LANES)
+            out[k] = product(halves(rows), block, PLAIN).reshape(2, W, LANES)
+
+
+def pick_kernel(position, kq, gathered, kept, sent, sems):
     core = position[3]
+    copies = []
     for q in range(4):
         offsets = offsets_of(position, kq, q)
         source = source_of(position, offsets)
         for l in range(2):
-            third = (2 * (1 - core) + l + offsets[2]) % 4
-            out[q, l] = gathered[source, third % 2]
-
-
-def keep_kernel(position, kq, gathered, swapped, old, out):
-    core = position[3]
-    for q in range(4):
-        offsets = offsets_of(position, kq, q)
-        source = source_of(position, offsets)
-        for l in range(2):
-            third = (2 * core + l + offsets[2]) % 4
-            mine = third // 2 == core
-
-            @pl.when(mine)
-            def _(q=q, l=l, third=third, source=source):
-                out[q, l] = gathered[source, third % 2]
-
-            @pl.when(jnp.logical_not(mine))
-            def _(q=q, l=l):
-                out[q, l] = swapped[q, l]
-
-
-def left_kernel(position, kq, arrived, out):
+            for side, out in enumerate((kept, sent)):
+                owner = core if side == 0 else 1 - core
+                third = (2 * owner + l + offsets[2]) % 4
+                copies.append(
+                    pltpu.make_async_copy(
+                        gathered.at[source, third % 2], out.at[q, l], sems.at[side, q, l]
+                    )
+                )
+                copies[-1].start()
+    for copy in copies:
+        copy.wait()
+
+
+def left_kernel(position, kq, exchanged, *products_and_out):
+    products, out = products_and_out[:4], products_and_out[4]
     offsets = offsets_of(position, kq, position[0])
     carry = (position[1] // 2 + offsets[0]) // 2
-    for z in range(4):
-        plane = (z + carry) % 4
+    for shift in range(4):
+        plane = (position[0] - shift + 4 + carry) % 4
         for l in range(2):
-            gauge = arrived[plane, 4 + l]
-            pair = jnp.concatenate([arrived[z, 2 * l], arrived[z, 2 * l + 1]], -1)
+            gauge = exchanged[plane, l]
+            pair = jnp.concatenate([products[shift][l, 0], products[shift][l, 1]], -1)
             for b, wannier in enumerate(apply_left(gauge, pair)):
                 for part in range(2):
-                    start = (z * 2 + l) * 4 + part * 2 + b
+                    start = (part * 2 + b) * 8 + shift * 2 + l
                     out[pl.ds(start, 32, stride=32), :] = wannier[part * 32 : part * 32 + 32]
 
 
-def phase_kernel(coords, tables, high, low):
+def phase_kernel(position, coords, tables, high, low):
     real, imag = None, None
     for axis in range(3):
         divisions = lax.broadcasted_iota(jnp.int32, (FG, NK), 0)
-        onehot = (divisions == coords[axis : axis + 1, :]).astype(jnp.float32)
+        steps = coords[axis : axis + 1, :]
+        if axis == 0:
+            steps = (steps + (FG - 8 * position[0])) & (FG - 1)
+        onehot = (divisions == steps).astype(jnp.float32)
         factor = [
             lax.dot_general(
                 onehot,
@@ -157,13 +152,19 @@
 
 
 def fourier_kernel(high, low, columns, out):
-    parts = [columns[pl.ds(c, NK, stride=4), :] for c in range(4)]
+    step = pl.program_id(0)
+    parts = [columns[:, at : at + 8, :].reshape(NK, LANES) for at in (0, 8)]
     result = product((high[...], low[...]), halves(jnp.concatenate(parts, -1)), PLAIN)
     sign = signs(-1.0)
-    for c in range(4):
+    for c in range(2):
         at = c * LANES
         rolled = pltpu.roll(result[NK:, at : at + LANES], W, 1)
-        out[pl.ds(c, NK, stride=4), :] = result[:NK, at : at + LANES] + sign * rolled
+        value = result[:NK, at : at + LANES] + sign * rolled
+        for half in range(2):
+
+            @pl.when(step == half)
+            def _(half=half, c=c, value=value):
+                out[pl.ds(half * 2 + c, NK, stride=4), :] = value
 
 
 def bloch_kernel(frequency, arrived, eig_right, eig_left, energy_k, energy_kq, occupied, out):
@@ -211,7 +212,7 @@
     column = np.arange(NK)
     source, z, l = column // 8, column // 2 % 4, column % 2
     y, x, core = source // 8, source // 2 % 4, source % 2
-    coordinates = (2 * z + y // 2, (y % 2) * 4 + x, 2 * core + l)
+    coordinates = (2 * -z + y // 2, (y % 2) * 4 + x, 2 * core + l)
     tables = np.zeros((3, 2, FG, NK), np.float64)
     for axis, (size, where) in enumerate(zip((8, 8, 4), coordinates)):
         steps = np.arange(FG)[:, None] - (FG // size) * where[None, :]
@@ -222,18 +223,23 @@
     return tables.astype(np.float32)
 
 
-def call(kernel, shapes, specs, flops, **more):
+def call(kernel, shapes, specs, flops, vmem=16, **more):
     return pl.pallas_call(
         kernel,
         out_shape=shapes,
         in_specs=specs,
         cost_estimate=pl.CostEstimate(flops=flops, bytes_accessed=1 << 20, transcendentals=0),
+        compiler_params=pltpu.CompilerParams(vmem_limit_bytes=vmem << 20),
         **more,
     )
 
 
 def f32(*shape):
     return jax.ShapeDtypeStruct(shape, jnp.float32)
+
+
+def spread(products, shift):
+    return lax.ppermute(products, "z", [(z, (z + shift) % 4) for z in range(4)])
 
 
 def shards(
@@ -251,34 +257,46 @@
     position = jnp.stack([lax.axis_index(name) for name in (*KA, "pb")])
     to_all = jnp.broadcast_to(gauge[None], (16, 2, W, LANES))
     gathered = lax.all_to_all(to_all, ("y", "x"), 0, 0, tiled=True)
-    products = call(right_kernel, f32(4, 6, W, LANES), [VMEM, VMEM], 1 << 27)(coupling, gauge)
+    products = call(right_kernel, [f32(2, 2, W, LANES)] * 4, [SMEM, VMEM, VMEM], 1 << 27)(
+        position, coupling, gauge
+    )
+    products = [products[0]] + [
+        spread(products[shift], shift) for shift in (1, 2, 3)
+    ]
     high, low = call(
         phase_kernel,
         [jax.ShapeDtypeStruct((2 * NK, NK), jnp.bfloat16)] * 2,
-        [VMEM, VMEM],
+        [SMEM, VMEM, VMEM],
         1 << 28,
-    )(fine_coords, jnp.asarray(phase_tables()))
-    sent = call(send_kernel, f32(4, 2, W, LANES), [SMEM, SMEM, VMEM], 1 << 20)(
-        position, kq_index, gathered
-    )
+    )(position, fine_coords, jnp.asarray(phase_tables()))
+    kept, sent = call(
+        pick_kernel,
+        [f32(4, 2, W, LANES)] * 2,
+        [SMEM, SMEM, pl.BlockSpec(memory_space=pl.ANY)],
+        1 << 20,
+        scratch_shapes=[pltpu.SemaphoreType.DMA((2, 4, 2))],
+    )(position, kq_index, gathered)
     swapped = lax.ppermute(sent, "core", [(0, 1), (1, 0)])
-    filled = call(
-        keep_kernel,
-        f32(4, 6, W, LANES),
-        [SMEM, SMEM, VMEM, VMEM, pl.BlockSpec(memory_space=pl.ANY)],
-        1 << 20,
-        grid=(1,),
-        out_specs=pl.BlockSpec((4, 2, W, LANES), lambda i: (0, 2, 0, 0)),
-        input_output_aliases={4: 0},
-    )(position, kq_index, gathered, swapped, products)
-    arrived = lax.all_to_all(filled, "z", 0, 0, tiled=True)
-    pieces = call(left_kernel, f32(1024, LANES), [SMEM, SMEM, VMEM], 1 << 27)(
-        position, kq_index, arrived
+    own_kq = lax.dynamic_slice_in_dim(kq_index[:, 0], lax.axis_index("pb") * 4, 4)
+    thirds = (own_kq[:, None] % 4 + jnp.arange(2)[None, :]) % 4
+    mine = thirds // 2 == lax.axis_index("core")
+    chosen = jnp.where(mine[:, :, None, None], kept, swapped)
+    exchanged = lax.all_to_all(chosen, "z", 0, 0, tiled=True)
+    pieces = call(left_kernel, f32(1024, LANES), [SMEM, SMEM] + [VMEM] * 5, 1 << 27)(
+        position, kq_index, exchanged, *products
     )
     columns = lax.all_to_all(
         pieces.reshape(32, 32, LANES), ("y", "x", "core"), 0, 0, tiled=True
-    ).reshape(1024, LANES)
-    fine = call(fourier_kernel, f32(1024, LANES), [VMEM, VMEM, VMEM], 1 << 28)(high, low, columns)
+    )
+    fixed = pl.BlockSpec((2 * NK, NK), lambda i: (0, 0))
+    fine = call(
+        fourier_kernel,
+        f32(1024, LANES),
+        [fixed, fixed, pl.BlockSpec((32, 16, LANES), lambda i: (0, i, 0))],
+        1 << 28,
+        grid=(2,),
+        out_specs=pl.BlockSpec((1024, LANES), lambda i: (0, 0)),
+    )(high, low, columns)
     blocks = lax.all_to_all(fine.reshape(128, 8, LANES), KA, 0, 0, tiled=True)
     terms = call(bloch_kernel, f32(2, W), [SMEM] + [VMEM] * 6, 1 << 27)(
         frequency,

time: 135 us -> 126 us (0.933)
  blocking collectives: 44.1 us -> 17.5 us
  starting transfers between devices: 24.1 us -> 43.1 us
  waiting for transfers between devices: 38.5 us -> 48.2 us
  Pallas kernels: 19.2 us -> 11.5 us
  local copies, waits for them, and re-layouts: 7.76 us -> 2.94 us
    all_to_all x1 -> x0, blocking collectives: 25.7 us -> none  [shards(): arrived = lax.all_to_all(filled, 'z', 0, 0, tiled=True)]
    ppermute x0 -> x3, starting transfers between devices: none -> 10.5 us  [spread(): return lax.ppermute(products, 'z', [(z, (z + shift) % 4) for z in range(4)])]
    ppermute x0 -> x3, waiting for transfers between devices: none -> 5.94 us  [spread(): return lax.ppermute(products, 'z', [(z, (z + shift) % 4) for z in range(4)])]
    all_to_all x0 -> x1, starting transfers between devices: none -> 5.83 us  [shards(): exchanged = lax.all_to_all(chosen, 'z', 0, 0, tiled=True)]
    pallas_call x5 -> x4, Pallas kernels: 12.5 us -> 7.27 us  [the longest x1 2.5 us: shards(): call(left_kernel, f32(1024, LANES), [SMEM, SMEM] + [VMEM] * 5, 1 << 27)]
    unnamed x14 -> x24, local copies, waits for them, and re-layouts: 5.27 us -> 0.89 us
    all_to_all x1, starting transfers between devices: 6.04 us -> 7.61 us  [shards(): blocks = lax.all_to_all(fine.reshape(128, 8, LANES), KA, 0, 0, tiled=True)]
  transfers between devices with their start and end apart: 4 -> 8, of which waited for: 3 -> 5; matrix products, arithmetic and copies ran while one was open for 1% -> 0% of each run, Pallas kernels for 4% -> 2%
where the time goes in v2:
time: 126 us; the launch traced here: 124 us
  waiting for transfers between devices  48.2 us (38%)
  starting transfers between devices  43.1 us (34%)
  blocking collectives  17.5 us (14%)
  Pallas kernels  11.5 us (9%)
  local copies, waits for them, and re-layouts  2.94 us (2%)
    all_to_all x1, waiting for transfers between devices, shards(): blocks = lax.all_to_all(fine.reshape(128, 8, LANES), KA, 0, 0, tiled=True)  18.1 us
    psum x1, blocking collectives, shards(): return lax.psum(terms, 'pb')  17.5 us
    all_to_all x1, waiting for transfers between devices, shards(): gathered = lax.all_to_all(to_all, ('y', 'x'), 0, 0, tiled=True)  13.8 us
    ppermute x3, starting transfers between devices, spread(): return lax.ppermute(products, 'z', [(z, (z + shift) % 4) for z in range(4)])  10.5 us
    all_to_all x1, waiting for transfers between devices, shards(): lax.all_to_all(pieces.reshape(32, 32, LANES), ('y', 'x', 'core'), 0, 0, t...  9.48 us
    all_to_all x1, starting transfers between devices, shards(): blocks = lax.all_to_all(fine.reshape(128, 8, LANES), KA, 0, 0, tiled=True)  7.61 us
    all_to_all x1, starting transfers between devices, shards(): gathered = lax.all_to_all(to_all, ('y', 'x'), 0, 0, tiled=True)  7.57 us
    ppermute x3, waiting for transfers between devices, spread(): return lax.ppermute(products, 'z', [(z, (z + shift) % 4) for z in range(4)])  5.94 us
  transfers between devices with their start and end apart: 8, of which 5 were waited for; matrix products, arithmetic and copies ran while one was open for 0% of the time, Pallas kernels for 2%

profile of v2, /device:TPU:1, one launch (start us, length us, event | category | flops | bytes accessed | tf_op | source)
XLA Modules:
  0.0 124.5 jit_solution(14983920765069615402)
XLA Ops:
  0.0 2.0 %broadcast_in_dim.8 = f32[16,2,64,128]{3,2,1,0:T(8,128)} broadcast(f32[2,64,128]{2,1,0:T(8,128)} %gauge.1), dimensions={1,2,3} | broadcast | bytes 1114112 | tf_op jit(solution)/shard_map/broadcast_in_dim | solution.py:258
  2.0 7.6 %all-to-all-start = ((f32[16,2,64,128]{3,2,1,0:T(8,128)}), f32[16,2,64,128]{3,2,1,0:T(8,128)S(1)}, u32[]{:S(2)}, u32[]{:S(2)}) async-start(f32[16,2,64,128]{3,2,1,0:T(8,128)} %broadcast_in_dim.8), calls=%async_computation | async-start | bytes 2097152 | tf_op jit(solution)/shard_map/all_to_all | solution.py:259
  9.5 0.0 copy-start.9
  9.6 0.7 copy-done.9
  10.2 0.1 copy.13.kq
  10.3 0.1 stack.23.position
  10.4 13.8 %all-to-all-done.gathered = f32[16,2,64,128]{3,2,1,0:T(8,128)S(1)} async-done(((f32[16,2,64,128]{3,2,1,0:T(8,128)}), f32[16,2,64,128]{3,2,1,0:T(8,128)S(1)}, u32[]{:S(2)}, u32[]{:S(2)}) %all-to-all-start) | async-done | bytes 1048608 | tf_op jit(solution)/shard_map/all_to_all | solution.py:259
  24.2 1.8 %shard_map.110 = (f32[4,2,64,128]{3,2,1,0:T(8,128)S(1)}, f32[4,2,64,128]{3,2,1,0:T(8,128)S(1)}) custom-call(s32[5]{0:T(128)S(1)} %stack.23.position, s32[16,2]{1,0:T(8,128)S(1)} %copy.13.kq, f32[16,2,64,128]{3,2,1,0:T(8,128)S(1)} %all-to-all-done.gathered), custom_call_target="tpu_custom_call" | custom-call | flops 1048576 | bytes 1048576 | tf_op jit(solution)/shard_map/pallas_call | solution.py:272
  26.0 0.0 slice-start
  26.0 5.8 %collective-permute-start = (f32[4,2,64,128]{3,2,1,0:T(8,128)S(1)}, f32[4,2,64,128]{3,2,1,0:T(8,128)S(1)}, u32[]{:S(2)}, u32[]{:S(2)}) collective-permute-start(f32[4,2,64,128]{3,2,1,0:T(8,128)S(1)} %get-tuple-element.16), channel_id=1, source_target_pairs={{0,4},{4,0},{1,5},{5,1},{2,6},{6,2},{3,7},{7,3},{8,12},{12,8},{9,1... | collective-permute-start | bytes 786440 | tf_op jit(solution)/shard_map/ppermute | solution.py:279
  31.9 0.1 fusion.4
  31.9 0.1 fusion.2
  32.0 1.0 collective-permute-done
  33.0 0.8 broadcast_select_fusion
  33.8 5.8 %all-to-all-start.1 = ((f32[4,2,64,128]{3,2,1,0:T(8,128)}), f32[4,2,64,128]{3,2,1,0:T(8,128)S(1)}, u32[]{:S(2)}, u32[]{:S(2)}) async-start(f32[4,2,64,128]{3,2,1,0:T(8,128)} %broadcast_select_fusion), calls=%async_computation.1 | async-start | bytes 524288 | tf_op jit(solution)/shard_map/all_to_all | solution.py:284
  39.6 1.0 shard_map.111
  40.6 3.4 %collective-permute-start.1 = (f32[2,2,64,128]{3,2,1,0:T(8,128)S(1)}, f32[2,2,64,128]{3,2,1,0:T(8,128)S(1)}, u32[]{:S(2)}, u32[]{:S(2)}) collective-permute-start(f32[2,2,64,128]{3,2,1,0:T(8,128)S(1)} %get-tuple-element.18), channel_id=1, source_target_pairs={{0,128},{128,256},{256,384},{384,0},{1,129},{129,257},{257,385},{3... | collective-permute-start | bytes 393224 | tf_op jit(solution)/shard_map/ppermute | solution.py:242
  44.0 4.0 %collective-permute-start.2 = (f32[2,2,64,128]{3,2,1,0:T(8,128)S(1)}, f32[2,2,64,128]{3,2,1,0:T(8,128)S(1)}, u32[]{:S(2)}, u32[]{:S(2)}) collective-permute-start(f32[2,2,64,128]{3,2,1,0:T(8,128)S(1)} %get-tuple-element.19), channel_id=1, source_target_pairs={{0,256},{128,384},{256,0},{384,128},{1,257},{129,385},{257,1},{385... | collective-permute-start | bytes 393224 | tf_op jit(solution)/shard_map/ppermute | solution.py:242
  48.0 3.1 %collective-permute-start.3 = (f32[2,2,64,128]{3,2,1,0:T(8,128)S(1)}, f32[2,2,64,128]{3,2,1,0:T(8,128)S(1)}, u32[]{:S(2)}, u32[]{:S(2)}) collective-permute-start(f32[2,2,64,128]{3,2,1,0:T(8,128)S(1)} %get-tuple-element.20), channel_id=1, source_target_pairs={{0,384},{128,0},{256,128},{384,256},{1,385},{129,1},{257,129},{385... | collective-permute-start | bytes 393224 | tf_op jit(solution)/shard_map/ppermute | solution.py:242
  51.1 5.9 %collective-permute-done.2.products_and_out_2_ = f32[2,2,64,128]{3,2,1,0:T(8,128)S(1)} collective-permute-done((f32[2,2,64,128]{3,2,1,0:T(8,128)S(1)}, f32[2,2,64,128]{3,2,1,0:T(8,128)S(1)}, u32[]{:S(2)}, u32[]{:S(2)}) %collective-permute-start.2) | collective-permute-done | bytes 131104 | tf_op jit(solution)/shard_map/ppermute | solution.py:242
  57.0 2.5 %shard_map.112 = f32[1024,128]{1,0:T(8,128)} custom-call(s32[5]{0:T(128)S(1)} %stack.23.position, s32[16,2]{1,0:T(8,128)S(1)} %copy.13.kq, f32[4,2,64,128]{3,2,1,0:T(8,128)S(1)} %all-to-all-done.1.exchanged, f32[2,2,64,128]{3,2,1,0:T(8,128)S(1)} %get-tuple-element.17.products_and_out_0_, f32[2,2,64,128]{3,2,1,0:T(8,128)S(1)} %collective-permute-done.1.products_and_out_1_, ...), custom_call_target="tpu_custom_call" | custom-call | flops 134217728 | bytes 1048576 | tf_op jit(solution)/shard_map/pallas_call | solution.py:285
  59.5 5.8 %all-to-all-start.2 = ((f32[32,32,128]{2,1,0:T(8,128)}), f32[32,32,128]{2,1,0:T(8,128)S(1)}, u32[]{:S(2)}, u32[]{:S(2)}) async-start(f32[32,32,128]{2,1,0:T(8,128)} %bitcast.6), calls=%async_computation.2 | async-start | bytes 1048576 | tf_op jit(solution)/shard_map/all_to_all | solution.py:288
  65.3 2.0 %shard_map.109 = (bf16[512,256]{1,0:T(8,128)(2,1)S(1)}, bf16[512,256]{1,0:T(8,128)(2,1)S(1)}) custom-call(s32[5]{0:T(128)S(1)} %stack.23.position, s32[3,256]{1,0:T(4,128)S(1)} %copy-done.7, f32[3,2,32,256]{3,2,1,0:T(8,128)S(1)} %copy-done.8), custom_call_target="tpu_custom_call" | custom-call | flops 268435456 | bytes 1048576 | tf_op jit(solution)/shard_map/pallas_call | solution.py:266
  67.4 9.5 %all-to-all-done.2.columns = f32[32,32,128]{2,1,0:T(8,128)S(1)} async-done(((f32[32,32,128]{2,1,0:T(8,128)}), f32[32,32,128]{2,1,0:T(8,128)S(1)}, u32[]{:S(2)}, u32[]{:S(2)}) %all-to-all-start.2) | async-done | bytes 524320 | tf_op jit(solution)/shard_map/all_to_all | solution.py:288
  76.9 2.0 %shard_map.113 = f32[1024,128]{1,0:T(8,128)} custom-call(bf16[512,256]{1,0:T(8,128)(2,1)S(1)} %get-tuple-element.13.high, bf16[512,256]{1,0:T(8,128)(2,1)S(1)} %get-tuple-element.14.low, f32[32,32,128]{2,1,0:T(8,128)S(1)} %all-to-all-done.2.columns), custom_call_target="tpu_custom_call" | custom-call | flops 268435456 | bytes 1048576 | tf_op jit(solution)/shard_map/pallas_call | solution.py:292
  78.9 7.6 %all-to-all-start.3 = ((f32[128,8,128]{2,1,0:T(8,128)}), f32[128,8,128]{2,1,0:T(8,128)S(1)}, u32[]{:S(2)}, u32[]{:S(2)}) async-start(f32[128,8,128]{2,1,0:T(8,128)} %bitcast.7), calls=%async_computation.3 | async-start | bytes 1048576 | tf_op jit(solution)/shard_map/all_to_all | solution.py:300
  86.5 0.0 copy-start.4
  86.5 0.0 copy-start.5
  86.5 0.1 copy.14.frequency
  86.6 18.1 %all-to-all-done.3 = f32[128,8,128]{2,1,0:T(8,128)S(1)} async-done(((f32[128,8,128]{2,1,0:T(8,128)}), f32[128,8,128]{2,1,0:T(8,128)S(1)}, u32[]{:S(2)}, u32[]{:S(2)}) %all-to-all-start.3) | async-done | bytes 524320 | tf_op jit(solution)/shard_map/all_to_all | solution.py:300
  104.7 2.2 %shard_map.114 = f32[2,64]{1,0:T(2,128)S(1)} custom-call(f32[4,2]{1,0:T(4,128)S(1)} %copy.14.frequency, f32[1024,128]{1,0:T(8,128)S(1)} %bitcast.12, f32[2,64,128]{2,1,0:T(8,128)S(1)} %copy-done.3, f32[2,4,64,128]{3,2,1,0:T(8,128)S(1)} %copy-done.1, f32[2,64]{1,0:T(2,128)S(1)} %copy-done.6, f32[8,64]{1,0:T(8,128)S(1)} %bitcast.13, s32[8,64]{1,0:T(8,128)S(1)} %bitcast.14), custom_call_target="tpu_custom_call" | custom-call | flops 134217728 | bytes 1048576 | tf_op jit(solution)/shard_map/pallas_call | solution.py:301
  106.9 17.5 %psum.7 = f32[2,64]{1,0:T(2,128)} all-reduce(f32[2,64]{1,0:T(2,128)S(1)} %shard_map.114), channel_id=1, replica_groups=mesh['z'=4,'y'=4,'x'=4,'core'=2,'pb'=4] {'pb'}, use_global_device_ids=true, to_apply=%region_0.1 | all-reduce | flops 128 | bytes 1024 | tf_op jit(solution)/shard_map/psum | solution.py:310
  (22 shorter events, 0.0 us)
Async XLA Ops:
  2.0 22.2 %all-to-all-start = ((f32[16,2,64,128]{3,2,1,0:T(8,128)}), f32[16,2,64,128]{3,2,1,0:T(8,128)S(1)}, u32[]{:S(2)}, u32[]{:S(2)}) async-start(f32[16,2,64,128]{3,2,1,0:T(8,128)} %broadcast_in_dim.8), calls=%async_computation | async-start | bytes 2097152 | tf_op jit(solution)/shard_map/all_to_all | solution.py:259
  9.5 0.7 copy-start.9
  26.0 5.9 %slice-start = ((s32[16,2]{0,1:T(2,128)}), s32[16,1]{0,1:T(1,128)S(1)}, s32[]{:S(2)}) async-start(s32[16,2]{0,1:T(2,128)} %param.13), calls=%async_computation.4 | async-start | bytes 1024 | tf_op jit(solution)/shard_map/slice | solution.py:280
  26.0 7.0 %collective-permute-start = (f32[4,2,64,128]{3,2,1,0:T(8,128)S(1)}, f32[4,2,64,128]{3,2,1,0:T(8,128)S(1)}, u32[]{:S(2)}, u32[]{:S(2)}) collective-permute-start(f32[4,2,64,128]{3,2,1,0:T(8,128)S(1)} %get-tuple-element.16), channel_id=1, source_target_pairs={{0,4},{4,0},{1,5},{5,1},{2,6},{6,2},{3,7},{7,3},{8,12},{12,8},{9,1... | collective-permute-start | bytes 786440 | tf_op jit(solution)/shard_map/ppermute | solution.py:279
  33.0 6.6 %copy-start = (f32[2,4,2,64,128]{4,3,2,1,0:T(8,128)S(1)}, f32[2,4,2,64,128]{4,3,2,1,0:T(8,128)}, u32[]{:S(2)}) copy-start(f32[2,4,2,64,128]{4,3,2,1,0:T(8,128)} %coupling.1) | copy-start | bytes 1572868
  33.8 5.8 %copy-start.2 = (f32[2,64,128]{2,1,0:T(8,128)S(1)}, f32[2,64,128]{2,1,0:T(8,128)}, u32[]{:S(2)}) copy-start(f32[2,64,128]{2,1,0:T(8,128)} %gauge.1) | copy-start | bytes 196612
  33.8 23.2 %all-to-all-start.1 = ((f32[4,2,64,128]{3,2,1,0:T(8,128)}), f32[4,2,64,128]{3,2,1,0:T(8,128)S(1)}, u32[]{:S(2)}, u32[]{:S(2)}) async-start(f32[4,2,64,128]{3,2,1,0:T(8,128)} %broadcast_select_fusion), calls=%async_computation.1 | async-start | bytes 524288 | tf_op jit(solution)/shard_map/all_to_all | solution.py:284
  40.6 10.5 %collective-permute-start.1 = (f32[2,2,64,128]{3,2,1,0:T(8,128)S(1)}, f32[2,2,64,128]{3,2,1,0:T(8,128)S(1)}, u32[]{:S(2)}, u32[]{:S(2)}) collective-permute-start(f32[2,2,64,128]{3,2,1,0:T(8,128)S(1)} %get-tuple-element.18), channel_id=1, source_target_pairs={{0,128},{128,256},{256,384},{384,0},{1,129},{129,257},{257,385},{3... | collective-permute-start | bytes 393224 | tf_op jit(solution)/shard_map/ppermute | solution.py:242
  44.0 13.0 %collective-permute-start.2 = (f32[2,2,64,128]{3,2,1,0:T(8,128)S(1)}, f32[2,2,64,128]{3,2,1,0:T(8,128)S(1)}, u32[]{:S(2)}, u32[]{:S(2)}) collective-permute-start(f32[2,2,64,128]{3,2,1,0:T(8,128)S(1)} %get-tuple-element.19), channel_id=1, source_target_pairs={{0,256},{128,384},{256,0},{384,128},{1,257},{129,385},{257,1},{385... | collective-permute-start | bytes 393224 | tf_op jit(solution)/shard_map/ppermute | solution.py:242
  48.0 9.0 %collective-permute-start.3 = (f32[2,2,64,128]{3,2,1,0:T(8,128)S(1)}, f32[2,2,64,128]{3,2,1,0:T(8,128)S(1)}, u32[]{:S(2)}, u32[]{:S(2)}) collective-permute-start(f32[2,2,64,128]{3,2,1,0:T(8,128)S(1)} %get-tuple-element.20), channel_id=1, source_target_pairs={{0,384},{128,0},{256,128},{384,256},{1,385},{129,1},{257,129},{385... | collective-permute-start | bytes 393224 | tf_op jit(solution)/shard_map/ppermute | solution.py:242
  59.5 5.8 %copy-start.7 = (s32[3,256]{1,0:T(4,128)S(1)}, s32[3,256]{1,0:T(4,128)}, u32[]{:S(2)}) copy-start(s32[3,256]{1,0:T(4,128)} %coords.1) | copy-start | bytes 9220
  59.5 5.8 %copy-start.8 = (f32[3,2,32,256]{3,2,1,0:T(8,128)S(1)}, f32[3,2,32,256]{3,2,1,0:T(8,128)}, u32[]{:S(2)}) copy-start(f32[3,2,32,256]{3,2,1,0:T(8,128)} %constant.62.clone.tables) | copy-start | bytes 589828
  59.5 17.3 %all-to-all-start.2 = ((f32[32,32,128]{2,1,0:T(8,128)}), f32[32,32,128]{2,1,0:T(8,128)S(1)}, u32[]{:S(2)}, u32[]{:S(2)}) async-start(f32[32,32,128]{2,1,0:T(8,128)} %bitcast.6), calls=%async_computation.2 | async-start | bytes 1048576 | tf_op jit(solution)/shard_map/all_to_all | solution.py:288
  78.8 7.6 %copy-start.10 = (f32[4,2]{0,1:T(2,128)S(1)}, f32[4,2]{0,1:T(2,128)}, u32[]{:S(2)}) copy-start(f32[4,2]{0,1:T(2,128)} %param.20) | copy-start | bytes 100
  78.9 25.8 %copy-start.1 = (f32[2,4,64,128]{3,2,1,0:T(8,128)S(1)}, f32[2,4,64,128]{3,2,1,0:T(8,128)}, u32[]{:S(2)}) copy-start(f32[2,4,64,128]{3,2,1,0:T(8,128)} %eig_left.1) | copy-start | bytes 786436
  78.9 25.8 %copy-start.3 = (f32[2,64,128]{2,1,0:T(8,128)S(1)}, f32[2,64,128]{2,1,0:T(8,128)}, u32[]{:S(2)}) copy-start(f32[2,64,128]{2,1,0:T(8,128)} %eig_right.1) | copy-start | bytes 196612
  78.9 25.8 %copy-start.6 = (f32[2,64]{1,0:T(2,128)S(1)}, f32[2,64]{1,0:T(2,128)}, u32[]{:S(2)}) copy-start(f32[2,64]{1,0:T(2,128)} %energy_k.1) | copy-start | bytes 1540
  78.9 25.8 %all-to-all-start.3 = ((f32[128,8,128]{2,1,0:T(8,128)}), f32[128,8,128]{2,1,0:T(8,128)S(1)}, u32[]{:S(2)}, u32[]{:S(2)}) async-start(f32[128,8,128]{2,1,0:T(8,128)} %bitcast.7), calls=%async_computation.3 | async-start | bytes 1048576 | tf_op jit(solution)/shard_map/all_to_all | solution.py:300
  86.5 18.2 %copy-start.4 = (f32[2,4,64]{2,1,0:T(4,128)S(1)}, f32[2,4,64]{2,1,0:T(4,128)}, u32[]{:S(2)}) copy-start(f32[2,4,64]{2,1,0:T(4,128)} %param.18) | copy-start | bytes 6148
  86.5 18.2 %copy-start.5 = (s32[2,4,64]{2,1,0:T(4,128)S(1)}, s32[2,4,64]{2,1,0:T(4,128)}, u32[]{:S(2)}) copy-start(s32[2,4,64]{2,1,0:T(4,128)} %param.19) | copy-start | bytes 6148

commit v3 on v2

v3 whole, which is shorter than its diff:
```python
import functools
import math

import jax
import jax.numpy as jnp
import numpy as np
from jax import lax
from jax.experimental import pallas as pl
from jax.experimental.pallas import tpu as pltpu
from jax.sharding import Mesh
from jax.sharding import PartitionSpec as P

FG = 32
W = 64
LANES = 128
NK = 256
BROADEN = 0.1
THERMAL = 0.05
KA = ("z", "y", "x", "core")
VMEM = pl.BlockSpec(memory_space=pltpu.VMEM)
SMEM = pl.BlockSpec(memory_space=pltpu.SMEM)
CONTRACT_ROWS = (((0,), (0,)), ((), ()))
PLAIN = (((1,), (0,)), ((), ()))


def halves(value):
    high = value.astype(jnp.bfloat16)
    low = (value - high.astype(jnp.float32)).astype(jnp.bfloat16)
    return high, low


def product(left, right, dims):
    left_high, left_low = left
    right_high, right_low = right
    dot = functools.partial(lax.dot_general, dimension_numbers=dims, preferred_element_type=jnp.float32)
    return dot(left_high, right_high) + (dot(left_high, right_low) + dot(left_low, right_high))


def right_block(matrix):
    real_part = matrix[:, :W]
    imag_part = matrix[:, W:]
    upper = jnp.concatenate([real_part, imag_part], -1)
    lower = jnp.concatenate([-imag_part, real_part], -1)
    return jnp.concatenate([upper, lower], 0)


def signs(first):
    lane = lax.broadcasted_iota(jnp.int32, (1, LANES), 1)
    return jnp.where(lane < W, first, -first)


def apply_left(left, right_pair):
    both = product(halves(left), halves(right_pair), CONTRACT_ROWS)
    sign = signs(1.0)
    return [
        both[:W, at : at + LANES] + sign * pltpu.roll(both[W:, at : at + LANES], W, 1)
        for at in (0, LANES)
    ]


def offsets_of(position, kq, qpoint):
    along_z, along_y, along_x, core = (position[i] for i in range(4))
    first = 2 * along_z + (along_y >> 1)
    second = ((along_y & 1) << 2) + along_x
    target = kq[(position[4] << 2) + qpoint, 0]
    return (
        ((target >> 5) - first) & 7,
        ((target >> 2) - second) & 7,
        (target - 2 * core) & 3,
    )


def translation(number):
    along_second, along_first = number % 8, number // 8
    pairs = []
    for y in range(4):
        for x in range(4):
            second = ((y % 2) * 4 + x + along_second) % 8
            first = (y // 2 + along_first) % 2
            pairs.append(((first * 2 + second // 4) * 4 + second % 4, y * 4 + x))
    return pairs


def translated(value, number):
    pairs = translation(number)
    if all(source == target for source, target in pairs):
        return value
    return lax.ppermute(value, ("y", "x"), pairs)


def right_kernel(position, coupling, gauge, *outs):
    for k in range(2):
        block = halves(right_block(gauge[k]))
        for shift, out in enumerate(outs):
            rows = coupling[k, (position[0] + shift) & 3].reshape(-1, LANES)
            out[k] = product(halves(rows), block, PLAIN).reshape(2, W, LANES)


def pack_kernel(position, eig_left, eig_right, energy_k, energy_kq, occupied, *outs):
    for shift, out in enumerate(outs):
        q = (position[0] + shift) & 3
        for f in range(2):
            out[f * W : f * W + W] = eig_left[f, q]
            out[LANES + f * W : LANES + f * W + W] = eig_right[f]
            filled = occupied[f, pl.ds(q, 1), :].astype(jnp.float32)
            row = 2 * LANES + f
            out[row : row + 1] = jnp.concatenate([energy_k[f : f + 1], energy_k[f : f + 1]], -1)
            out[row + 2 : row + 3] = jnp.concatenate([energy_kq[f, pl.ds(q, 1), :], filled], -1)
        out[2 * LANES + 4 :] = jnp.zeros((4, LANES), jnp.float32)


def left_kernel(position, kq, kept, swapped, *products_and_out):
    products, out = products_and_out[:4], products_and_out[4]
    core = position[3]
    offsets = offsets_of(position, kq, position[0])
    carry = ((position[1] >> 1) + offsets[0]) >> 1
    for l in range(2):
        third = (2 * core + l + offsets[2]) & 3
        mine = (third >> 1) == core
        for shift in range(4):
            plane = (position[0] - shift + 4 + carry) & 3
            gauge = jnp.where(mine, kept[plane, third & 1], swapped[plane, third & 1])
            pair = jnp.concatenate([products[shift][l, 0], products[shift][l, 1]], -1)
            for b, wannier in enumerate(apply_left(gauge, pair)):
                for part in range(2):
                    start = (part * 2 + b) * 8 + shift * 2 + l
                    out[pl.ds(start, 32, stride=32), :] = wannier[part * 32 : part * 32 + 32]


def phase_kernel(position, coords, tables, high, low):
    real, imag = None, None
    turned = pltpu.roll(coords[...], (NK - W * position[0]) & (NK - 1), 1)
    for axis in range(3):
        divisions = lax.broadcasted_iota(jnp.int32, (FG, NK), 0)
        steps = turned[axis : axis + 1, :]
        if axis == 0:
            steps = (steps + (FG - 8 * position[0])) & (FG - 1)
        onehot = (divisions == steps).astype(jnp.float32)
        factor = [
            lax.dot_general(
                onehot,
                tables[axis, part],
                CONTRACT_ROWS,
                precision=lax.Precision.HIGHEST,
                preferred_element_type=jnp.float32,
            )
            for part in range(2)
        ]
        if real is None:
            real, imag = factor
        else:
            real, imag = (
                real * factor[0] - imag * factor[1],
                real * factor[1] + imag * factor[0],
            )
    for row, part in enumerate((real, imag)):
        part_high, part_low = halves(part)
        high[row * NK : row * NK + NK] = part_high
        low[row * NK : row * NK + NK] = part_low


def fourier_kernel(high, low, columns, out):
    step = pl.program_id(0)
    parts = [columns[:, at : at + 8, :].reshape(NK, LANES) for at in (0, 8)]
    result = product((high[...], low[...]), halves(jnp.concatenate(parts, -1)), PLAIN)
    sign = signs(-1.0)
    for c in range(2):
        at = c * LANES
        rolled = pltpu.roll(result[NK:, at : at + LANES], W, 1)
        value = result[:NK, at : at + LANES] + sign * rolled
        for half in range(2):

            @pl.when(step == half)
            def _(half=half, c=c, value=value):
                for block in range(8):
                    start = block * 4 + half * 2 + c
                    out[pl.ds(start, 32, stride=32), :] = value[block * 32 : block * 32 + 32]


def bloch_kernel(position, frequency, arrived, *packs_and_out):
    packs, out = packs_and_out[:4], packs_and_out[4]
    lane = lax.broadcasted_iota(jnp.int32, (1, LANES), 1)
    first = lane < W
    phonons = [
        jnp.full((1, LANES), frequency[position[0], b], jnp.float32) for b in range(2)
    ]
    boses = [1.0 / (jnp.exp(phonon / THERMAL) - 1.0) for phonon in phonons]
    for shift, pack in enumerate(packs):
        tail = pack[2 * LANES :]
        energies = jnp.where(first, tail[0:1], tail[1:2])
        states = tail.T
        energy_left = jnp.where(first, states[:W, 2:3], states[:W, 3:4])
        filled = jnp.where(first, states[W:, 2:3], states[W:, 3:4])
        gap = energies - energy_left
        strengths = []
        for f in range(2):
            rows = [
                arrived[pl.ds((-shift % 4 * 2 + f) * 4 + part * 2 + b, 32, stride=32), :]
                for b in range(2)
                for part in range(2)
            ]
            eig_right = pack[LANES + f * W : LANES + f * W + W]
            half = product(
                halves(jnp.concatenate(rows, 0)), halves(right_block(eig_right)), PLAIN
            )
            pair = jnp.concatenate([half[:W], half[W:]], -1)
            blochs = apply_left(pack[f * W : f * W + W], pair)
            squares = [bloch * bloch for bloch in blochs]
            strengths.append([square + pltpu.roll(square, W, 1) for square in squares])
        total = jnp.zeros((W, LANES), jnp.float32)
        for b, (phonon, bose) in enumerate(zip(phonons, boses)):
            up = gap + phonon
            down = gap - phonon
            kernel = (bose + filled) * up / (up * up + BROADEN * BROADEN)
            kernel = kernel + (bose + 1.0 - filled) * down / (down * down + BROADEN * BROADEN)
            strength = jnp.where(first, strengths[0][b], strengths[1][b])
            total = total + strength / (2.0 * phonon) * kernel
        summed = jnp.sum(total, axis=0, keepdims=True) * (1.0 / 1024.0)
        plane = (position[0] - shift + 4) & 3
        for group in range(4):
            out[plane * 4 + group] = summed


def sum_kernel(terms, out):
    summed = jnp.sum(terms[...], axis=0)
    out[0:1] = summed[:, :W]
    out[1:2] = summed[:, W:]


def phase_tables():
    column = np.arange(NK)
    source, z, l = column // 8, column // 2 % 4, column % 2
    y, x, core = source // 8, source // 2 % 4, source % 2
    coordinates = (2 * -z + y // 2, (y % 2) * 4 + x, 2 * core + l)
    tables = np.zeros((3, 2, FG, NK), np.float64)
    for axis, (size, where) in enumerate(zip((8, 8, 4), coordinates)):
        steps = np.arange(FG)[:, None] - (FG // size) * where[None, :]
        for cell in range(-size // 2, size // 2):
            angle = 2.0 * math.pi * ((cell * steps) % FG) / FG
            tables[axis, 0] += np.cos(angle) / size
            tables[axis, 1] += np.sin(angle) / size
    return tables.astype(np.float32)


def call(kernel, shapes, specs, flops, vmem=16, **more):
    return pl.pallas_call(
        kernel,
        out_shape=shapes,
        in_specs=specs,
        cost_estimate=pl.CostEstimate(flops=flops, bytes_accessed=1 << 20, transcendentals=0),
        compiler_params=pltpu.CompilerParams(vmem_limit_bytes=vmem << 20),
        **more,
    )


def f32(*shape):
    return jax.ShapeDtypeStruct(shape, jnp.float32)


def spread(values):
    arrived = [values[0]]
    for shift in (1, 2, 3):
        pairs = [(z, (z + shift) % 4) for z in range(4)]
        arrived.append(lax.ppermute(values[shift], "z", pairs))
    return arrived


def shards(
    coupling,
    gauge,
    kq_index,
    fine_coords,
    eig_right,
    eig_left,
    energy_k,
    energy_kq,
    occupied,
    frequency,
):
    along_z, along_y, along_x, _, pb = (lax.axis_index(name) for name in (*KA, "pb"))
    position = jnp.stack([lax.axis_index(name) for name in (*KA, "pb")])
    planes = lax.all_to_all(jnp.broadcast_to(gauge[None], (4, 2, W, LANES)), "z", 0, 0, tiled=True)
    products = call(right_kernel, [f32(2, 2, W, LANES)] * 4, [SMEM, VMEM, VMEM], 1 << 27)(
        position, coupling, gauge
    )
    products = spread(products)
    packs = call(pack_kernel, [f32(264, LANES)] * 4, [SMEM] + [VMEM] * 5, 1 << 20)(
        position, eig_left, eig_right, energy_k, energy_kq, occupied
    )
    target = kq_index[pb * 4 + along_z, 0]
    number = (((target >> 2) - (along_y * 4 + along_x)) & 7) + (
        (((target >> 5) - (along_y >> 1)) & 1) << 3
    )
    branches = [functools.partial(translated, number=number) for number in range(16)]
    kept = lax.switch(number, branches, planes)
    swapped = lax.ppermute(kept, "core", [(0, 1), (1, 0)])
    pieces = call(left_kernel, f32(1024, LANES), [SMEM, SMEM] + [VMEM] * 6, 1 << 27)(
        position, kq_index, kept, swapped, *products
    )
    columns = lax.all_to_all(pieces.reshape(32, 32, LANES), ("y", "x", "core"), 0, 0, tiled=True)
    packs = spread(packs)
    coords = fine_coords.reshape(3, 4, 32, 2).transpose(0, 1, 3, 2).reshape(3, NK)
    coords = jnp.pad(coords, ((0, 5), (0, 0)))
    high, low = call(
        phase_kernel,
        [jax.ShapeDtypeStruct((2 * NK, NK), jnp.bfloat16)] * 2,
        [SMEM, VMEM, VMEM],
        1 << 28,
    )(position, coords, jnp.asarray(phase_tables()))
    fixed = pl.BlockSpec((2 * NK, NK), lambda i: (0, 0))
    fine = call(
        fourier_kernel,
        f32(1024, LANES),
        [fixed, fixed, pl.BlockSpec((32, 16, LANES), lambda i: (0, i, 0))],
        1 << 28,
        grid=(2,),
        out_specs=pl.BlockSpec((1024, LANES), lambda i: (0, 0)),
    )(high, low, columns)
    blocks = lax.all_to_all(fine.reshape(32, 32, LANES), ("y", "x", "core"), 0, 0, tiled=True)
    terms = call(bloch_kernel, f32(16, 1, LANES), [SMEM, SMEM] + [VMEM] * 5, 1 << 27)(
        position, frequency, blocks.reshape(1024, LANES), *packs
    )
    terms = lax.all_to_all(terms, ("z", "pb"), 0, 0, tiled=True)
    return call(sum_kernel, f32(2, W), [VMEM], 1 << 12)(terms)


def solution(mesh):
    split = Mesh(mesh.devices.reshape(4, 4, 4, 2, mesh.shape["pb"]), (*KA, "pb"))
    return jax.shard_map(
        shards,
        mesh=split,
        in_specs=(
            P(KA, "pb", None, None, None),
            P(KA, None, None),
            P(None, KA),
            P(),
            P(KA, None, None),
            P(KA, "pb", None, None),
            P(KA, None),
            P(KA, "pb", None),
            P(KA, "pb", None),
            P("pb", None),
        ),
        out_specs=P(KA, None),
        check_vma=False,
    )
```

time: 126 us -> 120 us (0.952)
  waiting for transfers between devices: 48.2 us -> 28.3 us
  starting transfers between devices: 43.1 us -> 50.2 us
  blocking collectives: 17.5 us -> 22.2 us
  between operations: 0.19 us -> 1.61 us
    all_to_all x3 -> x2, waiting for transfers between devices: 31.8 us -> 2.87 us  [the longest x1 2.87 us: shards(): lax.all_to_all(jnp.broadcast_to(gauge[None], (4, 2, W, LANES)), 'z', 0, 0...]
    all_to_all x0 -> x1, blocking collectives: none -> 22.2 us  [shards(): terms = lax.all_to_all(terms, ('z', 'pb'), 0, 0, tiled=True)]
    psum x1 -> x0, blocking collectives: 17.5 us -> none  [shards(): return lax.psum(terms, 'pb')]
    ppermute x4 -> x8, starting transfers between devices: 16.3 us -> 31.5 us  [the longest x6 18 us: spread(): arrived.append(lax.ppermute(values[shift], 'z', pairs))]
    all_to_all x3 -> x2, starting transfers between devices: 21 us -> 10.5 us  [the longest x1 6.43 us: shards(): lax.all_to_all(jnp.broadcast_to(gauge[None], (4, 2, W, LANES)), 'z', 0, 0...]
    ppermute x4 -> x8, waiting for transfers between devices: 6.9 us -> 17.1 us  [the longest x6 13.8 us: spread(): arrived.append(lax.ppermute(values[shift], 'z', pairs))]
    all_to_all x1, starting transfers between devices: 5.78 us -> 8.24 us  [shards(): lax.all_to_all(pieces.reshape(32, 32, LANES), ('y', 'x', 'core'), 0, 0, t...]
    pallas_call x3 -> x4, Pallas kernels: 6.55 us -> 6.16 us  [the longest x1 2.44 us: shards(): call(left_kernel, f32(1024, LANES), [SMEM, SMEM] + [VMEM] * 6, 1 << 27)]
  transfers between devices with their start and end apart: 8 -> 11, of which waited for: 5 -> 7; matrix products, arithmetic and copies ran while one was open for 0% -> 1% of each run, Pallas kernels for 2% -> 3%
where the time goes in v3:
time: 120 us; the launch traced here: 118 us
  starting transfers between devices  50.2 us (42%)
  waiting for transfers between devices  28.3 us (24%)
  blocking collectives  22.2 us (18%)
  Pallas kernels  11.5 us (10%)
  local copies, waits for them, and re-layouts  3.47 us (3%)
  between operations  1.61 us (1%)
    all_to_all x1, blocking collectives, shards(): terms = lax.all_to_all(terms, ('z', 'pb'), 0, 0, tiled=True)  22.2 us
    ppermute x6, starting transfers between devices, spread(): arrived.append(lax.ppermute(values[shift], 'z', pairs))  18 us
    ppermute x6, waiting for transfers between devices, spread(): arrived.append(lax.ppermute(values[shift], 'z', pairs))  13.8 us
    all_to_all x1, waiting for transfers between devices, shards(): lax.all_to_all(pieces.reshape(32, 32, LANES), ('y', 'x', 'core'), 0, 0, t...  8.38 us
    all_to_all x1, starting transfers between devices, shards(): lax.all_to_all(pieces.reshape(32, 32, LANES), ('y', 'x', 'core'), 0, 0, t...  8.24 us
    ppermute x1, starting transfers between devices, translated(): return lax.ppermute(value, ('y', 'x'), pairs)  7.72 us
    all_to_all x1, starting transfers between devices, shards(): lax.all_to_all(jnp.broadcast_to(gauge[None], (4, 2, W, LANES)), 'z', 0, 0...  6.43 us
    ppermute x1, starting transfers between devices, shards(): swapped = lax.ppermute(kept, 'core', [(0, 1), (1, 0)])  5.7 us
  transfers between devices with their start and end apart: 11, of which 7 were waited for; matrix products, arithmetic and copies ran while one was open for 1% of the time, Pallas kernels for 3%

profile of v3, /device:TPU:1, one launch (start us, length us, event | category | flops | bytes accessed | tf_op | source)
XLA Modules:
  0.0 118.0 jit_solution(774619243293153296)
XLA Ops:
  0.0 1.6 %broadcast_in_dim.2 = f32[4,2,64,128]{3,2,1,0:T(8,128)} broadcast(f32[2,64,128]{2,1,0:T(8,128)} %gauge.1), dimensions={1,2,3} | broadcast | bytes 327680 | tf_op jit(solution)/shard_map/broadcast_in_dim | solution.py:282
  1.6 6.4 %all-to-all-start = ((f32[4,2,64,128]{3,2,1,0:T(8,128)}), f32[4,2,64,128]{3,2,1,0:T(8,128)S(1)}, u32[]{:S(2)}, u32[]{:S(2)}) async-start(f32[4,2,64,128]{3,2,1,0:T(8,128)} %broadcast_in_dim.2), calls=%async_computation | async-start | bytes 524288 | tf_op jit(solution)/shard_map/all_to_all | solution.py:282
  8.0 0.7 copy-done.9
  8.7 0.7 fusion
  10.7 2.9 %all-to-all-done = f32[4,2,64,128]{3,2,1,0:T(8,128)S(1)} async-done(((f32[4,2,64,128]{3,2,1,0:T(8,128)}), f32[4,2,64,128]{3,2,1,0:T(8,128)S(1)}, u32[]{:S(2)}, u32[]{:S(2)}) %all-to-all-start) | async-done | bytes 262176 | tf_op jit(solution)/shard_map/all_to_all | solution.py:282
  13.6 11.1 %conditional.1 = (f32[4,2,64,128]{3,2,1,0:T(8,128)S(1)}) conditional(s32[]{:T(128)} %clamp.3, f32[4,2,64,128]{3,2,1,0:T(8,128)S(1)} %all-to-all-done, f32[4,2,64,128]{3,2,1,0:T(8,128)S(1)} %all-to-all-done, f32[4,2,64,128]{3,2,1,0:T(8,128)S(1)} %all-to-all-done, f32[4,2,64,128]{3,2,1,0:T(8,128)S(1)} %all-to-all-done, ...), branch_computations={%region_0.0_spmd, %region_1.0_spmd, %region_2.0_spmd, %region_3.0_... | conditional | bytes 1572912 | solution.py:295
  13.6 7.7 %collective-permute-start.1 = (f32[4,2,64,128]{3,2,1,0:T(8,128)S(1)}, f32[4,2,64,128]{3,2,1,0:T(8,128)S(1)}, u32[]{:S(2)}, u32[]{:S(2)}) collective-permute-start(f32[4,2,64,128]{3,2,1,0:T(8,128)S(1)} %param.2), channel_id=1, source_target_pairs={{16,0},{24,8},{32,16},{40,24},{48,32},{56,40},{0,48},{8,56},{80,64... | collective-permute-start | bytes 786440 | tf_op jit(solution)/shard_map/cond/branch_2_fun/ppermute | solution.py:88
  21.4 3.3 %collective-permute-done.1 = f32[4,2,64,128]{3,2,1,0:T(8,128)S(1)} collective-permute-done((f32[4,2,64,128]{3,2,1,0:T(8,128)S(1)}, f32[4,2,64,128]{3,2,1,0:T(8,128)S(1)}, u32[]{:S(2)}, u32[]{:S(2)}) %collective-permute-start.1) | collective-permute-done | bytes 262176 | tf_op jit(solution)/shard_map/cond/branch_2_fun/ppermute | solution.py:88
  24.7 5.7 %collective-permute-start.15 = (f32[4,2,64,128]{3,2,1,0:T(8,128)S(1)}, f32[4,2,64,128]{3,2,1,0:T(8,128)S(1)}, u32[]{:S(2)}, u32[]{:S(2)}) collective-permute-start(f32[4,2,64,128]{3,2,1,0:T(8,128)S(1)} %get-tuple-element.60.kept), channel_id=1, source_target_pairs={{0,4},{4,0},{1,5},{5,1},{2,6},{6,2},{3,7},{7,3},{8,12},{12,8},{9,1... | collective-permute-start | bytes 786440 | tf_op jit(solution)/shard_map/ppermute | solution.py:296
  30.5 1.0 shard_map.110
  31.5 1.9 %collective-permute-start.16 = (f32[2,2,64,128]{3,2,1,0:T(8,128)S(1)}, f32[2,2,64,128]{3,2,1,0:T(8,128)S(1)}, u32[]{:S(2)}, u32[]{:S(2)}) collective-permute-start(f32[2,2,64,128]{3,2,1,0:T(8,128)S(1)} %get-tuple-element.51), channel_id=1, source_target_pairs={{0,128},{128,256},{256,384},{384,0},{1,129},{129,257},{257,385},{3... | collective-permute-start | bytes 393224 | tf_op jit(solution)/shard_map/ppermute | solution.py:264
  33.4 5.0 %collective-permute-start.17 = (f32[2,2,64,128]{3,2,1,0:T(8,128)S(1)}, f32[2,2,64,128]{3,2,1,0:T(8,128)S(1)}, u32[]{:S(2)}, u32[]{:S(2)}) collective-permute-start(f32[2,2,64,128]{3,2,1,0:T(8,128)S(1)} %get-tuple-element.52), channel_id=1, source_target_pairs={{0,256},{128,384},{256,0},{384,128},{1,257},{129,385},{257,1},{385... | collective-permute-start | bytes 393224 | tf_op jit(solution)/shard_map/ppermute | solution.py:264
  38.4 2.1 %collective-permute-start.18 = (f32[2,2,64,128]{3,2,1,0:T(8,128)S(1)}, f32[2,2,64,128]{3,2,1,0:T(8,128)S(1)}, u32[]{:S(2)}, u32[]{:S(2)}) collective-permute-start(f32[2,2,64,128]{3,2,1,0:T(8,128)S(1)} %get-tuple-element.53), channel_id=1, source_target_pairs={{0,384},{128,0},{256,128},{384,256},{1,385},{129,1},{257,129},{385... | collective-permute-start | bytes 393224 | tf_op jit(solution)/shard_map/ppermute | solution.py:264
  40.6 5.7 %collective-permute-done.17.products_and_out_2_ = f32[2,2,64,128]{3,2,1,0:T(8,128)S(1)} collective-permute-done((f32[2,2,64,128]{3,2,1,0:T(8,128)S(1)}, f32[2,2,64,128]{3,2,1,0:T(8,128)S(1)}, u32[]{:S(2)}, u32[]{:S(2)}) %collective-permute-start.17) | collective-permute-done | bytes 131104 | tf_op jit(solution)/shard_map/ppermute | solution.py:264
  46.3 1.6 %collective-permute-done.18.products_and_out_3_ = f32[2,2,64,128]{3,2,1,0:T(8,128)S(1)} collective-permute-done((f32[2,2,64,128]{3,2,1,0:T(8,128)S(1)}, f32[2,2,64,128]{3,2,1,0:T(8,128)S(1)}, u32[]{:S(2)}, u32[]{:S(2)}) %collective-permute-start.18) | collective-permute-done | bytes 131104 | tf_op jit(solution)/shard_map/ppermute | solution.py:264
  47.9 2.4 %shard_map.111 = f32[1024,128]{1,0:T(8,128)} custom-call(s32[5]{0:T(128)S(1)} %stack.23.position, s32[16,2]{1,0:T(8,128)S(1)} %copy.16.kq, f32[4,2,64,128]{3,2,1,0:T(8,128)S(1)} %get-tuple-element.60.kept, f32[4,2,64,128]{3,2,1,0:T(8,128)S(1)} %collective-permute-done.15.swapped, f32[2,2,64,128]{3,2,1,0:T(8,128)S(1)} %get-tuple-element.50.products_and_out_0_, ...), custom_call_target="tpu_custom_call" | custom-call | flops 134217728 | bytes 1048576 | tf_op jit(solution)/shard_map/pallas_call | solution.py:297
  50.3 8.2 %all-to-all-start.1 = ((f32[32,32,128]{2,1,0:T(8,128)}), f32[32,32,128]{2,1,0:T(8,128)S(1)}, u32[]{:S(2)}, u32[]{:S(2)}) async-start(f32[32,32,128]{2,1,0:T(8,128)} %bitcast.8), calls=%async_computation.1 | async-start | bytes 1048576 | tf_op jit(solution)/shard_map/all_to_all | solution.py:300
  58.6 0.2 reshape.20
  59.0 0.5 copy-done.7
  59.5 2.1 %shard_map.109 = (bf16[512,256]{1,0:T(8,128)(2,1)S(1)}, bf16[512,256]{1,0:T(8,128)(2,1)S(1)}) custom-call(s32[5]{0:T(128)S(1)} %stack.23.position, s32[8,256]{1,0:T(8,128)S(1)} %pad.4.coords, f32[3,2,32,256]{3,2,1,0:T(8,128)S(1)} %copy-done.7), custom_call_target="tpu_custom_call" | custom-call | flops 268435456 | bytes 1048576 | tf_op jit(solution)/shard_map/pallas_call | solution.py:304
  61.6 8.4 %all-to-all-done.1.columns = f32[32,32,128]{2,1,0:T(8,128)S(1)} async-done(((f32[32,32,128]{2,1,0:T(8,128)}), f32[32,32,128]{2,1,0:T(8,128)S(1)}, u32[]{:S(2)}, u32[]{:S(2)}) %all-to-all-start.1) | async-done | bytes 524320 | tf_op jit(solution)/shard_map/all_to_all | solution.py:300
  70.0 2.3 %shard_map.112 = f32[1024,128]{1,0:T(8,128)} custom-call(bf16[512,256]{1,0:T(8,128)(2,1)S(1)} %get-tuple-element.48.high, bf16[512,256]{1,0:T(8,128)(2,1)S(1)} %get-tuple-element.49.low, f32[32,32,128]{2,1,0:T(8,128)S(1)} %all-to-all-done.1.columns), custom_call_target="tpu_custom_call" | custom-call | flops 268435456 | bytes 1048576 | tf_op jit(solution)/shard_map/pallas_call | solution.py:311
  72.3 4.1 %all-to-all-start.2 = ((f32[32,32,128]{2,1,0:T(8,128)}), f32[32,32,128]{2,1,0:T(8,128)S(1)}, u32[]{:S(2)}, u32[]{:S(2)}) async-start(f32[32,32,128]{2,1,0:T(8,128)} %bitcast.9), calls=%async_computation.2 | async-start | bytes 1048576 | tf_op jit(solution)/shard_map/all_to_all | solution.py:319
  76.5 0.6 shard_map.113
  77.1 3.1 %collective-permute-start.19 = (f32[264,128]{1,0:T(8,128)S(1)}, f32[264,128]{1,0:T(8,128)S(1)}, u32[]{:S(2)}, u32[]{:S(2)}) collective-permute-start(f32[264,128]{1,0:T(8,128)S(1)} %get-tuple-element.55), channel_id=1, source_target_pairs={{0,128},{128,256},{256,384},{384,0},{1,129},{129,257},{257,385},{3... | collective-permute-start | bytes 405512 | tf_op jit(solution)/shard_map/ppermute | solution.py:264
  80.2 3.3 %collective-permute-start.20 = (f32[264,128]{1,0:T(8,128)S(1)}, f32[264,128]{1,0:T(8,128)S(1)}, u32[]{:S(2)}, u32[]{:S(2)}) collective-permute-start(f32[264,128]{1,0:T(8,128)S(1)} %get-tuple-element.56), channel_id=1, source_target_pairs={{0,256},{128,384},{256,0},{384,128},{1,257},{129,385},{257,1},{385... | collective-permute-start | bytes 405512 | tf_op jit(solution)/shard_map/ppermute | solution.py:264
  83.5 2.6 %collective-permute-start.21 = (f32[264,128]{1,0:T(8,128)S(1)}, f32[264,128]{1,0:T(8,128)S(1)}, u32[]{:S(2)}, u32[]{:S(2)}) collective-permute-start(f32[264,128]{1,0:T(8,128)S(1)} %get-tuple-element.57), channel_id=1, source_target_pairs={{0,384},{128,0},{256,128},{384,256},{1,385},{129,1},{257,129},{385... | collective-permute-start | bytes 405512 | tf_op jit(solution)/shard_map/ppermute | solution.py:264
  86.3 5.9 %collective-permute-done.20.packs_and_out_2_ = f32[264,128]{1,0:T(8,128)S(1)} collective-permute-done((f32[264,128]{1,0:T(8,128)S(1)}, f32[264,128]{1,0:T(8,128)S(1)}, u32[]{:S(2)}, u32[]{:S(2)}) %collective-permute-start.20) | collective-permute-done | bytes 135200 | tf_op jit(solution)/shard_map/ppermute | solution.py:264
  92.1 0.6 collective-permute-done.21.packs_and_out_3_
  92.8 2.4 %shard_map.114 = f32[16,1,128]{2,1,0:T(1,128)S(1)} custom-call(s32[5]{0:T(128)S(1)} %stack.23.position, f32[4,2]{1,0:T(4,128)S(1)} %copy.17.frequency, f32[1024,128]{1,0:T(8,128)S(1)} %bitcast.11, f32[264,128]{1,0:T(8,128)S(1)} %get-tuple-element.54.packs_and_out_0_, f32[264,128]{1,0:T(8,128)S(1)} %collective-permute-done.19.packs_and_out_1_, ...), custom_call_target="tpu_custom_call" | custom-call | flops 134217728 | bytes 1048576 | tf_op jit(solution)/shard_map/pallas_call | solution.py:320
  95.2 22.2 %all_to_all.68.terms = f32[16,1,128]{2,1,0:T(1,128)S(1)} all-to-all(f32[16,1,128]{2,1,0:T(1,128)S(1)} %shard_map.114), channel_id=1, replica_groups=mesh['z'=4,'y'=4,'x'=4,'core'=2,'pb'=4] {'z','pb'}, dimensions={0} | all-to-all | bytes 16384 | tf_op jit(solution)/shard_map/all_to_all | solution.py:323
  117.4 0.6 shard_map.115
  (31 shorter events, 0.6 us)
Async XLA Ops:
  1.6 12.1 %all-to-all-start = ((f32[4,2,64,128]{3,2,1,0:T(8,128)}), f32[4,2,64,128]{3,2,1,0:T(8,128)S(1)}, u32[]{:S(2)}, u32[]{:S(2)}) async-start(f32[4,2,64,128]{3,2,1,0:T(8,128)} %broadcast_in_dim.2), calls=%async_computation | async-start | bytes 524288 | tf_op jit(solution)/shard_map/all_to_all | solution.py:282
  8.0 0.7 copy-start.9
  10.7 19.8 %copy-start = (f32[2,4,2,64,128]{4,3,2,1,0:T(8,128)S(1)}, f32[2,4,2,64,128]{4,3,2,1,0:T(8,128)}, u32[]{:S(2)}) copy-start(f32[2,4,2,64,128]{4,3,2,1,0:T(8,128)} %coupling.1) | copy-start | bytes 1572868
  13.6 16.9 %copy-start.2 = (f32[2,64,128]{2,1,0:T(8,128)S(1)}, f32[2,64,128]{2,1,0:T(8,128)}, u32[]{:S(2)}) copy-start(f32[2,64,128]{2,1,0:T(8,128)} %gauge.1) | copy-start | bytes 196612
  13.6 11.0 %collective-permute-start.1 = (f32[4,2,64,128]{3,2,1,0:T(8,128)S(1)}, f32[4,2,64,128]{3,2,1,0:T(8,128)S(1)}, u32[]{:S(2)}, u32[]{:S(2)}) collective-permute-start(f32[4,2,64,128]{3,2,1,0:T(8,128)S(1)} %param.2), channel_id=1, source_target_pairs={{16,0},{24,8},{32,16},{40,24},{48,32},{56,40},{0,48},{8,56},{80,64... | collective-permute-start | bytes 786440 | tf_op jit(solution)/shard_map/cond/branch_2_fun/ppermute | solution.py:88
  24.7 23.2 %collective-permute-start.15 = (f32[4,2,64,128]{3,2,1,0:T(8,128)S(1)}, f32[4,2,64,128]{3,2,1,0:T(8,128)S(1)}, u32[]{:S(2)}, u32[]{:S(2)}) collective-permute-start(f32[4,2,64,128]{3,2,1,0:T(8,128)S(1)} %get-tuple-element.60.kept), channel_id=1, source_target_pairs={{0,4},{4,0},{1,5},{5,1},{2,6},{6,2},{3,7},{7,3},{8,12},{12,8},{9,1... | collective-permute-start | bytes 786440 | tf_op jit(solution)/shard_map/ppermute | solution.py:296
  31.5 9.1 %collective-permute-start.16 = (f32[2,2,64,128]{3,2,1,0:T(8,128)S(1)}, f32[2,2,64,128]{3,2,1,0:T(8,128)S(1)}, u32[]{:S(2)}, u32[]{:S(2)}) collective-permute-start(f32[2,2,64,128]{3,2,1,0:T(8,128)S(1)} %get-tuple-element.51), channel_id=1, source_target_pairs={{0,128},{128,256},{256,384},{384,0},{1,129},{129,257},{257,385},{3... | collective-permute-start | bytes 393224 | tf_op jit(solution)/shard_map/ppermute | solution.py:264
  33.4 12.9 %collective-permute-start.17 = (f32[2,2,64,128]{3,2,1,0:T(8,128)S(1)}, f32[2,2,64,128]{3,2,1,0:T(8,128)S(1)}, u32[]{:S(2)}, u32[]{:S(2)}) collective-permute-start(f32[2,2,64,128]{3,2,1,0:T(8,128)S(1)} %get-tuple-element.52), channel_id=1, source_target_pairs={{0,256},{128,384},{256,0},{384,128},{1,257},{129,385},{257,1},{385... | collective-permute-start | bytes 393224 | tf_op jit(solution)/shard_map/ppermute | solution.py:264
  38.4 9.5 %collective-permute-start.18 = (f32[2,2,64,128]{3,2,1,0:T(8,128)S(1)}, f32[2,2,64,128]{3,2,1,0:T(8,128)S(1)}, u32[]{:S(2)}, u32[]{:S(2)}) collective-permute-start(f32[2,2,64,128]{3,2,1,0:T(8,128)S(1)} %get-tuple-element.53), channel_id=1, source_target_pairs={{0,384},{128,0},{256,128},{384,256},{1,385},{129,1},{257,129},{385... | collective-permute-start | bytes 393224 | tf_op jit(solution)/shard_map/ppermute | solution.py:264
  50.3 8.3 %copy-start.8 = (s32[3,256]{1,0:T(4,128)S(1)}, s32[3,256]{1,0:T(4,128)}, u32[]{:S(2)}) copy-start(s32[3,256]{1,0:T(4,128)} %param.30) | copy-start | bytes 9220
  50.3 19.7 %all-to-all-start.1 = ((f32[32,32,128]{2,1,0:T(8,128)}), f32[32,32,128]{2,1,0:T(8,128)S(1)}, u32[]{:S(2)}, u32[]{:S(2)}) async-start(f32[32,32,128]{2,1,0:T(8,128)} %bitcast.8), calls=%async_computation.1 | async-start | bytes 1048576 | tf_op jit(solution)/shard_map/all_to_all | solution.py:300
  58.6 0.9 copy-start.7
  72.3 4.1 %copy-start.1 = (f32[2,4,64,128]{3,2,1,0:T(8,128)S(1)}, f32[2,4,64,128]{3,2,1,0:T(8,128)}, u32[]{:S(2)}) copy-start(f32[2,4,64,128]{3,2,1,0:T(8,128)} %eig_left.1) | copy-start | bytes 786436
  72.3 4.1 %copy-start.3 = (f32[2,64,128]{2,1,0:T(8,128)S(1)}, f32[2,64,128]{2,1,0:T(8,128)}, u32[]{:S(2)}) copy-start(f32[2,64,128]{2,1,0:T(8,128)} %eig_right.1) | copy-start | bytes 196612
  72.3 4.1 %copy-start.4 = (f32[2,4,64]{2,1,0:T(4,128)S(1)}, f32[2,4,64]{2,1,0:T(4,128)}, u32[]{:S(2)}) copy-start(f32[2,4,64]{2,1,0:T(4,128)} %energy_kq.1) | copy-start | bytes 6148
  72.3 4.1 %copy-start.5 = (s32[2,4,64]{2,1,0:T(4,128)S(1)}, s32[2,4,64]{2,1,0:T(4,128)}, u32[]{:S(2)}) copy-start(s32[2,4,64]{2,1,0:T(4,128)} %occupied.1) | copy-start | bytes 6148
  72.3 4.1 %copy-start.6 = (f32[2,64]{1,0:T(2,128)S(1)}, f32[2,64]{1,0:T(2,128)}, u32[]{:S(2)}) copy-start(f32[2,64]{1,0:T(2,128)} %energy_k.1) | copy-start | bytes 1540
  72.3 20.4 %all-to-all-start.2 = ((f32[32,32,128]{2,1,0:T(8,128)}), f32[32,32,128]{2,1,0:T(8,128)S(1)}, u32[]{:S(2)}, u32[]{:S(2)}) async-start(f32[32,32,128]{2,1,0:T(8,128)} %bitcast.9), calls=%async_computation.2 | async-start | bytes 1048576 | tf_op jit(solution)/shard_map/all_to_all | solution.py:319
  77.1 9.2 %collective-permute-start.19 = (f32[264,128]{1,0:T(8,128)S(1)}, f32[264,128]{1,0:T(8,128)S(1)}, u32[]{:S(2)}, u32[]{:S(2)}) collective-permute-start(f32[264,128]{1,0:T(8,128)S(1)} %get-tuple-element.55), channel_id=1, source_target_pairs={{0,128},{128,256},{256,384},{384,0},{1,129},{129,257},{257,385},{3... | collective-permute-start | bytes 405512 | tf_op jit(solution)/shard_map/ppermute | solution.py:264
  80.2 5.9 %copy-start.10 = (f32[4,2]{0,1:T(2,128)S(1)}, f32[4,2]{0,1:T(2,128)}, u32[]{:S(2)}) copy-start(f32[4,2]{0,1:T(2,128)} %param.36) | copy-start | bytes 100
  80.2 11.9 %collective-permute-start.20 = (f32[264,128]{1,0:T(8,128)S(1)}, f32[264,128]{1,0:T(8,128)S(1)}, u32[]{:S(2)}, u32[]{:S(2)}) collective-permute-start(f32[264,128]{1,0:T(8,128)S(1)} %get-tuple-element.56), channel_id=1, source_target_pairs={{0,256},{128,384},{256,0},{384,128},{1,257},{129,385},{257,1},{385... | collective-permute-start | bytes 405512 | tf_op jit(solution)/shard_map/ppermute | solution.py:264
  83.5 9.2 %collective-permute-start.21 = (f32[264,128]{1,0:T(8,128)S(1)}, f32[264,128]{1,0:T(8,128)S(1)}, u32[]{:S(2)}, u32[]{:S(2)}) collective-permute-start(f32[264,128]{1,0:T(8,128)S(1)} %get-tuple-element.57), channel_id=1, source_target_pairs={{0,384},{128,0},{256,128},{384,256},{1,385},{129,1},{257,129},{385... | collective-permute-start | bytes 405512 | tf_op jit(solution)/shard_map/ppermute | solution.py:264

commit v4 on v3

--- a/solution.py
+++ b/solution.py
@@ -58,11 +58,11 @@
     ]
 
 
-def offsets_of(position, kq, qpoint):
+def offsets_of(position):
     along_z, along_y, along_x, core = (position[i] for i in range(4))
     first = 2 * along_z + (along_y >> 1)
     second = ((along_y & 1) << 2) + along_x
-    target = kq[(position[4] << 2) + qpoint, 0]
+    target = position[4]
     return (
         ((target >> 5) - first) & 7,
         ((target >> 2) - second) & 7,
@@ -88,12 +88,13 @@
     return lax.ppermute(value, ("y", "x"), pairs)
 
 
-def right_kernel(position, coupling, gauge, *outs):
+def right_kernel(coupling, gauge, out):
     for k in range(2):
         block = halves(right_block(gauge[k]))
-        for shift, out in enumerate(outs):
-            rows = coupling[k, (position[0] + shift) & 3].reshape(-1, LANES)
-            out[k] = product(halves(rows), block, PLAIN).reshape(2, W, LANES)
+        rows = coupling[k].reshape(-1, LANES)
+        result = product(halves(rows), block, PLAIN).reshape(4, 2, W, LANES)
+        for q in range(4):
+            out[q, k] = result[q]
 
 
 def pack_kernel(position, eig_left, eig_right, energy_k, energy_kq, occupied, *outs):
@@ -109,21 +110,20 @@
         out[2 * LANES + 4 :] = jnp.zeros((4, LANES), jnp.float32)
 
 
-def left_kernel(position, kq, kept, swapped, *products_and_out):
-    products, out = products_and_out[:4], products_and_out[4]
+def left_kernel(position, kept, swapped, products, out):
     core = position[3]
-    offsets = offsets_of(position, kq, position[0])
+    offsets = offsets_of(position)
     carry = ((position[1] >> 1) + offsets[0]) >> 1
     for l in range(2):
         third = (2 * core + l + offsets[2]) & 3
         mine = (third >> 1) == core
-        for shift in range(4):
-            plane = (position[0] - shift + 4 + carry) & 3
+        for z in range(4):
+            plane = (z + carry) & 3
             gauge = jnp.where(mine, kept[plane, third & 1], swapped[plane, third & 1])
-            pair = jnp.concatenate([products[shift][l, 0], products[shift][l, 1]], -1)
+            pair = jnp.concatenate([products[z, l, 0], products[z, l, 1]], -1)
             for b, wannier in enumerate(apply_left(gauge, pair)):
                 for part in range(2):
-                    start = (part * 2 + b) * 8 + shift * 2 + l
+                    start = (part * 2 + b) * 8 + z * 2 + l
                     out[pl.ds(start, 32, stride=32), :] = wannier[part * 32 : part * 32 + 32]
 
 
@@ -133,8 +133,6 @@
     for axis in range(3):
         divisions = lax.broadcasted_iota(jnp.int32, (FG, NK), 0)
         steps = turned[axis : axis + 1, :]
-        if axis == 0:
-            steps = (steps + (FG - 8 * position[0])) & (FG - 1)
         onehot = (divisions == steps).astype(jnp.float32)
         factor = [
             lax.dot_general(
@@ -231,7 +229,7 @@
     column = np.arange(NK)
     source, z, l = column // 8, column // 2 % 4, column % 2
     y, x, core = source // 8, source // 2 % 4, source % 2
-    coordinates = (2 * -z + y // 2, (y % 2) * 4 + x, 2 * core + l)
+    coordinates = (2 * z + y // 2, (y % 2) * 4 + x, 2 * core + l)
     tables = np.zeros((3, 2, FG, NK), np.float64)
     for axis, (size, where) in enumerate(zip((8, 8, 4), coordinates)):
         steps = np.arange(FG)[:, None] - (FG // size) * where[None, :]
@@ -257,7 +255,11 @@
     return jax.ShapeDtypeStruct(shape, jnp.float32)
 
 
-def spread(values):
+def spread(value):
+    return lax.all_to_all(value, "z", 0, 0, tiled=True)
+
+
+def shifted(values):
     arrived = [values[0]]
     for shift in (1, 2, 3):
         pairs = [(z, (z + shift) % 4) for z in range(4)]
@@ -277,28 +279,26 @@
     occupied,
     frequency,
 ):
-    along_z, along_y, along_x, _, pb = (lax.axis_index(name) for name in (*KA, "pb"))
-    position = jnp.stack([lax.axis_index(name) for name in (*KA, "pb")])
-    planes = lax.all_to_all(jnp.broadcast_to(gauge[None], (4, 2, W, LANES)), "z", 0, 0, tiled=True)
-    products = call(right_kernel, [f32(2, 2, W, LANES)] * 4, [SMEM, VMEM, VMEM], 1 << 27)(
-        position, coupling, gauge
-    )
+    along_z, along_y, along_x, core = (lax.axis_index(name) for name in KA)
+    target = kq_index[lax.axis_index("pb") * 4 + along_z, 0]
+    position = jnp.stack([along_z, along_y, along_x, core, target])
+    planes = spread(jnp.broadcast_to(gauge[None], (4, 2, W, LANES)))
+    products = call(right_kernel, f32(4, 2, 2, W, LANES), [VMEM, VMEM], 1 << 27)(coupling, gauge)
     products = spread(products)
     packs = call(pack_kernel, [f32(264, LANES)] * 4, [SMEM] + [VMEM] * 5, 1 << 20)(
         position, eig_left, eig_right, energy_k, energy_kq, occupied
     )
-    target = kq_index[pb * 4 + along_z, 0]
     number = (((target >> 2) - (along_y * 4 + along_x)) & 7) + (
         (((target >> 5) - (along_y >> 1)) & 1) << 3
     )
     branches = [functools.partial(translated, number=number) for number in range(16)]
     kept = lax.switch(number, branches, planes)
     swapped = lax.ppermute(kept, "core", [(0, 1), (1, 0)])
-    pieces = call(left_kernel, f32(1024, LANES), [SMEM, SMEM] + [VMEM] * 6, 1 << 27)(
-        position, kq_index, kept, swapped, *products
+    pieces = call(left_kernel, f32(1024, LANES), [SMEM] + [VMEM] * 3, 1 << 27)(
+        position, kept, swapped, products
     )
     columns = lax.all_to_all(pieces.reshape(32, 32, LANES), ("y", "x", "core"), 0, 0, tiled=True)
-    packs = spread(packs)
+    packs = shifted(packs)
     coords = fine_coords.reshape(3, 4, 32, 2).transpose(0, 1, 3, 2).reshape(3, NK)
     coords = jnp.pad(coords, ((0, 5), (0, 0)))
     high, low = call(
@@ -316,7 +316,9 @@
         grid=(2,),
         out_specs=pl.BlockSpec((1024, LANES), lambda i: (0, 0)),
     )(high, low, columns)
-    blocks = lax.all_to_all(fine.reshape(32, 32, LANES), ("y", "x", "core"), 0, 0, tiled=True)
+    blocks = lax.all_to_all(
+        fine.reshape(32, 32, LANES), ("y", "x", "core"), 0, 0, tiled=True
+    )
     terms = call(bloch_kernel, f32(16, 1, LANES), [SMEM, SMEM] + [VMEM] * 5, 1 << 27)(
         position, frequency, blocks.reshape(1024, LANES), *packs
     )

time: 120 us -> 112 us (0.933)
  starting transfers between devices: 50.2 us -> 45.2 us
  waiting for transfers between devices: 28.3 us -> 24.3 us
    ppermute x6 -> x3, starting transfers between devices: 18 us -> 9.94 us  [shifted(): arrived.append(lax.ppermute(values[shift], 'z', pairs))]
    ppermute x6 -> x3, waiting for transfers between devices: 13.8 us -> 7.7 us  [shifted(): arrived.append(lax.ppermute(values[shift], 'z', pairs))]
    all_to_all x1 -> x2, starting transfers between devices: 6.43 us -> 10 us  [spread(): return lax.all_to_all(value, 'z', 0, 0, tiled=True)]
    all_to_all x1 -> x2, waiting for transfers between devices: 2.87 us -> 4.39 us  [spread(): return lax.all_to_all(value, 'z', 0, 0, tiled=True)]
  transfers between devices with their start and end apart: 11 -> 9, of which waited for: 7 -> 6; matrix products, arithmetic and copies ran while one was open for 1% -> 2% of each run, Pallas kernels for 3% -> 4%
where the time goes in v4:
time: 112 us; the launch traced here: 110 us
  starting transfers between devices  45.2 us (40%)
  waiting for transfers between devices  24.3 us (22%)
  blocking collectives  22.3 us (20%)
  Pallas kernels  11.7 us (10%)
  local copies, waits for them, and re-layouts  4.01 us (4%)
  between operations  1.48 us (1%)
    all_to_all x1, blocking collectives, shards(): terms = lax.all_to_all(terms, ('z', 'pb'), 0, 0, tiled=True)  22.3 us
    all_to_all x2, starting transfers between devices, spread(): return lax.all_to_all(value, 'z', 0, 0, tiled=True)  10 us
    ppermute x3, starting transfers between devices, shifted(): arrived.append(lax.ppermute(values[shift], 'z', pairs))  9.94 us
    all_to_all x1, waiting for transfers between devices, shards(): lax.all_to_all(pieces.reshape(32, 32, LANES), ('y', 'x', 'core'), 0, 0, t...  8.38 us
    all_to_all x1, starting transfers between devices, shards(): lax.all_to_all(pieces.reshape(32, 32, LANES), ('y', 'x', 'core'), 0, 0, t...  7.84 us
    ppermute x3, waiting for transfers between devices, shifted(): arrived.append(lax.ppermute(values[shift], 'z', pairs))  7.7 us
    ppermute x1, starting transfers between devices, translated(): return lax.ppermute(value, ('y', 'x'), pairs)  7.6 us
    ppermute x1, starting transfers between devices, shards(): swapped = lax.ppermute(kept, 'core', [(0, 1), (1, 0)])  5.7 us
  transfers between devices with their start and end apart: 9, of which 6 were waited for; matrix products, arithmetic and copies ran while one was open for 2% of the time, Pallas kernels for 4%

profile of v4, /device:TPU:1, one launch (start us, length us, event | category | flops | bytes accessed | tf_op | source)
XLA Modules:
  0.0 109.6 jit_solution(3045459685801679231)
XLA Ops:
  0.0 1.6 %broadcast_in_dim.2 = f32[4,2,64,128]{3,2,1,0:T(8,128)} broadcast(f32[2,64,128]{2,1,0:T(8,128)} %gauge.1), dimensions={1,2,3} | broadcast | bytes 327680 | tf_op jit(solution)/shard_map/broadcast_in_dim | solution.py:285
  1.6 6.6 %all-to-all-start = ((f32[4,2,64,128]{3,2,1,0:T(8,128)}), f32[4,2,64,128]{3,2,1,0:T(8,128)S(1)}, u32[]{:S(2)}, u32[]{:S(2)}) async-start(f32[4,2,64,128]{3,2,1,0:T(8,128)} %broadcast_in_dim.2), calls=%async_computation | async-start | bytes 524288 | tf_op jit(solution)/shard_map/all_to_all | solution.py:259
  8.2 1.2 %shard_map.110 = f32[4,2,2,64,128]{4,3,2,1,0:T(8,128)} custom-call(f32[2,4,2,64,128]{4,3,2,1,0:T(8,128)S(1)} %copy-done, f32[2,64,128]{2,1,0:T(8,128)S(1)} %copy-done.1), custom_call_target="tpu_custom_call" | custom-call | flops 134217728 | bytes 1048576 | tf_op jit(solution)/shard_map/pallas_call | solution.py:286
  9.4 4.4 %all-to-all-done = f32[4,2,64,128]{3,2,1,0:T(8,128)S(1)} async-done(((f32[4,2,64,128]{3,2,1,0:T(8,128)}), f32[4,2,64,128]{3,2,1,0:T(8,128)S(1)}, u32[]{:S(2)}, u32[]{:S(2)}) %all-to-all-start) | async-done | bytes 262176 | tf_op jit(solution)/shard_map/all_to_all | solution.py:259
  13.8 3.5 %all-to-all-start.1 = ((f32[4,2,2,64,128]{4,3,2,1,0:T(8,128)}), f32[4,2,2,64,128]{4,3,2,1,0:T(8,128)S(1)}, u32[]{:S(2)}, u32[]{:S(2)}) async-start(f32[4,2,2,64,128]{4,3,2,1,0:T(8,128)} %shard_map.110), calls=%async_computation.1 | async-start | bytes 1048576 | tf_op jit(solution)/shard_map/all_to_all | solution.py:259
  17.3 0.7 copy-done.10
  18.0 0.7 fusion
  19.9 11.0 %conditional.1 = (f32[4,2,64,128]{3,2,1,0:T(8,128)S(1)}) conditional(s32[]{:T(128)} %clamp.3, f32[4,2,64,128]{3,2,1,0:T(8,128)S(1)} %all-to-all-done, f32[4,2,64,128]{3,2,1,0:T(8,128)S(1)} %all-to-all-done, f32[4,2,64,128]{3,2,1,0:T(8,128)S(1)} %all-to-all-done, f32[4,2,64,128]{3,2,1,0:T(8,128)S(1)} %all-to-all-done, ...), branch_computations={%region_0.0_spmd, %region_1.0_spmd, %region_2.0_spmd, %region_3.0_... | conditional | bytes 1572912 | solution.py:295
  20.0 7.6 %collective-permute-start.1 = (f32[4,2,64,128]{3,2,1,0:T(8,128)S(1)}, f32[4,2,64,128]{3,2,1,0:T(8,128)S(1)}, u32[]{:S(2)}, u32[]{:S(2)}) collective-permute-start(f32[4,2,64,128]{3,2,1,0:T(8,128)S(1)} %param.2), channel_id=1, source_target_pairs={{16,0},{24,8},{32,16},{40,24},{48,32},{56,40},{0,48},{8,56},{80,64... | collective-permute-start | bytes 786440 | tf_op jit(solution)/shard_map/cond/branch_2_fun/ppermute | solution.py:88
  27.6 3.3 %collective-permute-done.1 = f32[4,2,64,128]{3,2,1,0:T(8,128)S(1)} collective-permute-done((f32[4,2,64,128]{3,2,1,0:T(8,128)S(1)}, f32[4,2,64,128]{3,2,1,0:T(8,128)S(1)}, u32[]{:S(2)}, u32[]{:S(2)}) %collective-permute-start.1) | collective-permute-done | bytes 262176 | tf_op jit(solution)/shard_map/cond/branch_2_fun/ppermute | solution.py:88
  30.9 5.7 %collective-permute-start.15 = (f32[4,2,64,128]{3,2,1,0:T(8,128)S(1)}, f32[4,2,64,128]{3,2,1,0:T(8,128)S(1)}, u32[]{:S(2)}, u32[]{:S(2)}) collective-permute-start(f32[4,2,64,128]{3,2,1,0:T(8,128)S(1)} %get-tuple-element.52.kept), channel_id=1, source_target_pairs={{0,4},{4,0},{1,5},{5,1},{2,6},{6,2},{3,7},{7,3},{8,12},{12,8},{9,1... | collective-permute-start | bytes 786440 | tf_op jit(solution)/shard_map/ppermute | solution.py:296
  36.6 0.6 stack.19.position
  37.3 0.5 collective-permute-done.15.swapped
  37.8 2.3 %shard_map.111 = f32[1024,128]{1,0:T(8,128)} custom-call(s32[5]{0:T(128)S(1)} %stack.19.position, f32[4,2,64,128]{3,2,1,0:T(8,128)S(1)} %get-tuple-element.52.kept, f32[4,2,64,128]{3,2,1,0:T(8,128)S(1)} %collective-permute-done.15.swapped, f32[4,2,2,64,128]{4,3,2,1,0:T(8,128)S(1)} %all-to-all-done.1.products), custom_call_target="tpu_custom_call" | custom-call | flops 134217728 | bytes 1048576 | tf_op jit(solution)/shard_map/pallas_call | solution.py:297
  40.1 7.8 %all-to-all-start.2 = ((f32[32,32,128]{2,1,0:T(8,128)}), f32[32,32,128]{2,1,0:T(8,128)S(1)}, u32[]{:S(2)}, u32[]{:S(2)}) async-start(f32[32,32,128]{2,1,0:T(8,128)} %bitcast.8), calls=%async_computation.2 | async-start | bytes 1048576 | tf_op jit(solution)/shard_map/all_to_all | solution.py:300
  48.0 0.2 reshape.20
  48.1 0.1 copy.14
  48.3 0.1 reshape.21
  48.4 0.5 copy-done.7
  48.9 2.1 %shard_map.109 = (bf16[512,256]{1,0:T(8,128)(2,1)S(1)}, bf16[512,256]{1,0:T(8,128)(2,1)S(1)}) custom-call(s32[5]{0:T(128)S(1)} %stack.19.position, s32[8,256]{1,0:T(8,128)S(1)} %pad.4.coords, f32[3,2,32,256]{3,2,1,0:T(8,128)S(1)} %copy-done.7), custom_call_target="tpu_custom_call" | custom-call | flops 268435456 | bytes 1048576 | tf_op jit(solution)/shard_map/pallas_call | solution.py:304
  51.0 8.4 %all-to-all-done.2.columns = f32[32,32,128]{2,1,0:T(8,128)S(1)} async-done(((f32[32,32,128]{2,1,0:T(8,128)}), f32[32,32,128]{2,1,0:T(8,128)S(1)}, u32[]{:S(2)}, u32[]{:S(2)}) %all-to-all-start.2) | async-done | bytes 524320 | tf_op jit(solution)/shard_map/all_to_all | solution.py:300
  59.4 2.3 %shard_map.112 = f32[1024,128]{1,0:T(8,128)} custom-call(bf16[512,256]{1,0:T(8,128)(2,1)S(1)} %get-tuple-element.44.high, bf16[512,256]{1,0:T(8,128)(2,1)S(1)} %get-tuple-element.45.low, f32[32,32,128]{2,1,0:T(8,128)S(1)} %all-to-all-done.2.columns), custom_call_target="tpu_custom_call" | custom-call | flops 268435456 | bytes 1048576 | tf_op jit(solution)/shard_map/pallas_call | solution.py:311
  61.7 4.1 %all-to-all-start.3 = ((f32[32,32,128]{2,1,0:T(8,128)}), f32[32,32,128]{2,1,0:T(8,128)S(1)}, u32[]{:S(2)}, u32[]{:S(2)}) async-start(f32[32,32,128]{2,1,0:T(8,128)} %bitcast.9), calls=%async_computation.3 | async-start | bytes 1048576 | tf_op jit(solution)/shard_map/all_to_all | solution.py:319
  65.8 0.6 shard_map.113
  66.5 3.0 %collective-permute-start.16 = (f32[264,128]{1,0:T(8,128)S(1)}, f32[264,128]{1,0:T(8,128)S(1)}, u32[]{:S(2)}, u32[]{:S(2)}) collective-permute-start(f32[264,128]{1,0:T(8,128)S(1)} %get-tuple-element.47), channel_id=1, source_target_pairs={{0,128},{128,256},{256,384},{384,0},{1,129},{129,257},{257,385},{3... | collective-permute-start | bytes 405512 | tf_op jit(solution)/shard_map/ppermute | solution.py:266
  69.5 5.0 %collective-permute-start.17 = (f32[264,128]{1,0:T(8,128)S(1)}, f32[264,128]{1,0:T(8,128)S(1)}, u32[]{:S(2)}, u32[]{:S(2)}) collective-permute-start(f32[264,128]{1,0:T(8,128)S(1)} %get-tuple-element.48), channel_id=1, source_target_pairs={{0,256},{128,384},{256,0},{384,128},{1,257},{129,385},{257,1},{385... | collective-permute-start | bytes 405512 | tf_op jit(solution)/shard_map/ppermute | solution.py:266
  74.5 1.9 %collective-permute-start.18 = (f32[264,128]{1,0:T(8,128)S(1)}, f32[264,128]{1,0:T(8,128)S(1)}, u32[]{:S(2)}, u32[]{:S(2)}) collective-permute-start(f32[264,128]{1,0:T(8,128)S(1)} %get-tuple-element.49), channel_id=1, source_target_pairs={{0,384},{128,0},{256,128},{384,256},{1,385},{129,1},{257,129},{385... | collective-permute-start | bytes 405512 | tf_op jit(solution)/shard_map/ppermute | solution.py:266
  76.6 5.6 %collective-permute-done.17.packs_and_out_2_ = f32[264,128]{1,0:T(8,128)S(1)} collective-permute-done((f32[264,128]{1,0:T(8,128)S(1)}, f32[264,128]{1,0:T(8,128)S(1)}, u32[]{:S(2)}, u32[]{:S(2)}) %collective-permute-start.17) | collective-permute-done | bytes 135200 | tf_op jit(solution)/shard_map/ppermute | solution.py:266
  82.2 2.1 %collective-permute-done.18.packs_and_out_3_ = f32[264,128]{1,0:T(8,128)S(1)} collective-permute-done((f32[264,128]{1,0:T(8,128)S(1)}, f32[264,128]{1,0:T(8,128)S(1)}, u32[]{:S(2)}, u32[]{:S(2)}) %collective-permute-start.18) | collective-permute-done | bytes 135200 | tf_op jit(solution)/shard_map/ppermute | solution.py:266
  84.3 2.4 %shard_map.114 = f32[16,1,128]{2,1,0:T(1,128)S(1)} custom-call(s32[5]{0:T(128)S(1)} %stack.19.position, f32[4,2]{1,0:T(4,128)S(1)} %copy.15.frequency, f32[1024,128]{1,0:T(8,128)S(1)} %bitcast.11, f32[264,128]{1,0:T(8,128)S(1)} %get-tuple-element.46.packs_and_out_0_, f32[264,128]{1,0:T(8,128)S(1)} %collective-permute-done.16.packs_and_out_1_, ...), custom_call_target="tpu_custom_call" | custom-call | flops 134217728 | bytes 1048576 | tf_op jit(solution)/shard_map/pallas_call | solution.py:322
  86.7 22.3 %all_to_all.73.terms = f32[16,1,128]{2,1,0:T(1,128)S(1)} all-to-all(f32[16,1,128]{2,1,0:T(1,128)S(1)} %shard_map.114), channel_id=1, replica_groups=mesh['z'=4,'y'=4,'x'=4,'core'=2,'pb'=4] {'z','pb'}, dimensions={0} | all-to-all | bytes 16384 | tf_op jit(solution)/shard_map/all_to_all | solution.py:325
  109.0 0.6 shard_map.115
  (26 shorter events, 0.2 us)
Async XLA Ops:
  0.0 8.2 %copy-start = (f32[2,4,2,64,128]{4,3,2,1,0:T(8,128)S(1)}, f32[2,4,2,64,128]{4,3,2,1,0:T(8,128)}, u32[]{:S(2)}) copy-start(f32[2,4,2,64,128]{4,3,2,1,0:T(8,128)} %coupling.1) | copy-start | bytes 1572868
  1.6 6.6 %copy-start.1 = (f32[2,64,128]{2,1,0:T(8,128)S(1)}, f32[2,64,128]{2,1,0:T(8,128)}, u32[]{:S(2)}) copy-start(f32[2,64,128]{2,1,0:T(8,128)} %gauge.1) | copy-start | bytes 196612
  1.6 12.2 %all-to-all-start = ((f32[4,2,64,128]{3,2,1,0:T(8,128)}), f32[4,2,64,128]{3,2,1,0:T(8,128)S(1)}, u32[]{:S(2)}, u32[]{:S(2)}) async-start(f32[4,2,64,128]{3,2,1,0:T(8,128)} %broadcast_in_dim.2), calls=%async_computation | async-start | bytes 524288 | tf_op jit(solution)/shard_map/all_to_all | solution.py:259
  13.8 23.9 %all-to-all-start.1 = ((f32[4,2,2,64,128]{4,3,2,1,0:T(8,128)}), f32[4,2,2,64,128]{4,3,2,1,0:T(8,128)S(1)}, u32[]{:S(2)}, u32[]{:S(2)}) async-start(f32[4,2,2,64,128]{4,3,2,1,0:T(8,128)} %shard_map.110), calls=%async_computation.1 | async-start | bytes 1048576 | tf_op jit(solution)/shard_map/all_to_all | solution.py:259
  17.3 0.7 copy-start.10
  20.0 10.9 %collective-permute-start.1 = (f32[4,2,64,128]{3,2,1,0:T(8,128)S(1)}, f32[4,2,64,128]{3,2,1,0:T(8,128)S(1)}, u32[]{:S(2)}, u32[]{:S(2)}) collective-permute-start(f32[4,2,64,128]{3,2,1,0:T(8,128)S(1)} %param.2), channel_id=1, source_target_pairs={{16,0},{24,8},{32,16},{40,24},{48,32},{56,40},{0,48},{8,56},{80,64... | collective-permute-start | bytes 786440 | tf_op jit(solution)/shard_map/cond/branch_2_fun/ppermute | solution.py:88
  30.9 6.9 %collective-permute-start.15 = (f32[4,2,64,128]{3,2,1,0:T(8,128)S(1)}, f32[4,2,64,128]{3,2,1,0:T(8,128)S(1)}, u32[]{:S(2)}, u32[]{:S(2)}) collective-permute-start(f32[4,2,64,128]{3,2,1,0:T(8,128)S(1)} %get-tuple-element.52.kept), channel_id=1, source_target_pairs={{0,4},{4,0},{1,5},{5,1},{2,6},{6,2},{3,7},{7,3},{8,12},{12,8},{9,1... | collective-permute-start | bytes 786440 | tf_op jit(solution)/shard_map/ppermute | solution.py:296
  40.1 7.9 %copy-start.8 = (s32[3,256]{1,0:T(4,128)S(1)}, s32[3,256]{1,0:T(4,128)}, u32[]{:S(2)}) copy-start(s32[3,256]{1,0:T(4,128)} %param.30) | copy-start | bytes 9220
  40.1 19.3 %all-to-all-start.2 = ((f32[32,32,128]{2,1,0:T(8,128)}), f32[32,32,128]{2,1,0:T(8,128)S(1)}, u32[]{:S(2)}, u32[]{:S(2)}) async-start(f32[32,32,128]{2,1,0:T(8,128)} %bitcast.8), calls=%async_computation.2 | async-start | bytes 1048576 | tf_op jit(solution)/shard_map/all_to_all | solution.py:300
  47.9 0.9 copy-start.7
  61.7 4.1 %copy-start.2 = (f32[2,4,64,128]{3,2,1,0:T(8,128)S(1)}, f32[2,4,64,128]{3,2,1,0:T(8,128)}, u32[]{:S(2)}) copy-start(f32[2,4,64,128]{3,2,1,0:T(8,128)} %eig_left.1) | copy-start | bytes 786436
  61.7 4.1 %copy-start.3 = (f32[2,64,128]{2,1,0:T(8,128)S(1)}, f32[2,64,128]{2,1,0:T(8,128)}, u32[]{:S(2)}) copy-start(f32[2,64,128]{2,1,0:T(8,128)} %eig_right.1) | copy-start | bytes 196612
  61.7 4.1 %copy-start.4 = (f32[2,4,64]{2,1,0:T(4,128)S(1)}, f32[2,4,64]{2,1,0:T(4,128)}, u32[]{:S(2)}) copy-start(f32[2,4,64]{2,1,0:T(4,128)} %energy_kq.1) | copy-start | bytes 6148
  61.7 4.1 %copy-start.5 = (s32[2,4,64]{2,1,0:T(4,128)S(1)}, s32[2,4,64]{2,1,0:T(4,128)}, u32[]{:S(2)}) copy-start(s32[2,4,64]{2,1,0:T(4,128)} %occupied.1) | copy-start | bytes 6148
  61.7 4.1 %copy-start.6 = (f32[2,64]{1,0:T(2,128)S(1)}, f32[2,64]{1,0:T(2,128)}, u32[]{:S(2)}) copy-start(f32[2,64]{1,0:T(2,128)} %energy_k.1) | copy-start | bytes 1540
  61.7 22.6 %all-to-all-start.3 = ((f32[32,32,128]{2,1,0:T(8,128)}), f32[32,32,128]{2,1,0:T(8,128)S(1)}, u32[]{:S(2)}, u32[]{:S(2)}) async-start(f32[32,32,128]{2,1,0:T(8,128)} %bitcast.9), calls=%async_computation.3 | async-start | bytes 1048576 | tf_op jit(solution)/shard_map/all_to_all | solution.py:319
  66.5 10.1 %collective-permute-start.16 = (f32[264,128]{1,0:T(8,128)S(1)}, f32[264,128]{1,0:T(8,128)S(1)}, u32[]{:S(2)}, u32[]{:S(2)}) collective-permute-start(f32[264,128]{1,0:T(8,128)S(1)} %get-tuple-element.47), channel_id=1, source_target_pairs={{0,128},{128,256},{256,384},{384,0},{1,129},{129,257},{257,385},{3... | collective-permute-start | bytes 405512 | tf_op jit(solution)/shard_map/ppermute | solution.py:266
  69.5 7.0 %copy-start.9 = (f32[4,2]{0,1:T(2,128)S(1)}, f32[4,2]{0,1:T(2,128)}, u32[]{:S(2)}) copy-start(f32[4,2]{0,1:T(2,128)} %param.36) | copy-start | bytes 100
  69.5 12.7 %collective-permute-start.17 = (f32[264,128]{1,0:T(8,128)S(1)}, f32[264,128]{1,0:T(8,128)S(1)}, u32[]{:S(2)}, u32[]{:S(2)}) collective-permute-start(f32[264,128]{1,0:T(8,128)S(1)} %get-tuple-element.48), channel_id=1, source_target_pairs={{0,256},{128,384},{256,0},{384,128},{1,257},{129,385},{257,1},{385... | collective-permute-start | bytes 405512 | tf_op jit(solution)/shard_map/ppermute | solution.py:266
  74.5 9.7 %collective-permute-start.18 = (f32[264,128]{1,0:T(8,128)S(1)}, f32[264,128]{1,0:T(8,128)S(1)}, u32[]{:S(2)}, u32[]{:S(2)}) collective-permute-start(f32[264,128]{1,0:T(8,128)S(1)} %get-tuple-element.49), channel_id=1, source_target_pairs={{0,384},{128,0},{256,128},{384,256},{1,385},{129,1},{257,129},{385... | collective-permute-start | bytes 405512 | tf_op jit(solution)/shard_map/ppermute | solution.py:266

commit v5 on v4

--- a/solution.py
+++ b/solution.py
@@ -58,18 +58,6 @@
     ]
 
 
-def offsets_of(position):
-    along_z, along_y, along_x, core = (position[i] for i in range(4))
-    first = 2 * along_z + (along_y >> 1)
-    second = ((along_y & 1) << 2) + along_x
-    target = position[4]
-    return (
-        ((target >> 5) - first) & 7,
-        ((target >> 2) - second) & 7,
-        (target - 2 * core) & 3,
-    )
-
-
 def translation(number):
     along_second, along_first = number % 8, number // 8
     pairs = []
@@ -97,7 +85,7 @@
             out[q, k] = result[q]
 
 
-def pack_kernel(position, eig_left, eig_right, energy_k, energy_kq, occupied, *outs):
+def pack_kernel(position, _, eig_left, eig_right, energy_k, energy_kq, occupied, *outs):
     for shift, out in enumerate(outs):
         q = (position[0] + shift) & 3
         for f in range(2):
@@ -110,18 +98,23 @@
         out[2 * LANES + 4 :] = jnp.zeros((4, LANES), jnp.float32)
 
 
-def left_kernel(position, kept, swapped, products, out):
+def align_kernel(position, kq, own, other, out):
     core = position[3]
-    offsets = offsets_of(position)
-    carry = ((position[1] >> 1) + offsets[0]) >> 1
-    for l in range(2):
-        third = (2 * core + l + offsets[2]) & 3
-        mine = (third >> 1) == core
-        for z in range(4):
-            plane = (z + carry) & 3
-            gauge = jnp.where(mine, kept[plane, third & 1], swapped[plane, third & 1])
+    for q in range(4):
+        target = kq[(position[4] << 2) + q, 0]
+        for l in range(2):
+            third = (target + l) & 3
+            mine = (third >> 1) == core
+            out[q, l] = jnp.where(mine, own[third & 1], other[third & 1])
+
+
+def left_kernel(position, number, moved, products, out):
+    carry = ((position[1] >> 1) + number[1]) >> 1
+    for z in range(4):
+        plane = (z + carry) & 3
+        for l in range(2):
             pair = jnp.concatenate([products[z, l, 0], products[z, l, 1]], -1)
-            for b, wannier in enumerate(apply_left(gauge, pair)):
+            for b, wannier in enumerate(apply_left(moved[plane, l], pair)):
                 for part in range(2):
                     start = (part * 2 + b) * 8 + z * 2 + l
                     out[pl.ds(start, 32, stride=32), :] = wannier[part * 32 : part * 32 + 32]
@@ -216,7 +209,7 @@
         summed = jnp.sum(total, axis=0, keepdims=True) * (1.0 / 1024.0)
         plane = (position[0] - shift + 4) & 3
         for group in range(4):
-            out[plane * 4 + group] = summed
+            out[group * 4 + plane] = summed
 
 
 def sum_kernel(terms, out):
@@ -279,23 +272,27 @@
     occupied,
     frequency,
 ):
-    along_z, along_y, along_x, core = (lax.axis_index(name) for name in KA)
-    target = kq_index[lax.axis_index("pb") * 4 + along_z, 0]
-    position = jnp.stack([along_z, along_y, along_x, core, target])
-    planes = spread(jnp.broadcast_to(gauge[None], (4, 2, W, LANES)))
+    along_z, along_y, along_x, core, pb = (lax.axis_index(name) for name in (*KA, "pb"))
+    position = jnp.stack([along_z, along_y, along_x, core, pb])
+    other = lax.ppermute(gauge, "core", [(0, 1), (1, 0)])
+    aligned = call(align_kernel, f32(4, 2, W, LANES), [SMEM, SMEM, VMEM, VMEM], 1 << 20)(
+        position, kq_index, gauge, other
+    )
+    planes = spread(aligned)
     products = call(right_kernel, f32(4, 2, 2, W, LANES), [VMEM, VMEM], 1 << 27)(coupling, gauge)
     products = spread(products)
-    packs = call(pack_kernel, [f32(264, LANES)] * 4, [SMEM] + [VMEM] * 5, 1 << 20)(
-        position, eig_left, eig_right, energy_k, energy_kq, occupied
-    )
-    number = (((target >> 2) - (along_y * 4 + along_x)) & 7) + (
-        (((target >> 5) - (along_y >> 1)) & 1) << 3
-    )
+    target = kq_index[pb * 4 + along_z, 0]
+    along_first = ((target >> 5) - 2 * along_z - (along_y >> 1)) & 7
+    along_second = ((target >> 2) - (along_y * 4 + along_x)) & 7
+    number = along_second + ((along_first & 1) << 3)
     branches = [functools.partial(translated, number=number) for number in range(16)]
-    kept = lax.switch(number, branches, planes)
-    swapped = lax.ppermute(kept, "core", [(0, 1), (1, 0)])
-    pieces = call(left_kernel, f32(1024, LANES), [SMEM] + [VMEM] * 3, 1 << 27)(
-        position, kept, swapped, products
+    numbers = jnp.stack([number, along_first])
+    packs = call(pack_kernel, [f32(264, LANES)] * 4, [SMEM, SMEM] + [VMEM] * 5, 1 << 20)(
+        position, numbers, eig_left, eig_right, energy_k, energy_kq, occupied
+    )
+    moved = lax.switch(number, branches, planes)
+    pieces = call(left_kernel, f32(1024, LANES), [SMEM, SMEM] + [VMEM] * 2, 1 << 27)(
+        position, numbers, moved, products
     )
     columns = lax.all_to_all(pieces.reshape(32, 32, LANES), ("y", "x", "core"), 0, 0, tiled=True)
     packs = shifted(packs)
@@ -322,7 +319,7 @@
     terms = call(bloch_kernel, f32(16, 1, LANES), [SMEM, SMEM] + [VMEM] * 5, 1 << 27)(
         position, frequency, blocks.reshape(1024, LANES), *packs
     )
-    terms = lax.all_to_all(terms, ("z", "pb"), 0, 0, tiled=True)
+    terms = lax.all_to_all(terms, ("pb", "z"), 0, 0, tiled=True)
     return call(sum_kernel, f32(2, W), [VMEM], 1 << 12)(terms)
 
 

time: 112 us -> 113 us (level)
  waiting for transfers between devices: 24.3 us -> 30.8 us
  starting transfers between devices: 45.2 us -> 38.9 us
  Pallas kernels: 11.7 us -> 13.1 us
    ppermute x1, starting transfers between devices: 7.6 us -> 2.55 us  [translated(): return lax.ppermute(value, ('y', 'x'), pairs)]
    all_to_all x2, waiting for transfers between devices: 4.39 us -> 8.38 us  [spread(): return lax.all_to_all(value, 'z', 0, 0, tiled=True)]
    ppermute x1, starting transfers between devices: 5.7 us -> 8.87 us  [shards(): other = lax.ppermute(gauge, 'core', [(0, 1), (1, 0)])]
    all_to_all x2, starting transfers between devices: 10 us -> 7.01 us  [spread(): return lax.all_to_all(value, 'z', 0, 0, tiled=True)]
    ppermute x1, waiting for transfers between devices: 3.29 us -> 6.06 us  [translated(): return lax.ppermute(value, ('y', 'x'), pairs)]
    broadcast_in_dim x1 -> x0, local copies, waits for them, and re-layouts: 1.62 us -> none  [shards(): planes = spread(jnp.broadcast_to(gauge[None], (4, 2, W, LANES)))]
    unnamed x23 -> x26, local copies, waits for them, and re-layouts: 1.31 us -> 2.9 us
    all_to_all x1, starting transfers between devices: 7.84 us -> 6.37 us  [shards(): lax.all_to_all(pieces.reshape(32, 32, LANES), ('y', 'x', 'core'), 0, 0, t...]
  transfers between devices with their start and end apart: 9 -> 9, of which waited for: 6 -> 7; matrix products, arithmetic and copies ran while one was open for 2% -> 2% of each run, Pallas kernels for 4% -> 4%
where the time goes in v5:
time: 113 us; the launch traced here: 111 us
  starting transfers between devices  38.9 us (34%)
  waiting for transfers between devices  30.8 us (27%)
  blocking collectives  22.3 us (20%)
  Pallas kernels  13.1 us (12%)
  local copies, waits for them, and re-layouts  3.42 us (3%)
  between operations  1.53 us (1%)
    all_to_all x1, blocking collectives, shards(): terms = lax.all_to_all(terms, ('pb', 'z'), 0, 0, tiled=True)  22.3 us
    ppermute x3, starting transfers between devices, shifted(): arrived.append(lax.ppermute(values[shift], 'z', pairs))  9.98 us
    ppermute x1, starting transfers between devices, shards(): other = lax.ppermute(gauge, 'core', [(0, 1), (1, 0)])  8.87 us
    all_to_all x1, waiting for transfers between devices, shards(): lax.all_to_all(pieces.reshape(32, 32, LANES), ('y', 'x', 'core'), 0, 0, t...  8.38 us
    all_to_all x2, waiting for transfers between devices, spread(): return lax.all_to_all(value, 'z', 0, 0, tiled=True)  8.38 us
    ppermute x3, waiting for transfers between devices, shifted(): arrived.append(lax.ppermute(values[shift], 'z', pairs))  7.7 us
    all_to_all x2, starting transfers between devices, spread(): return lax.all_to_all(value, 'z', 0, 0, tiled=True)  7.01 us
    all_to_all x1, starting transfers between devices, shards(): lax.all_to_all(pieces.reshape(32, 32, LANES), ('y', 'x', 'core'), 0, 0, t...  6.37 us
  transfers between devices with their start and end apart: 9, of which 7 were waited for; matrix products, arithmetic and copies ran while one was open for 2% of the time, Pallas kernels for 4%

profile of v5, /device:TPU:1, one launch (start us, length us, event | category | flops | bytes accessed | tf_op | source)
XLA Modules:
  0.0 110.7 jit_solution(13484322859987135731)
XLA Ops:
  0.0 8.9 %collective-permute-start.15 = (f32[2,64,128]{2,1,0:T(8,128)}, f32[2,64,128]{2,1,0:T(8,128)S(1)}, u32[]{:S(2)}, u32[]{:S(2)}) collective-permute-start(f32[2,64,128]{2,1,0:T(8,128)} %gauge.1), channel_id=1, source_target_pairs={{0,4},{4,0},{1,5},{5,1},{2,6},{6,2},{3,7},{7,3},{8,12},{12,8},{9,1... | collective-permute-start | bytes 196616 | tf_op jit(solution)/shard_map/ppermute | solution.py:277
  8.9 0.8 copy.16.kq
  9.7 0.2 collective-permute-done.15.other
  10.0 0.8 copy-done.1
  10.8 1.4 %shard_map.110 = f32[4,2,64,128]{3,2,1,0:T(8,128)} custom-call(s32[5]{0:T(128)S(1)} %stack.32.position, s32[16,2]{1,0:T(8,128)S(1)} %copy.16.kq, f32[2,64,128]{2,1,0:T(8,128)S(1)} %copy-done.1, f32[2,64,128]{2,1,0:T(8,128)S(1)} %collective-permute-done.15.other), custom_call_target="tpu_custom_call" | custom-call | flops 1048576 | bytes 1048576 | tf_op jit(solution)/shard_map/pallas_call | solution.py:278
  12.2 3.5 %all-to-all-start = ((f32[4,2,64,128]{3,2,1,0:T(8,128)}), f32[4,2,64,128]{3,2,1,0:T(8,128)S(1)}, u32[]{:S(2)}, u32[]{:S(2)}) async-start(f32[4,2,64,128]{3,2,1,0:T(8,128)} %shard_map.110), calls=%async_computation | async-start | bytes 524288 | tf_op jit(solution)/shard_map/all_to_all | solution.py:252
  15.8 1.2 %shard_map.111 = f32[4,2,2,64,128]{4,3,2,1,0:T(8,128)} custom-call(f32[2,4,2,64,128]{4,3,2,1,0:T(8,128)S(1)} %copy-done, f32[2,64,128]{2,1,0:T(8,128)S(1)} %copy-done.2), custom_call_target="tpu_custom_call" | custom-call | flops 134217728 | bytes 1048576 | tf_op jit(solution)/shard_map/pallas_call | solution.py:282
  17.0 6.1 %all-to-all-done = f32[4,2,64,128]{3,2,1,0:T(8,128)S(1)} async-done(((f32[4,2,64,128]{3,2,1,0:T(8,128)}), f32[4,2,64,128]{3,2,1,0:T(8,128)S(1)}, u32[]{:S(2)}, u32[]{:S(2)}) %all-to-all-start) | async-done | bytes 262176 | tf_op jit(solution)/shard_map/all_to_all | solution.py:252
  23.2 3.5 %all-to-all-start.1 = ((f32[4,2,2,64,128]{4,3,2,1,0:T(8,128)}), f32[4,2,2,64,128]{4,3,2,1,0:T(8,128)S(1)}, u32[]{:S(2)}, u32[]{:S(2)}) async-start(f32[4,2,2,64,128]{4,3,2,1,0:T(8,128)} %shard_map.111), calls=%async_computation.1 | async-start | bytes 1048576 | tf_op jit(solution)/shard_map/all_to_all | solution.py:252
  26.7 0.7 copy-done.10
  27.3 0.6 fusion
  29.3 8.6 %conditional.1 = (f32[4,2,64,128]{3,2,1,0:T(8,128)S(1)}) conditional(s32[]{:T(128)} %clamp.3, f32[4,2,64,128]{3,2,1,0:T(8,128)S(1)} %all-to-all-done, f32[4,2,64,128]{3,2,1,0:T(8,128)S(1)} %all-to-all-done, f32[4,2,64,128]{3,2,1,0:T(8,128)S(1)} %all-to-all-done, f32[4,2,64,128]{3,2,1,0:T(8,128)S(1)} %all-to-all-done, ...), branch_computations={%region_0.0_spmd, %region_1.0_spmd, %region_2.0_spmd, %region_3.0_... | conditional | bytes 1572912 | solution.py:293
  29.3 2.5 %collective-permute-start.1 = (f32[4,2,64,128]{3,2,1,0:T(8,128)S(1)}, f32[4,2,64,128]{3,2,1,0:T(8,128)S(1)}, u32[]{:S(2)}, u32[]{:S(2)}) collective-permute-start(f32[4,2,64,128]{3,2,1,0:T(8,128)S(1)} %param.2), channel_id=1, source_target_pairs={{16,0},{24,8},{32,16},{40,24},{48,32},{56,40},{0,48},{8,56},{80,64... | collective-permute-start | bytes 786440 | tf_op jit(solution)/shard_map/cond/branch_2_fun/ppermute | solution.py:76
  31.9 6.1 %collective-permute-done.1 = f32[4,2,64,128]{3,2,1,0:T(8,128)S(1)} collective-permute-done((f32[4,2,64,128]{3,2,1,0:T(8,128)S(1)}, f32[4,2,64,128]{3,2,1,0:T(8,128)S(1)}, u32[]{:S(2)}, u32[]{:S(2)}) %collective-permute-start.1) | collective-permute-done | bytes 262176 | tf_op jit(solution)/shard_map/cond/branch_2_fun/ppermute | solution.py:76
  38.0 2.3 %all-to-all-done.1.products = f32[4,2,2,64,128]{4,3,2,1,0:T(8,128)S(1)} async-done(((f32[4,2,2,64,128]{4,3,2,1,0:T(8,128)}), f32[4,2,2,64,128]{4,3,2,1,0:T(8,128)S(1)}, u32[]{:S(2)}, u32[]{:S(2)}) %all-to-all-start.1) | async-done | bytes 524320 | tf_op jit(solution)/shard_map/all_to_all | solution.py:252
  40.2 2.3 %shard_map.112 = f32[1024,128]{1,0:T(8,128)} custom-call(s32[5]{0:T(128)S(1)} %stack.32.position, s32[2]{0:T(128)S(1)} %pad_add_fusion.number._, f32[4,2,64,128]{3,2,1,0:T(8,128)S(1)} %get-tuple-element.52.moved, f32[4,2,2,64,128]{4,3,2,1,0:T(8,128)S(1)} %all-to-all-done.1.products), custom_call_target="tpu_custom_call" | custom-call | flops 134217728 | bytes 1048576 | tf_op jit(solution)/shard_map/pallas_call | solution.py:294
  42.5 6.4 %all-to-all-start.2 = ((f32[32,32,128]{2,1,0:T(8,128)}), f32[32,32,128]{2,1,0:T(8,128)S(1)}, u32[]{:S(2)}, u32[]{:S(2)}) async-start(f32[32,32,128]{2,1,0:T(8,128)} %bitcast.10), calls=%async_computation.2 | async-start | bytes 1048576 | tf_op jit(solution)/shard_map/all_to_all | solution.py:297
  48.9 0.2 reshape.19
  49.4 0.5 copy-done.8
  49.9 2.1 %shard_map.109 = (bf16[512,256]{1,0:T(8,128)(2,1)S(1)}, bf16[512,256]{1,0:T(8,128)(2,1)S(1)}) custom-call(s32[5]{0:T(128)S(1)} %stack.32.position, s32[8,256]{1,0:T(8,128)S(1)} %pad.4.coords, f32[3,2,32,256]{3,2,1,0:T(8,128)S(1)} %copy-done.8), custom_call_target="tpu_custom_call" | custom-call | flops 268435456 | bytes 1048576 | tf_op jit(solution)/shard_map/pallas_call | solution.py:301
  52.0 8.4 %all-to-all-done.2.columns = f32[32,32,128]{2,1,0:T(8,128)S(1)} async-done(((f32[32,32,128]{2,1,0:T(8,128)}), f32[32,32,128]{2,1,0:T(8,128)S(1)}, u32[]{:S(2)}, u32[]{:S(2)}) %all-to-all-start.2) | async-done | bytes 524320 | tf_op jit(solution)/shard_map/all_to_all | solution.py:297
  60.4 2.3 %shard_map.113 = f32[1024,128]{1,0:T(8,128)} custom-call(bf16[512,256]{1,0:T(8,128)(2,1)S(1)} %get-tuple-element.44.high, bf16[512,256]{1,0:T(8,128)(2,1)S(1)} %get-tuple-element.45.low, f32[32,32,128]{2,1,0:T(8,128)S(1)} %all-to-all-done.2.columns), custom_call_target="tpu_custom_call" | custom-call | flops 268435456 | bytes 1048576 | tf_op jit(solution)/shard_map/pallas_call | solution.py:308
  62.7 4.1 %all-to-all-start.3 = ((f32[32,32,128]{2,1,0:T(8,128)}), f32[32,32,128]{2,1,0:T(8,128)S(1)}, u32[]{:S(2)}, u32[]{:S(2)}) async-start(f32[32,32,128]{2,1,0:T(8,128)} %bitcast.11), calls=%async_computation.3 | async-start | bytes 1048576 | tf_op jit(solution)/shard_map/all_to_all | solution.py:316
  66.8 0.6 shard_map.114
  67.5 3.0 %collective-permute-start.16 = (f32[264,128]{1,0:T(8,128)S(1)}, f32[264,128]{1,0:T(8,128)S(1)}, u32[]{:S(2)}, u32[]{:S(2)}) collective-permute-start(f32[264,128]{1,0:T(8,128)S(1)} %get-tuple-element.47), channel_id=1, source_target_pairs={{0,128},{128,256},{256,384},{384,0},{1,129},{129,257},{257,385},{3... | collective-permute-start | bytes 405512 | tf_op jit(solution)/shard_map/ppermute | solution.py:259
  70.5 5.0 %collective-permute-start.17 = (f32[264,128]{1,0:T(8,128)S(1)}, f32[264,128]{1,0:T(8,128)S(1)}, u32[]{:S(2)}, u32[]{:S(2)}) collective-permute-start(f32[264,128]{1,0:T(8,128)S(1)} %get-tuple-element.48), channel_id=1, source_target_pairs={{0,256},{128,384},{256,0},{384,128},{1,257},{129,385},{257,1},{385... | collective-permute-start | bytes 405512 | tf_op jit(solution)/shard_map/ppermute | solution.py:259
  75.6 1.9 %collective-permute-start.18 = (f32[264,128]{1,0:T(8,128)S(1)}, f32[264,128]{1,0:T(8,128)S(1)}, u32[]{:S(2)}, u32[]{:S(2)}) collective-permute-start(f32[264,128]{1,0:T(8,128)S(1)} %get-tuple-element.49), channel_id=1, source_target_pairs={{0,384},{128,0},{256,128},{384,256},{1,385},{129,1},{257,129},{385... | collective-permute-start | bytes 405512 | tf_op jit(solution)/shard_map/ppermute | solution.py:259
  77.6 5.6 %collective-permute-done.17.packs_and_out_2_ = f32[264,128]{1,0:T(8,128)S(1)} collective-permute-done((f32[264,128]{1,0:T(8,128)S(1)}, f32[264,128]{1,0:T(8,128)S(1)}, u32[]{:S(2)}, u32[]{:S(2)}) %collective-permute-start.17) | collective-permute-done | bytes 135200 | tf_op jit(solution)/shard_map/ppermute | solution.py:259
  83.3 2.1 %collective-permute-done.18.packs_and_out_3_ = f32[264,128]{1,0:T(8,128)S(1)} collective-permute-done((f32[264,128]{1,0:T(8,128)S(1)}, f32[264,128]{1,0:T(8,128)S(1)}, u32[]{:S(2)}, u32[]{:S(2)}) %collective-permute-start.18) | collective-permute-done | bytes 135200 | tf_op jit(solution)/shard_map/ppermute | solution.py:259
  85.3 2.4 %shard_map.115 = f32[16,1,128]{2,1,0:T(1,128)S(1)} custom-call(s32[5]{0:T(128)S(1)} %stack.32.position, f32[4,2]{1,0:T(4,128)S(1)} %copy.17.frequency, f32[1024,128]{1,0:T(8,128)S(1)} %bitcast.13, f32[264,128]{1,0:T(8,128)S(1)} %get-tuple-element.46.packs_and_out_0_, f32[264,128]{1,0:T(8,128)S(1)} %collective-permute-done.16.packs_and_out_1_, ...), custom_call_target="tpu_custom_call" | custom-call | flops 134217728 | bytes 1048576 | tf_op jit(solution)/shard_map/pallas_call | solution.py:319
  87.7 22.3 %all_to_all.73.terms = f32[16,1,128]{2,1,0:T(1,128)S(1)} all-to-all(f32[16,1,128]{2,1,0:T(1,128)S(1)} %shard_map.115), channel_id=1, replica_groups=mesh['z'=4,'y'=4,'x'=4,'core'=2,'pb'=4] {'pb','z'}, dimensions={0} | all-to-all | bytes 16384 | tf_op jit(solution)/shard_map/all_to_all | solution.py:322
  110.0 0.6 shard_map.116
  (30 shorter events, 0.6 us)
Async XLA Ops:
  0.0 15.8 %copy-start = (f32[2,4,2,64,128]{4,3,2,1,0:T(8,128)S(1)}, f32[2,4,2,64,128]{4,3,2,1,0:T(8,128)}, u32[]{:S(2)}) copy-start(f32[2,4,2,64,128]{4,3,2,1,0:T(8,128)} %coupling.1) | copy-start | bytes 1572868
  0.0 10.0 %collective-permute-start.15 = (f32[2,64,128]{2,1,0:T(8,128)}, f32[2,64,128]{2,1,0:T(8,128)S(1)}, u32[]{:S(2)}, u32[]{:S(2)}) collective-permute-start(f32[2,64,128]{2,1,0:T(8,128)} %gauge.1), channel_id=1, source_target_pairs={{0,4},{4,0},{1,5},{5,1},{2,6},{6,2},{3,7},{7,3},{8,12},{12,8},{9,1... | collective-permute-start | bytes 196616 | tf_op jit(solution)/shard_map/ppermute | solution.py:277
  10.0 0.8 copy-start.1
  12.2 3.6 %copy-start.2 = (f32[2,64,128]{2,1,0:T(8,128)S(1)}, f32[2,64,128]{2,1,0:T(8,128)}, u32[]{:S(2)}) copy-start(f32[2,64,128]{2,1,0:T(8,128)} %gauge.1) | copy-start | bytes 196612
  12.2 10.9 %all-to-all-start = ((f32[4,2,64,128]{3,2,1,0:T(8,128)}), f32[4,2,64,128]{3,2,1,0:T(8,128)S(1)}, u32[]{:S(2)}, u32[]{:S(2)}) async-start(f32[4,2,64,128]{3,2,1,0:T(8,128)} %shard_map.110), calls=%async_computation | async-start | bytes 524288 | tf_op jit(solution)/shard_map/all_to_all | solution.py:252
  23.2 17.1 %all-to-all-start.1 = ((f32[4,2,2,64,128]{4,3,2,1,0:T(8,128)}), f32[4,2,2,64,128]{4,3,2,1,0:T(8,128)S(1)}, u32[]{:S(2)}, u32[]{:S(2)}) async-start(f32[4,2,2,64,128]{4,3,2,1,0:T(8,128)} %shard_map.111), calls=%async_computation.1 | async-start | bytes 1048576 | tf_op jit(solution)/shard_map/all_to_all | solution.py:252
  26.6 0.7 copy-start.10
  29.3 8.6 %collective-permute-start.1 = (f32[4,2,64,128]{3,2,1,0:T(8,128)S(1)}, f32[4,2,64,128]{3,2,1,0:T(8,128)S(1)}, u32[]{:S(2)}, u32[]{:S(2)}) collective-permute-start(f32[4,2,64,128]{3,2,1,0:T(8,128)S(1)} %param.2), channel_id=1, source_target_pairs={{16,0},{24,8},{32,16},{40,24},{48,32},{56,40},{0,48},{8,56},{80,64... | collective-permute-start | bytes 786440 | tf_op jit(solution)/shard_map/cond/branch_2_fun/ppermute | solution.py:76
  42.5 6.4 %copy-start.9 = (s32[3,256]{1,0:T(4,128)S(1)}, s32[3,256]{1,0:T(4,128)}, u32[]{:S(2)}) copy-start(s32[3,256]{1,0:T(4,128)} %param.30) | copy-start | bytes 9220
  42.5 17.8 %all-to-all-start.2 = ((f32[32,32,128]{2,1,0:T(8,128)}), f32[32,32,128]{2,1,0:T(8,128)S(1)}, u32[]{:S(2)}, u32[]{:S(2)}) async-start(f32[32,32,128]{2,1,0:T(8,128)} %bitcast.10), calls=%async_computation.2 | async-start | bytes 1048576 | tf_op jit(solution)/shard_map/all_to_all | solution.py:297
  48.9 0.9 copy-start.8
  62.7 4.1 %copy-start.3 = (f32[2,4,64,128]{3,2,1,0:T(8,128)S(1)}, f32[2,4,64,128]{3,2,1,0:T(8,128)}, u32[]{:S(2)}) copy-start(f32[2,4,64,128]{3,2,1,0:T(8,128)} %eig_left.1) | copy-start | bytes 786436
  62.7 4.1 %copy-start.4 = (f32[2,64,128]{2,1,0:T(8,128)S(1)}, f32[2,64,128]{2,1,0:T(8,128)}, u32[]{:S(2)}) copy-start(f32[2,64,128]{2,1,0:T(8,128)} %eig_right.1) | copy-start | bytes 196612
  62.7 4.1 %copy-start.5 = (f32[2,4,64]{2,1,0:T(4,128)S(1)}, f32[2,4,64]{2,1,0:T(4,128)}, u32[]{:S(2)}) copy-start(f32[2,4,64]{2,1,0:T(4,128)} %energy_kq.1) | copy-start | bytes 6148
  62.7 4.1 %copy-start.6 = (s32[2,4,64]{2,1,0:T(4,128)S(1)}, s32[2,4,64]{2,1,0:T(4,128)}, u32[]{:S(2)}) copy-start(s32[2,4,64]{2,1,0:T(4,128)} %occupied.1) | copy-start | bytes 6148
  62.7 4.1 %copy-start.7 = (f32[2,64]{1,0:T(2,128)S(1)}, f32[2,64]{1,0:T(2,128)}, u32[]{:S(2)}) copy-start(f32[2,64]{1,0:T(2,128)} %energy_k.1) | copy-start | bytes 1540
  62.7 22.6 %all-to-all-start.3 = ((f32[32,32,128]{2,1,0:T(8,128)}), f32[32,32,128]{2,1,0:T(8,128)S(1)}, u32[]{:S(2)}, u32[]{:S(2)}) async-start(f32[32,32,128]{2,1,0:T(8,128)} %bitcast.11), calls=%async_computation.3 | async-start | bytes 1048576 | tf_op jit(solution)/shard_map/all_to_all | solution.py:316
  67.5 10.1 %collective-permute-start.16 = (f32[264,128]{1,0:T(8,128)S(1)}, f32[264,128]{1,0:T(8,128)S(1)}, u32[]{:S(2)}, u32[]{:S(2)}) collective-permute-start(f32[264,128]{1,0:T(8,128)S(1)} %get-tuple-element.47), channel_id=1, source_target_pairs={{0,128},{128,256},{256,384},{384,0},{1,129},{129,257},{257,385},{3... | collective-permute-start | bytes 405512 | tf_op jit(solution)/shard_map/ppermute | solution.py:259
  70.5 7.0 %copy-start.11 = (f32[4,2]{0,1:T(2,128)S(1)}, f32[4,2]{0,1:T(2,128)}, u32[]{:S(2)}) copy-start(f32[4,2]{0,1:T(2,128)} %param.36) | copy-start | bytes 100
  70.5 12.7 %collective-permute-start.17 = (f32[264,128]{1,0:T(8,128)S(1)}, f32[264,128]{1,0:T(8,128)S(1)}, u32[]{:S(2)}, u32[]{:S(2)}) collective-permute-start(f32[264,128]{1,0:T(8,128)S(1)} %get-tuple-element.48), channel_id=1, source_target_pairs={{0,256},{128,384},{256,0},{384,128},{1,257},{129,385},{257,1},{385... | collective-permute-start | bytes 405512 | tf_op jit(solution)/shard_map/ppermute | solution.py:259
  75.6 9.7 %collective-permute-start.18 = (f32[264,128]{1,0:T(8,128)S(1)}, f32[264,128]{1,0:T(8,128)S(1)}, u32[]{:S(2)}, u32[]{:S(2)}) collective-permute-start(f32[264,128]{1,0:T(8,128)S(1)} %get-tuple-element.49), channel_id=1, source_target_pairs={{0,384},{128,0},{256,128},{384,256},{1,385},{129,1},{257,129},{385... | collective-permute-start | bytes 405512 | tf_op jit(solution)/shard_map/ppermute | solution.py:259

commit v6 on v4

--- a/solution.py
+++ b/solution.py
@@ -19,8 +19,6 @@
 KA = ("z", "y", "x", "core")
 VMEM = pl.BlockSpec(memory_space=pltpu.VMEM)
 SMEM = pl.BlockSpec(memory_space=pltpu.SMEM)
-CONTRACT_ROWS = (((0,), (0,)), ((), ()))
-PLAIN = (((1,), (0,)), ((), ()))
 
 
 def halves(value):
@@ -29,19 +27,22 @@
     return high, low
 
 
-def product(left, right, dims):
+def product(left, right, axes):
     left_high, left_low = left
     right_high, right_low = right
-    dot = functools.partial(lax.dot_general, dimension_numbers=dims, preferred_element_type=jnp.float32)
-    return dot(left_high, right_high) + (dot(left_high, right_low) + dot(left_low, right_high))
+    return lax.dot_general(
+        jnp.concatenate([left_high, left_high, left_low], axes[0]),
+        jnp.concatenate([right_high, right_low, right_high], axes[1]),
+        (((axes[0],), (axes[1],)), ((), ())),
+        preferred_element_type=jnp.float32,
+    )
 
 
 def right_block(matrix):
-    real_part = matrix[:, :W]
-    imag_part = matrix[:, W:]
-    upper = jnp.concatenate([real_part, imag_part], -1)
-    lower = jnp.concatenate([-imag_part, real_part], -1)
-    return jnp.concatenate([upper, lower], 0)
+    turned = signs(-1.0) * pltpu.roll(matrix, W, 1)
+    high, low = halves(matrix)
+    turned_high, turned_low = halves(turned)
+    return jnp.concatenate([high, turned_high], 0), jnp.concatenate([low, turned_low], 0)
 
 
 def signs(first):
@@ -50,24 +51,12 @@
 
 
 def apply_left(left, right_pair):
-    both = product(halves(left), halves(right_pair), CONTRACT_ROWS)
+    both = product(halves(left), halves(right_pair), (0, 0))
     sign = signs(1.0)
     return [
         both[:W, at : at + LANES] + sign * pltpu.roll(both[W:, at : at + LANES], W, 1)
         for at in (0, LANES)
     ]
-
-
-def offsets_of(position):
-    along_z, along_y, along_x, core = (position[i] for i in range(4))
-    first = 2 * along_z + (along_y >> 1)
-    second = ((along_y & 1) << 2) + along_x
-    target = position[4]
-    return (
-        ((target >> 5) - first) & 7,
-        ((target >> 2) - second) & 7,
-        (target - 2 * core) & 3,
-    )
 
 
 def translation(number):
@@ -90,9 +79,9 @@
 
 def right_kernel(coupling, gauge, out):
     for k in range(2):
-        block = halves(right_block(gauge[k]))
+        block = right_block(gauge[k])
         rows = coupling[k].reshape(-1, LANES)
-        result = product(halves(rows), block, PLAIN).reshape(4, 2, W, LANES)
+        result = product(halves(rows), block, (1, 0)).reshape(4, 2, W, LANES)
         for q in range(4):
             out[q, k] = result[q]
 
@@ -111,39 +100,38 @@
 
 
 def left_kernel(position, kept, swapped, products, out):
-    core = position[3]
-    offsets = offsets_of(position)
-    carry = ((position[1] >> 1) + offsets[0]) >> 1
+    core, target = position[3], position[4]
+    first = (target >> 5) - 2 * position[0] - (position[1] >> 1)
+    carry = ((position[1] >> 1) + (first & 7)) >> 1
+    wanniers = []
     for l in range(2):
-        third = (2 * core + l + offsets[2]) & 3
+        third = (target + l) & 3
         mine = (third >> 1) == core
         for z in range(4):
             plane = (z + carry) & 3
             gauge = jnp.where(mine, kept[plane, third & 1], swapped[plane, third & 1])
             pair = jnp.concatenate([products[z, l, 0], products[z, l, 1]], -1)
-            for b, wannier in enumerate(apply_left(gauge, pair)):
-                for part in range(2):
-                    start = (part * 2 + b) * 8 + z * 2 + l
-                    out[pl.ds(start, 32, stride=32), :] = wannier[part * 32 : part * 32 + 32]
-
-
-def phase_kernel(position, coords, tables, high, low):
+            wanniers.append((l, z, apply_left(gauge, pair)))
+    for l, z, both in wanniers:
+        for b, wannier in enumerate(both):
+            for part in range(2):
+                start = (part * 2 + b) * 8 + z * 2 + l
+                out[pl.ds(start, 32, stride=32), :] = wannier[part * 32 : part * 32 + 32]
+
+
+def phase_kernel(coords, tables, high, low):
     real, imag = None, None
-    turned = pltpu.roll(coords[...], (NK - W * position[0]) & (NK - 1), 1)
+    divisions = lax.broadcasted_iota(jnp.int32, (FG, NK), 0)
     for axis in range(3):
-        divisions = lax.broadcasted_iota(jnp.int32, (FG, NK), 0)
-        steps = turned[axis : axis + 1, :]
-        onehot = (divisions == steps).astype(jnp.float32)
-        factor = [
-            lax.dot_general(
-                onehot,
-                tables[axis, part],
-                CONTRACT_ROWS,
-                precision=lax.Precision.HIGHEST,
-                preferred_element_type=jnp.float32,
-            )
-            for part in range(2)
-        ]
+        onehot = (divisions == coords[axis : axis + 1, :]).astype(jnp.float32)
+        onehot = onehot.astype(jnp.bfloat16)
+        factor = lax.dot_general(
+            jnp.concatenate([onehot] * 3, 0),
+            tables[axis],
+            (((0,), (0,)), ((), ())),
+            preferred_element_type=jnp.float32,
+        )
+        factor = factor[:, :NK], factor[:, NK:]
         if real is None:
             real, imag = factor
         else:
@@ -158,21 +146,14 @@
 
 
 def fourier_kernel(high, low, columns, out):
-    step = pl.program_id(0)
     parts = [columns[:, at : at + 8, :].reshape(NK, LANES) for at in (0, 8)]
-    result = product((high[...], low[...]), halves(jnp.concatenate(parts, -1)), PLAIN)
+    result = product((high[...], low[...]), halves(jnp.concatenate(parts, -1)), (1, 0))
     sign = signs(-1.0)
     for c in range(2):
         at = c * LANES
         rolled = pltpu.roll(result[NK:, at : at + LANES], W, 1)
         value = result[:NK, at : at + LANES] + sign * rolled
-        for half in range(2):
-
-            @pl.when(step == half)
-            def _(half=half, c=c, value=value):
-                for block in range(8):
-                    start = block * 4 + half * 2 + c
-                    out[pl.ds(start, 32, stride=32), :] = value[block * 32 : block * 32 + 32]
+        out[:, c] = value.reshape(32, 8, LANES)
 
 
 def bloch_kernel(position, frequency, arrived, *packs_and_out):
@@ -183,6 +164,24 @@
         jnp.full((1, LANES), frequency[position[0], b], jnp.float32) for b in range(2)
     ]
     boses = [1.0 / (jnp.exp(phonon / THERMAL) - 1.0) for phonon in phonons]
+    scales = [1.0 / (2.0 * phonon) for phonon in phonons]
+    pairs = []
+    for shift, pack in enumerate(packs):
+        plane = (position[0] - shift + 4) & 3
+        for f in range(2):
+            rows = [
+                arrived[pl.ds((part * 2 + b) * 8 + plane * 2 + f, 32, stride=32), :]
+                for b in range(2)
+                for part in range(2)
+            ]
+            eig_right = pack[LANES + f * W : LANES + f * W + W]
+            half = product(halves(jnp.concatenate(rows, 0)), right_block(eig_right), (1, 0))
+            pairs.append(jnp.concatenate([half[:W], half[W:]], -1))
+    squares = []
+    for shift, pack in enumerate(packs):
+        for f in range(2):
+            blochs = apply_left(pack[f * W : f * W + W], pairs[shift * 2 + f])
+            squares.append([bloch * bloch for bloch in blochs])
     for shift, pack in enumerate(packs):
         tail = pack[2 * LANES :]
         energies = jnp.where(first, tail[0:1], tail[1:2])
@@ -190,29 +189,16 @@
         energy_left = jnp.where(first, states[:W, 2:3], states[:W, 3:4])
         filled = jnp.where(first, states[W:, 2:3], states[W:, 3:4])
         gap = energies - energy_left
-        strengths = []
-        for f in range(2):
-            rows = [
-                arrived[pl.ds((-shift % 4 * 2 + f) * 4 + part * 2 + b, 32, stride=32), :]
-                for b in range(2)
-                for part in range(2)
-            ]
-            eig_right = pack[LANES + f * W : LANES + f * W + W]
-            half = product(
-                halves(jnp.concatenate(rows, 0)), halves(right_block(eig_right)), PLAIN
-            )
-            pair = jnp.concatenate([half[:W], half[W:]], -1)
-            blochs = apply_left(pack[f * W : f * W + W], pair)
-            squares = [bloch * bloch for bloch in blochs]
-            strengths.append([square + pltpu.roll(square, W, 1) for square in squares])
         total = jnp.zeros((W, LANES), jnp.float32)
         for b, (phonon, bose) in enumerate(zip(phonons, boses)):
             up = gap + phonon
             down = gap - phonon
-            kernel = (bose + filled) * up / (up * up + BROADEN * BROADEN)
-            kernel = kernel + (bose + 1.0 - filled) * down / (down * down + BROADEN * BROADEN)
-            strength = jnp.where(first, strengths[0][b], strengths[1][b])
-            total = total + strength / (2.0 * phonon) * kernel
+            up_square = up * up + BROADEN * BROADEN
+            down_square = down * down + BROADEN * BROADEN
+            terms = (bose + filled) * up * down_square + (bose + 1.0 - filled) * down * up_square
+            one, two = squares[shift * 2][b], squares[shift * 2 + 1][b]
+            strength = jnp.where(first, one, two) + pltpu.roll(jnp.where(first, two, one), W, 1)
+            total = total + strength * scales[b] * terms / (up_square * down_square)
         summed = jnp.sum(total, axis=0, keepdims=True) * (1.0 / 1024.0)
         plane = (position[0] - shift + 4) & 3
         for group in range(4):
@@ -237,7 +223,12 @@
             angle = 2.0 * math.pi * ((cell * steps) % FG) / FG
             tables[axis, 0] += np.cos(angle) / size
             tables[axis, 1] += np.sin(angle) / size
-    return tables.astype(np.float32)
+    tables = np.concatenate([tables[:, 0], tables[:, 1]], -1)
+    terms = []
+    for _ in range(3):
+        terms.append(tables.astype(jnp.bfloat16))
+        tables = tables - terms[-1].astype(np.float64)
+    return np.concatenate(terms, 1)
 
 
 def call(kernel, shapes, specs, flops, vmem=16, **more):
@@ -281,16 +272,16 @@
 ):
     along_z, along_y, along_x, core = (lax.axis_index(name) for name in KA)
     target = kq_index[lax.axis_index("pb") * 4 + along_z, 0]
-    position = jnp.stack([along_z, along_y, along_x, core, target])
+    number = (((target >> 2) - (along_y * 4 + along_x)) & 7) + (
+        (((target >> 5) - (along_y >> 1)) & 1) << 3
+    )
+    position = jnp.stack([along_z, along_y, along_x, core, target, number])
     planes = spread(jnp.broadcast_to(gauge[None], (4, 2, W, LANES)))
     products = call(right_kernel, f32(4, 2, 2, W, LANES), [VMEM, VMEM], 1 << 27)(coupling, gauge)
     products = spread(products)
     packs = call(pack_kernel, [f32(264, LANES)] * 4, [SMEM] + [VMEM] * 5, 1 << 20)(
         position, eig_left, eig_right, energy_k, energy_kq, occupied
     )
-    number = (((target >> 2) - (along_y * 4 + along_x)) & 7) + (
-        (((target >> 5) - (along_y >> 1)) & 1) << 3
-    )
     branches = [functools.partial(translated, number=number) for number in range(16)]
     kept = lax.switch(number, branches, planes)
     swapped = lax.ppermute(kept, "core", [(0, 1), (1, 0)])
@@ -299,22 +290,21 @@
     )
     columns = lax.all_to_all(pieces.reshape(32, 32, LANES), ("y", "x", "core"), 0, 0, tiled=True)
     packs = shifted(packs)
-    coords = fine_coords.reshape(3, 4, 32, 2).transpose(0, 1, 3, 2).reshape(3, NK)
-    coords = jnp.pad(coords, ((0, 5), (0, 0)))
+    coords = fine_coords.reshape(3, 4, 32, 2).transpose(0, 2, 1, 3).reshape(3, NK)
     high, low = call(
         phase_kernel,
         [jax.ShapeDtypeStruct((2 * NK, NK), jnp.bfloat16)] * 2,
-        [SMEM, VMEM, VMEM],
+        [VMEM, VMEM],
         1 << 28,
-    )(position, coords, jnp.asarray(phase_tables()))
+    )(coords, jnp.asarray(phase_tables()))
     fixed = pl.BlockSpec((2 * NK, NK), lambda i: (0, 0))
     fine = call(
         fourier_kernel,
-        f32(1024, LANES),
+        f32(32, 4, 8, LANES),
         [fixed, fixed, pl.BlockSpec((32, 16, LANES), lambda i: (0, i, 0))],
         1 << 28,
         grid=(2,),
-        out_specs=pl.BlockSpec((1024, LANES), lambda i: (0, 0)),
+        out_specs=pl.BlockSpec((32, 2, 8, LANES), lambda i: (0, i, 0, 0)),
     )(high, low, columns)
     blocks = lax.all_to_all(
         fine.reshape(32, 32, LANES), ("y", "x", "core"), 0, 0, tiled=True

time: 112 us -> 110 us (0.982)
  Pallas kernels: 11.7 us -> 8.35 us
  waiting for transfers between devices: 24.3 us -> 25.7 us
    pallas_call x1, Pallas kernels: 2.1 us -> 0.44 us  [shards(): call(phase_kernel, [jax.ShapeDtypeStruct((2 * NK, NK), jnp.bfloat16)] * 2...]
    all_to_all x1, waiting for transfers between devices: 8.38 us -> 9.82 us  [shards(): lax.all_to_all(pieces.reshape(32, 32, LANES), ('y', 'x', 'core'), 0, 0, t...]
  transfers between devices with their start and end apart: 9 -> 9, of which waited for: 6 -> 6; matrix products, arithmetic and copies ran while one was open for 2% -> 2% of each run, Pallas kernels for 4% -> 2%
where the time goes in v6:
time: 110 us; the launch traced here: 108 us
  starting transfers between devices  45.2 us (41%)
  waiting for transfers between devices  25.7 us (23%)
  blocking collectives  22.3 us (20%)
  Pallas kernels  8.35 us (8%)
  local copies, waits for them, and re-layouts  4.22 us (4%)
  between operations  1.49 us (1%)
    all_to_all x1, blocking collectives, shards(): terms = lax.all_to_all(terms, ('z', 'pb'), 0, 0, tiled=True)  22.3 us
    all_to_all x2, starting transfers between devices, spread(): return lax.all_to_all(value, 'z', 0, 0, tiled=True)  10 us
    ppermute x3, starting transfers between devices, shifted(): arrived.append(lax.ppermute(values[shift], 'z', pairs))  9.93 us
    all_to_all x1, waiting for transfers between devices, shards(): lax.all_to_all(pieces.reshape(32, 32, LANES), ('y', 'x', 'core'), 0, 0, t...  9.82 us
    all_to_all x1, starting transfers between devices, shards(): lax.all_to_all(pieces.reshape(32, 32, LANES), ('y', 'x', 'core'), 0, 0, t...  7.84 us
    ppermute x3, waiting for transfers between devices, shifted(): arrived.append(lax.ppermute(values[shift], 'z', pairs))  7.7 us
    ppermute x1, starting transfers between devices, translated(): return lax.ppermute(value, ('y', 'x'), pairs)  7.6 us
    ppermute x1, starting transfers between devices, shards(): swapped = lax.ppermute(kept, 'core', [(0, 1), (1, 0)])  5.7 us
  transfers between devices with their start and end apart: 9, of which 6 were waited for; matrix products, arithmetic and copies ran while one was open for 2% of the time, Pallas kernels for 2%

profile of v6, /device:TPU:1, one launch (start us, length us, event | category | flops | bytes accessed | tf_op | source)
XLA Modules:
  0.0 108.0 jit_solution(10854800725942761605)
XLA Ops:
  0.0 1.6 %broadcast_in_dim.2 = f32[4,2,64,128]{3,2,1,0:T(8,128)} broadcast(f32[2,64,128]{2,1,0:T(8,128)} %gauge.1), dimensions={1,2,3} | broadcast | bytes 327680 | tf_op jit(solution)/shard_map/broadcast_in_dim | solution.py:279
  1.6 6.6 %all-to-all-start = ((f32[4,2,64,128]{3,2,1,0:T(8,128)}), f32[4,2,64,128]{3,2,1,0:T(8,128)S(1)}, u32[]{:S(2)}, u32[]{:S(2)}) async-start(f32[4,2,64,128]{3,2,1,0:T(8,128)} %broadcast_in_dim.2), calls=%async_computation | async-start | bytes 524288 | tf_op jit(solution)/shard_map/all_to_all | solution.py:250
  8.2 1.2 %shard_map.110 = f32[4,2,2,64,128]{4,3,2,1,0:T(8,128)} custom-call(f32[2,4,2,64,128]{4,3,2,1,0:T(8,128)S(1)} %copy-done, f32[2,64,128]{2,1,0:T(8,128)S(1)} %copy-done.1), custom_call_target="tpu_custom_call" | custom-call | flops 134217728 | bytes 1048576 | tf_op jit(solution)/shard_map/pallas_call | solution.py:280
  9.4 4.4 %all-to-all-done = f32[4,2,64,128]{3,2,1,0:T(8,128)S(1)} async-done(((f32[4,2,64,128]{3,2,1,0:T(8,128)}), f32[4,2,64,128]{3,2,1,0:T(8,128)S(1)}, u32[]{:S(2)}, u32[]{:S(2)}) %all-to-all-start) | async-done | bytes 262176 | tf_op jit(solution)/shard_map/all_to_all | solution.py:250
  13.8 3.5 %all-to-all-start.1 = ((f32[4,2,2,64,128]{4,3,2,1,0:T(8,128)}), f32[4,2,2,64,128]{4,3,2,1,0:T(8,128)S(1)}, u32[]{:S(2)}, u32[]{:S(2)}) async-start(f32[4,2,2,64,128]{4,3,2,1,0:T(8,128)} %shard_map.110), calls=%async_computation.1 | async-start | bytes 1048576 | tf_op jit(solution)/shard_map/all_to_all | solution.py:250
  17.3 0.7 copy-done.10
  18.0 0.7 fusion
  19.9 11.0 %conditional.1 = (f32[4,2,64,128]{3,2,1,0:T(8,128)S(1)}) conditional(s32[]{:T(128)} %clamp.3, f32[4,2,64,128]{3,2,1,0:T(8,128)S(1)} %all-to-all-done, f32[4,2,64,128]{3,2,1,0:T(8,128)S(1)} %all-to-all-done, f32[4,2,64,128]{3,2,1,0:T(8,128)S(1)} %all-to-all-done, f32[4,2,64,128]{3,2,1,0:T(8,128)S(1)} %all-to-all-done, ...), branch_computations={%region_0.0_spmd, %region_1.0_spmd, %region_2.0_spmd, %region_3.0_... | conditional | bytes 1572912 | solution.py:286
  20.0 7.6 %collective-permute-start.1 = (f32[4,2,64,128]{3,2,1,0:T(8,128)S(1)}, f32[4,2,64,128]{3,2,1,0:T(8,128)S(1)}, u32[]{:S(2)}, u32[]{:S(2)}) collective-permute-start(f32[4,2,64,128]{3,2,1,0:T(8,128)S(1)} %param.2), channel_id=1, source_target_pairs={{16,0},{24,8},{32,16},{40,24},{48,32},{56,40},{0,48},{8,56},{80,64... | collective-permute-start | bytes 786440 | tf_op jit(solution)/shard_map/cond/branch_2_fun/ppermute | solution.py:77
  27.6 3.3 %collective-permute-done.1 = f32[4,2,64,128]{3,2,1,0:T(8,128)S(1)} collective-permute-done((f32[4,2,64,128]{3,2,1,0:T(8,128)S(1)}, f32[4,2,64,128]{3,2,1,0:T(8,128)S(1)}, u32[]{:S(2)}, u32[]{:S(2)}) %collective-permute-start.1) | collective-permute-done | bytes 262176 | tf_op jit(solution)/shard_map/cond/branch_2_fun/ppermute | solution.py:77
  30.9 5.7 %collective-permute-start.15 = (f32[4,2,64,128]{3,2,1,0:T(8,128)S(1)}, f32[4,2,64,128]{3,2,1,0:T(8,128)S(1)}, u32[]{:S(2)}, u32[]{:S(2)}) collective-permute-start(f32[4,2,64,128]{3,2,1,0:T(8,128)S(1)} %get-tuple-element.52.kept), channel_id=1, source_target_pairs={{0,4},{4,0},{1,5},{5,1},{2,6},{6,2},{3,7},{7,3},{8,12},{12,8},{9,1... | collective-permute-start | bytes 786440 | tf_op jit(solution)/shard_map/ppermute | solution.py:287
  36.6 0.6 stack.23.position
  37.3 0.5 collective-permute-done.15.swapped
  37.8 2.0 %shard_map.111 = f32[1024,128]{1,0:T(8,128)} custom-call(s32[6]{0:T(128)S(1)} %stack.23.position, f32[4,2,64,128]{3,2,1,0:T(8,128)S(1)} %get-tuple-element.52.kept, f32[4,2,64,128]{3,2,1,0:T(8,128)S(1)} %collective-permute-done.15.swapped, f32[4,2,2,64,128]{4,3,2,1,0:T(8,128)S(1)} %all-to-all-done.1.products), custom_call_target="tpu_custom_call" | custom-call | flops 134217728 | bytes 1048576 | tf_op jit(solution)/shard_map/pallas_call | solution.py:288
  39.7 7.8 %all-to-all-start.2 = ((f32[32,32,128]{2,1,0:T(8,128)}), f32[32,32,128]{2,1,0:T(8,128)S(1)}, u32[]{:S(2)}, u32[]{:S(2)}) async-start(f32[32,32,128]{2,1,0:T(8,128)} %bitcast.9), calls=%async_computation.2 | async-start | bytes 1048576 | tf_op jit(solution)/shard_map/all_to_all | solution.py:291
  47.6 0.2 reshape.20
  47.8 0.1 copy.14
  47.9 0.2 reshape.21.coords
  48.1 0.6 copy-done.7
  48.7 0.4 shard_map.109
  49.2 9.8 %all-to-all-done.2.columns = f32[32,32,128]{2,1,0:T(8,128)S(1)} async-done(((f32[32,32,128]{2,1,0:T(8,128)}), f32[32,32,128]{2,1,0:T(8,128)S(1)}, u32[]{:S(2)}, u32[]{:S(2)}) %all-to-all-start.2) | async-done | bytes 524320 | tf_op jit(solution)/shard_map/all_to_all | solution.py:291
  59.0 1.7 %shard_map.112 = f32[32,4,8,128]{3,2,1,0:T(8,128)} custom-call(bf16[512,256]{1,0:T(8,128)(2,1)S(1)} %get-tuple-element.44.high, bf16[512,256]{1,0:T(8,128)(2,1)S(1)} %get-tuple-element.45.low, f32[32,32,128]{2,1,0:T(8,128)S(1)} %all-to-all-done.2.columns), custom_call_target="tpu_custom_call" | custom-call | flops 268435456 | bytes 1048576 | tf_op jit(solution)/shard_map/pallas_call | solution.py:301
  60.7 4.1 %all-to-all-start.3 = ((f32[32,32,128]{2,1,0:T(8,128)}), f32[32,32,128]{2,1,0:T(8,128)S(1)}, u32[]{:S(2)}, u32[]{:S(2)}) async-start(f32[32,32,128]{2,1,0:T(8,128)} %bitcast.10), calls=%async_computation.3 | async-start | bytes 1048576 | tf_op jit(solution)/shard_map/all_to_all | solution.py:309
  64.9 0.6 shard_map.113
  65.5 3.0 %collective-permute-start.16 = (f32[264,128]{1,0:T(8,128)S(1)}, f32[264,128]{1,0:T(8,128)S(1)}, u32[]{:S(2)}, u32[]{:S(2)}) collective-permute-start(f32[264,128]{1,0:T(8,128)S(1)} %get-tuple-element.47), channel_id=1, source_target_pairs={{0,128},{128,256},{256,384},{384,0},{1,129},{129,257},{257,385},{3... | collective-permute-start | bytes 405512 | tf_op jit(solution)/shard_map/ppermute | solution.py:257
  68.5 5.0 %collective-permute-start.17 = (f32[264,128]{1,0:T(8,128)S(1)}, f32[264,128]{1,0:T(8,128)S(1)}, u32[]{:S(2)}, u32[]{:S(2)}) collective-permute-start(f32[264,128]{1,0:T(8,128)S(1)} %get-tuple-element.48), channel_id=1, source_target_pairs={{0,256},{128,384},{256,0},{384,128},{1,257},{129,385},{257,1},{385... | collective-permute-start | bytes 405512 | tf_op jit(solution)/shard_map/ppermute | solution.py:257
  73.5 1.9 %collective-permute-start.18 = (f32[264,128]{1,0:T(8,128)S(1)}, f32[264,128]{1,0:T(8,128)S(1)}, u32[]{:S(2)}, u32[]{:S(2)}) collective-permute-start(f32[264,128]{1,0:T(8,128)S(1)} %get-tuple-element.49), channel_id=1, source_target_pairs={{0,384},{128,0},{256,128},{384,256},{1,385},{129,1},{257,129},{385... | collective-permute-start | bytes 405512 | tf_op jit(solution)/shard_map/ppermute | solution.py:257
  75.6 5.6 %collective-permute-done.17.packs_and_out_2_ = f32[264,128]{1,0:T(8,128)S(1)} collective-permute-done((f32[264,128]{1,0:T(8,128)S(1)}, f32[264,128]{1,0:T(8,128)S(1)}, u32[]{:S(2)}, u32[]{:S(2)}) %collective-permute-start.17) | collective-permute-done | bytes 135200 | tf_op jit(solution)/shard_map/ppermute | solution.py:257
  81.2 2.1 %collective-permute-done.18.packs_and_out_3_ = f32[264,128]{1,0:T(8,128)S(1)} collective-permute-done((f32[264,128]{1,0:T(8,128)S(1)}, f32[264,128]{1,0:T(8,128)S(1)}, u32[]{:S(2)}, u32[]{:S(2)}) %collective-permute-start.18) | collective-permute-done | bytes 135200 | tf_op jit(solution)/shard_map/ppermute | solution.py:257
  83.3 1.8 %shard_map.114 = f32[16,1,128]{2,1,0:T(1,128)S(1)} custom-call(s32[6]{0:T(128)S(1)} %stack.23.position, f32[4,2]{1,0:T(4,128)S(1)} %copy.15.frequency, f32[1024,128]{1,0:T(8,128)S(1)} %bitcast.12, f32[264,128]{1,0:T(8,128)S(1)} %get-tuple-element.46.packs_and_out_0_, f32[264,128]{1,0:T(8,128)S(1)} %collective-permute-done.16.packs_and_out_1_, ...), custom_call_target="tpu_custom_call" | custom-call | flops 134217728 | bytes 1048576 | tf_op jit(solution)/shard_map/pallas_call | solution.py:312
  85.1 22.3 %all_to_all.73.terms = f32[16,1,128]{2,1,0:T(1,128)S(1)} all-to-all(f32[16,1,128]{2,1,0:T(1,128)S(1)} %shard_map.114), channel_id=1, replica_groups=mesh['z'=4,'y'=4,'x'=4,'core'=2,'pb'=4] {'z','pb'}, dimensions={0} | all-to-all | bytes 16384 | tf_op jit(solution)/shard_map/all_to_all | solution.py:315
  107.3 0.6 shard_map.115
  (25 shorter events, 0.2 us)
Async XLA Ops:
  0.0 8.2 %copy-start = (f32[2,4,2,64,128]{4,3,2,1,0:T(8,128)S(1)}, f32[2,4,2,64,128]{4,3,2,1,0:T(8,128)}, u32[]{:S(2)}) copy-start(f32[2,4,2,64,128]{4,3,2,1,0:T(8,128)} %coupling.1) | copy-start | bytes 1572868
  1.6 6.6 %copy-start.1 = (f32[2,64,128]{2,1,0:T(8,128)S(1)}, f32[2,64,128]{2,1,0:T(8,128)}, u32[]{:S(2)}) copy-start(f32[2,64,128]{2,1,0:T(8,128)} %gauge.1) | copy-start | bytes 196612
  1.6 12.2 %all-to-all-start = ((f32[4,2,64,128]{3,2,1,0:T(8,128)}), f32[4,2,64,128]{3,2,1,0:T(8,128)S(1)}, u32[]{:S(2)}, u32[]{:S(2)}) async-start(f32[4,2,64,128]{3,2,1,0:T(8,128)} %broadcast_in_dim.2), calls=%async_computation | async-start | bytes 524288 | tf_op jit(solution)/shard_map/all_to_all | solution.py:250
  13.8 23.9 %all-to-all-start.1 = ((f32[4,2,2,64,128]{4,3,2,1,0:T(8,128)}), f32[4,2,2,64,128]{4,3,2,1,0:T(8,128)S(1)}, u32[]{:S(2)}, u32[]{:S(2)}) async-start(f32[4,2,2,64,128]{4,3,2,1,0:T(8,128)} %shard_map.110), calls=%async_computation.1 | async-start | bytes 1048576 | tf_op jit(solution)/shard_map/all_to_all | solution.py:250
  17.3 0.7 copy-start.10
  20.0 10.9 %collective-permute-start.1 = (f32[4,2,64,128]{3,2,1,0:T(8,128)S(1)}, f32[4,2,64,128]{3,2,1,0:T(8,128)S(1)}, u32[]{:S(2)}, u32[]{:S(2)}) collective-permute-start(f32[4,2,64,128]{3,2,1,0:T(8,128)S(1)} %param.2), channel_id=1, source_target_pairs={{16,0},{24,8},{32,16},{40,24},{48,32},{56,40},{0,48},{8,56},{80,64... | collective-permute-start | bytes 786440 | tf_op jit(solution)/shard_map/cond/branch_2_fun/ppermute | solution.py:77
  30.9 6.9 %collective-permute-start.15 = (f32[4,2,64,128]{3,2,1,0:T(8,128)S(1)}, f32[4,2,64,128]{3,2,1,0:T(8,128)S(1)}, u32[]{:S(2)}, u32[]{:S(2)}) collective-permute-start(f32[4,2,64,128]{3,2,1,0:T(8,128)S(1)} %get-tuple-element.52.kept), channel_id=1, source_target_pairs={{0,4},{4,0},{1,5},{5,1},{2,6},{6,2},{3,7},{7,3},{8,12},{12,8},{9,1... | collective-permute-start | bytes 786440 | tf_op jit(solution)/shard_map/ppermute | solution.py:287
  39.7 7.9 %copy-start.8 = (s32[3,256]{1,0:T(4,128)S(1)}, s32[3,256]{1,0:T(4,128)}, u32[]{:S(2)}) copy-start(s32[3,256]{1,0:T(4,128)} %param.30) | copy-start | bytes 9220
  39.7 19.3 %all-to-all-start.2 = ((f32[32,32,128]{2,1,0:T(8,128)}), f32[32,32,128]{2,1,0:T(8,128)S(1)}, u32[]{:S(2)}, u32[]{:S(2)}) async-start(f32[32,32,128]{2,1,0:T(8,128)} %bitcast.9), calls=%async_computation.2 | async-start | bytes 1048576 | tf_op jit(solution)/shard_map/all_to_all | solution.py:291
  47.8 1.0 copy-start.7
  60.7 4.1 %copy-start.2 = (f32[2,4,64,128]{3,2,1,0:T(8,128)S(1)}, f32[2,4,64,128]{3,2,1,0:T(8,128)}, u32[]{:S(2)}) copy-start(f32[2,4,64,128]{3,2,1,0:T(8,128)} %eig_left.1) | copy-start | bytes 786436
  60.7 4.1 %copy-start.3 = (f32[2,64,128]{2,1,0:T(8,128)S(1)}, f32[2,64,128]{2,1,0:T(8,128)}, u32[]{:S(2)}) copy-start(f32[2,64,128]{2,1,0:T(8,128)} %eig_right.1) | copy-start | bytes 196612
  60.7 4.1 %copy-start.4 = (f32[2,4,64]{2,1,0:T(4,128)S(1)}, f32[2,4,64]{2,1,0:T(4,128)}, u32[]{:S(2)}) copy-start(f32[2,4,64]{2,1,0:T(4,128)} %energy_kq.1) | copy-start | bytes 6148
  60.7 4.1 %copy-start.5 = (s32[2,4,64]{2,1,0:T(4,128)S(1)}, s32[2,4,64]{2,1,0:T(4,128)}, u32[]{:S(2)}) copy-start(s32[2,4,64]{2,1,0:T(4,128)} %occupied.1) | copy-start | bytes 6148
  60.7 4.1 %copy-start.6 = (f32[2,64]{1,0:T(2,128)S(1)}, f32[2,64]{1,0:T(2,128)}, u32[]{:S(2)}) copy-start(f32[2,64]{1,0:T(2,128)} %energy_k.1) | copy-start | bytes 1540
  60.7 22.6 %all-to-all-start.3 = ((f32[32,32,128]{2,1,0:T(8,128)}), f32[32,32,128]{2,1,0:T(8,128)S(1)}, u32[]{:S(2)}, u32[]{:S(2)}) async-start(f32[32,32,128]{2,1,0:T(8,128)} %bitcast.10), calls=%async_computation.3 | async-start | bytes 1048576 | tf_op jit(solution)/shard_map/all_to_all | solution.py:309
  65.5 10.1 %collective-permute-start.16 = (f32[264,128]{1,0:T(8,128)S(1)}, f32[264,128]{1,0:T(8,128)S(1)}, u32[]{:S(2)}, u32[]{:S(2)}) collective-permute-start(f32[264,128]{1,0:T(8,128)S(1)} %get-tuple-element.47), channel_id=1, source_target_pairs={{0,128},{128,256},{256,384},{384,0},{1,129},{129,257},{257,385},{3... | collective-permute-start | bytes 405512 | tf_op jit(solution)/shard_map/ppermute | solution.py:257
  68.5 7.0 %copy-start.9 = (f32[4,2]{0,1:T(2,128)S(1)}, f32[4,2]{0,1:T(2,128)}, u32[]{:S(2)}) copy-start(f32[4,2]{0,1:T(2,128)} %param.36) | copy-start | bytes 100
  68.5 12.7 %collective-permute-start.17 = (f32[264,128]{1,0:T(8,128)S(1)}, f32[264,128]{1,0:T(8,128)S(1)}, u32[]{:S(2)}, u32[]{:S(2)}) collective-permute-start(f32[264,128]{1,0:T(8,128)S(1)} %get-tuple-element.48), channel_id=1, source_target_pairs={{0,256},{128,384},{256,0},{384,128},{1,257},{129,385},{257,1},{385... | collective-permute-start | bytes 405512 | tf_op jit(solution)/shard_map/ppermute | solution.py:257
  73.5 9.7 %collective-permute-start.18 = (f32[264,128]{1,0:T(8,128)S(1)}, f32[264,128]{1,0:T(8,128)S(1)}, u32[]{:S(2)}, u32[]{:S(2)}) collective-permute-start(f32[264,128]{1,0:T(8,128)S(1)} %get-tuple-element.49), channel_id=1, source_target_pairs={{0,384},{128,0},{256,128},{384,256},{1,385},{129,1},{257,129},{385... | collective-permute-start | bytes 405512 | tf_op jit(solution)/shard_map/ppermute | solution.py:257

commit v7 on v6

--- a/solution.py
+++ b/solution.py
@@ -77,18 +77,25 @@
     return lax.ppermute(value, ("y", "x"), pairs)
 
 
-def right_kernel(coupling, gauge, out):
+def prepare_kernel(
+    coupling, gauge, coords, tables, eig_left, eig_right, energy_k, energy_kq, occupied, *outs
+):
+    right_part(coupling, gauge, outs[0])
+    pack_part(eig_left, eig_right, energy_k, energy_kq, occupied, outs[3:])
+    phase_part(coords, tables, outs[1], outs[2])
+
+
+def right_part(coupling, gauge, out):
     for k in range(2):
-        block = right_block(gauge[k])
         rows = coupling[k].reshape(-1, LANES)
-        result = product(halves(rows), block, (1, 0)).reshape(4, 2, W, LANES)
+        result = product(halves(rows), right_block(gauge[k]), (1, 0)).reshape(4, 2, W, LANES)
         for q in range(4):
             out[q, k] = result[q]
 
 
-def pack_kernel(position, eig_left, eig_right, energy_k, energy_kq, occupied, *outs):
+def pack_part(eig_left, eig_right, energy_k, energy_kq, occupied, outs):
     for shift, out in enumerate(outs):
-        q = (position[0] + shift) & 3
+        q = (lax.axis_index("z") + shift) & 3
         for f in range(2):
             out[f * W : f * W + W] = eig_left[f, q]
             out[LANES + f * W : LANES + f * W + W] = eig_right[f]
@@ -99,16 +106,17 @@
         out[2 * LANES + 4 :] = jnp.zeros((4, LANES), jnp.float32)
 
 
-def left_kernel(position, kept, swapped, products, out):
-    core, target = position[3], position[4]
-    first = (target >> 5) - 2 * position[0] - (position[1] >> 1)
-    carry = ((position[1] >> 1) + (first & 7)) >> 1
+def left_kernel(target, kept, swapped, products, out):
+    along_z, along_y, core = (lax.axis_index(name) for name in ("z", "y", "core"))
+    target = target[0]
+    first = (target >> 5) - 2 * along_z - (along_y >> 1)
+    carry = ((along_y >> 1) + (first & 7)) >> 1
     wanniers = []
     for l in range(2):
         third = (target + l) & 3
         mine = (third >> 1) == core
         for z in range(4):
-            plane = (z + carry) & 3
+            plane = (z + carry - along_z + 4) & 3
             gauge = jnp.where(mine, kept[plane, third & 1], swapped[plane, third & 1])
             pair = jnp.concatenate([products[z, l, 0], products[z, l, 1]], -1)
             wanniers.append((l, z, apply_left(gauge, pair)))
@@ -119,9 +127,15 @@
                 out[pl.ds(start, 32, stride=32), :] = wannier[part * 32 : part * 32 + 32]
 
 
-def phase_kernel(coords, tables, high, low):
+def phase_part(coords, tables, high, low):
+    source = lax.broadcasted_iota(jnp.int32, (NK, NK), 0)
+    row = lax.broadcasted_iota(jnp.int32, (NK, NK), 1)
+    wanted = (((row >> 1) & 3) << 6) + ((row >> 3) << 1) + (row & 1)
+    turn = (source == wanted).astype(jnp.float32).astype(jnp.bfloat16)
+    points = coords[...].astype(jnp.float32).astype(jnp.bfloat16)
+    coords = jnp.dot(points, turn, preferred_element_type=jnp.float32)
     real, imag = None, None
-    divisions = lax.broadcasted_iota(jnp.int32, (FG, NK), 0)
+    divisions = lax.broadcasted_iota(jnp.int32, (FG, NK), 0).astype(jnp.float32)
     for axis in range(3):
         onehot = (divisions == coords[axis : axis + 1, :]).astype(jnp.float32)
         onehot = onehot.astype(jnp.bfloat16)
@@ -156,18 +170,18 @@
         out[:, c] = value.reshape(32, 8, LANES)
 
 
-def bloch_kernel(position, frequency, arrived, *packs_and_out):
+def bloch_kernel(frequency, arrived, *packs_and_out):
     packs, out = packs_and_out[:4], packs_and_out[4]
     lane = lax.broadcasted_iota(jnp.int32, (1, LANES), 1)
     first = lane < W
     phonons = [
-        jnp.full((1, LANES), frequency[position[0], b], jnp.float32) for b in range(2)
+        jnp.full((1, LANES), frequency[lax.axis_index("z"), b], jnp.float32) for b in range(2)
     ]
     boses = [1.0 / (jnp.exp(phonon / THERMAL) - 1.0) for phonon in phonons]
     scales = [1.0 / (2.0 * phonon) for phonon in phonons]
     pairs = []
     for shift, pack in enumerate(packs):
-        plane = (position[0] - shift + 4) & 3
+        plane = (lax.axis_index("z") - shift + 4) & 3
         for f in range(2):
             rows = [
                 arrived[pl.ds((part * 2 + b) * 8 + plane * 2 + f, 32, stride=32), :]
@@ -200,7 +214,7 @@
             strength = jnp.where(first, one, two) + pltpu.roll(jnp.where(first, two, one), W, 1)
             total = total + strength * scales[b] * terms / (up_square * down_square)
         summed = jnp.sum(total, axis=0, keepdims=True) * (1.0 / 1024.0)
-        plane = (position[0] - shift + 4) & 3
+        plane = (lax.axis_index("z") - shift + 4) & 3
         for group in range(4):
             out[plane * 4 + group] = summed
 
@@ -270,33 +284,49 @@
     occupied,
     frequency,
 ):
-    along_z, along_y, along_x, core = (lax.axis_index(name) for name in KA)
+    along_z, along_y, along_x, _ = (lax.axis_index(name) for name in KA)
     target = kq_index[lax.axis_index("pb") * 4 + along_z, 0]
     number = (((target >> 2) - (along_y * 4 + along_x)) & 7) + (
         (((target >> 5) - (along_y >> 1)) & 1) << 3
     )
-    position = jnp.stack([along_z, along_y, along_x, core, target, number])
-    planes = spread(jnp.broadcast_to(gauge[None], (4, 2, W, LANES)))
-    products = call(right_kernel, f32(4, 2, 2, W, LANES), [VMEM, VMEM], 1 << 27)(coupling, gauge)
+    planes = [gauge]
+    for ahead in (1, 2, 15):
+        ring = [place % 4 * 4 + place // 4 for place in range(16)]
+        pairs = [(ring[(place + ahead) % 16], ring[place]) for place in range(16)]
+        planes.append(lax.ppermute(gauge, ("z", "pb"), pairs))
+    planes = jnp.stack(planes)
+    products, high, low, *packs = call(
+        prepare_kernel,
+        [f32(4, 2, 2, W, LANES)]
+        + [jax.ShapeDtypeStruct((2 * NK, NK), jnp.bfloat16)] * 2
+        + [f32(264, LANES)] * 4,
+        [VMEM] * 9,
+        1 << 27,
+    )(
+        *(
+            pltpu.with_memory_space_constraint(value, pltpu.HBM)
+            for value in (
+                coupling,
+                gauge,
+                fine_coords,
+                jnp.asarray(phase_tables()),
+                eig_left,
+                eig_right,
+                energy_k,
+                energy_kq,
+                occupied,
+            )
+        )
+    )
     products = spread(products)
-    packs = call(pack_kernel, [f32(264, LANES)] * 4, [SMEM] + [VMEM] * 5, 1 << 20)(
-        position, eig_left, eig_right, energy_k, energy_kq, occupied
-    )
     branches = [functools.partial(translated, number=number) for number in range(16)]
     kept = lax.switch(number, branches, planes)
     swapped = lax.ppermute(kept, "core", [(0, 1), (1, 0)])
     pieces = call(left_kernel, f32(1024, LANES), [SMEM] + [VMEM] * 3, 1 << 27)(
-        position, kept, swapped, products
+        target.reshape(1), kept, swapped, products
     )
     columns = lax.all_to_all(pieces.reshape(32, 32, LANES), ("y", "x", "core"), 0, 0, tiled=True)
     packs = shifted(packs)
-    coords = fine_coords.reshape(3, 4, 32, 2).transpose(0, 2, 1, 3).reshape(3, NK)
-    high, low = call(
-        phase_kernel,
-        [jax.ShapeDtypeStruct((2 * NK, NK), jnp.bfloat16)] * 2,
-        [VMEM, VMEM],
-        1 << 28,
-    )(coords, jnp.asarray(phase_tables()))
     fixed = pl.BlockSpec((2 * NK, NK), lambda i: (0, 0))
     fine = call(
         fourier_kernel,
@@ -309,8 +339,8 @@
     blocks = lax.all_to_all(
         fine.reshape(32, 32, LANES), ("y", "x", "core"), 0, 0, tiled=True
     )
-    terms = call(bloch_kernel, f32(16, 1, LANES), [SMEM, SMEM] + [VMEM] * 5, 1 << 27)(
-        position, frequency, blocks.reshape(1024, LANES), *packs
+    terms = call(bloch_kernel, f32(16, 1, LANES), [SMEM] + [VMEM] * 5, 1 << 27)(
+        frequency, blocks.reshape(1024, LANES), *packs
     )
     terms = lax.all_to_all(terms, ("z", "pb"), 0, 0, tiled=True)
     return call(sum_kernel, f32(2, W), [VMEM], 1 << 12)(terms)

time: 110 us -> 111 us (level)
  blocking collectives: 22.3 us -> 41.6 us
  waiting for transfers between devices: 25.7 us -> 10.9 us
  local copies, waits for them, and re-layouts: 4.22 us -> 0.8 us
    all_to_all x0 -> x1, blocking collectives: none -> 19.5 us  [shards(): lax.all_to_all(pieces.reshape(32, 32, LANES), ('y', 'x', 'core'), 0, 0, t...]
    ppermute x0 -> x3, starting transfers between devices: none -> 15.8 us  [shards(): planes.append(lax.ppermute(gauge, ('z', 'pb'), pairs))]
    all_to_all x1 -> x0, waiting for transfers between devices: 9.82 us -> none  [shards(): lax.all_to_all(pieces.reshape(32, 32, LANES), ('y', 'x', 'core'), 0, 0, t...]
    all_to_all x1 -> x0, starting transfers between devices: 7.84 us -> none  [shards(): lax.all_to_all(pieces.reshape(32, 32, LANES), ('y', 'x', 'core'), 0, 0, t...]
    all_to_all x2 -> x1, waiting for transfers between devices: 4.42 us -> 0.01 us  [spread(): return lax.all_to_all(value, 'z', 0, 0, tiled=True)]
    all_to_all x2 -> x1, starting transfers between devices: 10 us -> 6.56 us  [spread(): return lax.all_to_all(value, 'z', 0, 0, tiled=True)]
    ppermute x1, starting transfers between devices: 7.6 us -> 5.66 us  [translated(): return lax.ppermute(value, ('y', 'x'), pairs)]
    ppermute x3, waiting for transfers between devices: 7.7 us -> 5.9 us  [shifted(): arrived.append(lax.ppermute(values[shift], 'z', pairs))]
  transfers between devices with their start and end apart: 9 -> 10, of which waited for: 6 -> 4; matrix products, arithmetic and copies ran while one was open for 2% -> 1% of each run, Pallas kernels for 2% -> 0%
where the time goes in v7:
time: 111 us; the launch traced here: 110 us
  starting transfers between devices  46.3 us (42%)
  blocking collectives  41.6 us (37%)
  waiting for transfers between devices  10.9 us (10%)
  Pallas kernels  7.98 us (7%)
  between operations  1.5 us (1%)
    all_to_all x1, blocking collectives, shards(): terms = lax.all_to_all(terms, ('z', 'pb'), 0, 0, tiled=True)  22.1 us
    all_to_all x1, blocking collectives, shards(): lax.all_to_all(pieces.reshape(32, 32, LANES), ('y', 'x', 'core'), 0, 0, t...  19.5 us
    ppermute x3, starting transfers between devices, shards(): planes.append(lax.ppermute(gauge, ('z', 'pb'), pairs))  15.8 us
    ppermute x3, starting transfers between devices, shifted(): arrived.append(lax.ppermute(values[shift], 'z', pairs))  9 us
    all_to_all x1, starting transfers between devices, spread(): return lax.all_to_all(value, 'z', 0, 0, tiled=True)  6.56 us
    ppermute x3, waiting for transfers between devices, shifted(): arrived.append(lax.ppermute(values[shift], 'z', pairs))  5.9 us
    ppermute x1, starting transfers between devices, translated(): return lax.ppermute(value, ('y', 'x'), pairs)  5.66 us
    ppermute x1, starting transfers between devices, shards(): swapped = lax.ppermute(kept, 'core', [(0, 1), (1, 0)])  5.29 us
  transfers between devices with their start and end apart: 10, of which 4 were waited for; matrix products, arithmetic and copies ran while one was open for 1% of the time, Pallas kernels for 0%

profile of v7, /device:TPU:1, one launch (start us, length us, event | category | flops | bytes accessed | tf_op | source)
XLA Modules:
  0.0 109.8 jit_solution(8416225118980852534)
XLA Ops:
  0.0 2.5 %shard_map.109 = (f32[4,2,2,64,128]{4,3,2,1,0:T(8,128)}, bf16[512,256]{1,0:T(8,128)(2,1)S(1)}, bf16[512,256]{1,0:T(8,128)(2,1)S(1)}, f32[264,128]{1,0:T(8,128)S(...) custom-call(f32[2,4,2,64,128]{4,3,2,1,0:T(8,128)} %coupling.1, f32[2,64,128]{2,1,0:T(8,128)} %gauge.1, ...), custom_call_target="tpu_custom_call" | custom-call | flops 134217728 | bytes 1048576 | tf_op jit(solution)/shard_map/pallas_call | solution.py:298
  2.6 6.6 %all-to-all-start = ((f32[4,2,2,64,128]{4,3,2,1,0:T(8,128)}), f32[4,2,2,64,128]{4,3,2,1,0:T(8,128)S(1)}, u32[]{:S(2)}, u32[]{:S(2)}) async-start(f32[4,2,2,64,128]{4,3,2,1,0:T(8,128)} %get-tuple-element.47), calls=%async_computation | async-start | bytes 1048576 | tf_op jit(solution)/shard_map/all_to_all | solution.py:264
  9.1 10.6 %collective-permute-start.15 = (f32[2,64,128]{2,1,0:T(8,128)S(1)}, f32[2,64,128]{2,1,0:T(8,128)S(1)}, u32[]{:S(2)}, u32[]{:S(2)}) collective-permute-start(f32[2,64,128]{2,1,0:T(8,128)S(1)} %copy-done), channel_id=1, source_target_pairs={{128,0},{256,128},{384,256},{1,384},{129,1},{257,129},{385,257},{2... | collective-permute-start | bytes 196616 | tf_op jit(solution)/shard_map/ppermute | solution.py:296
  19.7 2.2 %collective-permute-start.16 = (f32[2,64,128]{2,1,0:T(8,128)S(1)}, f32[2,64,128]{2,1,0:T(8,128)S(1)}, u32[]{:S(2)}, u32[]{:S(2)}) collective-permute-start(f32[2,64,128]{2,1,0:T(8,128)S(1)} %copy-done), channel_id=1, source_target_pairs={{256,0},{384,128},{1,256},{129,384},{257,1},{385,129},{2,257},{130... | collective-permute-start | bytes 196616 | tf_op jit(solution)/shard_map/ppermute | solution.py:296
  21.9 3.1 %collective-permute-start.17 = (f32[2,64,128]{2,1,0:T(8,128)S(1)}, f32[2,64,128]{2,1,0:T(8,128)S(1)}, u32[]{:S(2)}, u32[]{:S(2)}) collective-permute-start(f32[2,64,128]{2,1,0:T(8,128)S(1)} %copy-done), channel_id=1, source_target_pairs={{387,0},{0,128},{128,256},{256,384},{384,1},{1,129},{129,257},{257... | collective-permute-start | bytes 196616 | tf_op jit(solution)/shard_map/ppermute | solution.py:296
  25.0 0.0 copy-start.2
  25.0 0.7 copy-done.2
  25.7 0.7 fusion
  27.7 0.0 collective-permute-done.15
  27.7 0.5 collective-permute-done.17
  28.3 9.0 %conditional.1 = (f32[4,2,64,128]{3,2,1,0:T(8,128)S(1)}) conditional(s32[]{:T(128)} %clamp.3, f32[4,2,64,128]{3,2,1,0:T(8,128)S(1)} %pad_maximum_fusion, f32[4,2,64,128]{3,2,1,0:T(8,128)S(1)} %pad_maximum_fusion, f32[4,2,64,128]{3,2,1,0:T(8,128)S(1)} %pad_maximum_fusion, ...), branch_computations={%region_0.0_spmd, %region_1.0_spmd, %region_2.0_spmd, %region_3.0_... | conditional | bytes 1572912 | solution.py:323
  28.3 5.7 %collective-permute-start.1 = (f32[4,2,64,128]{3,2,1,0:T(8,128)S(1)}, f32[4,2,64,128]{3,2,1,0:T(8,128)S(1)}, u32[]{:S(2)}, u32[]{:S(2)}) collective-permute-start(f32[4,2,64,128]{3,2,1,0:T(8,128)S(1)} %param.2), channel_id=1, source_target_pairs={{16,0},{24,8},{32,16},{40,24},{48,32},{56,40},{0,48},{8,56},{80,64... | collective-permute-start | bytes 786440 | tf_op jit(solution)/shard_map/cond/branch_2_fun/ppermute | solution.py:77
  34.0 3.3 %collective-permute-done.1 = f32[4,2,64,128]{3,2,1,0:T(8,128)S(1)} collective-permute-done((f32[4,2,64,128]{3,2,1,0:T(8,128)S(1)}, f32[4,2,64,128]{3,2,1,0:T(8,128)S(1)}, u32[]{:S(2)}, u32[]{:S(2)}) %collective-permute-start.1) | collective-permute-done | bytes 262176 | tf_op jit(solution)/shard_map/cond/branch_2_fun/ppermute | solution.py:77
  37.3 5.3 %collective-permute-start.18 = (f32[4,2,64,128]{3,2,1,0:T(8,128)S(1)}, f32[4,2,64,128]{3,2,1,0:T(8,128)S(1)}, u32[]{:S(2)}, u32[]{:S(2)}) collective-permute-start(f32[4,2,64,128]{3,2,1,0:T(8,128)S(1)} %get-tuple-element.54.kept), channel_id=1, source_target_pairs={{0,4},{4,0},{1,5},{5,1},{2,6},{6,2},{3,7},{7,3},{8,12},{12,8},{9,1... | collective-permute-start | bytes 786440 | tf_op jit(solution)/shard_map/ppermute | solution.py:324
  42.6 1.1 %collective-permute-done.18.swapped = f32[4,2,64,128]{3,2,1,0:T(8,128)S(1)} collective-permute-done((f32[4,2,64,128]{3,2,1,0:T(8,128)S(1)}, f32[4,2,64,128]{3,2,1,0:T(8,128)S(1)}, u32[]{:S(2)}, u32[]{:S(2)}) %collective-permute-start.18) | collective-permute-done | bytes 262176 | tf_op jit(solution)/shard_map/ppermute | solution.py:324
  43.7 0.0 all-to-all-done.products
  43.7 1.3 %shard_map.110 = f32[1024,128]{1,0:T(8,128)S(1)} custom-call(s32[1]{0:T(128)} %bitcast.target, f32[4,2,64,128]{3,2,1,0:T(8,128)S(1)} %get-tuple-element.54.kept, f32[4,2,64,128]{3,2,1,0:T(8,128)S(1)} %collective-permute-done.18.swapped, f32[4,2,2,64,128]{4,3,2,1,0:T(8,128)S(1)} %all-to-all-done.products), custom_call_target="tpu_custom_call" | custom-call | flops 134217728 | bytes 1048576 | tf_op jit(solution)/shard_map/pallas_call | solution.py:325
  45.1 19.5 %all_to_all.20.columns = f32[32,32,128]{2,1,0:T(8,128)S(1)} all-to-all(f32[32,32,128]{2,1,0:T(8,128)S(1)} %bitcast.11), channel_id=1, replica_groups=mesh['z'=4,'y'=4,'x'=4,'core'=2,'pb'=4] {'y','x','core'}, dimensions={0} | all-to-all | bytes 1048576 | tf_op jit(solution)/shard_map/all_to_all | solution.py:328
  64.6 1.7 %shard_map.111 = f32[32,4,8,128]{3,2,1,0:T(8,128)} custom-call(bf16[512,256]{1,0:T(8,128)(2,1)S(1)} %get-tuple-element.45.high, bf16[512,256]{1,0:T(8,128)(2,1)S(1)} %get-tuple-element.46.low, f32[32,32,128]{2,1,0:T(8,128)S(1)} %all_to_all.20.columns), custom_call_target="tpu_custom_call" | custom-call | flops 268435456 | bytes 1048576 | tf_op jit(solution)/shard_map/pallas_call | solution.py:331
  66.3 3.9 %all-to-all-start.2 = ((f32[32,32,128]{2,1,0:T(8,128)}), f32[32,32,128]{2,1,0:T(8,128)S(1)}, u32[]{:S(2)}, u32[]{:S(2)}) async-start(f32[32,32,128]{2,1,0:T(8,128)} %bitcast.8), calls=%async_computation.2 | async-start | bytes 1048576 | tf_op jit(solution)/shard_map/all_to_all | solution.py:339
  70.2 1.9 %collective-permute-start.19 = (f32[264,128]{1,0:T(8,128)S(1)}, f32[264,128]{1,0:T(8,128)S(1)}, u32[]{:S(2)}, u32[]{:S(2)}) collective-permute-start(f32[264,128]{1,0:T(8,128)S(1)} %get-tuple-element.49), channel_id=1, source_target_pairs={{0,128},{128,256},{256,384},{384,0},{1,129},{129,257},{257,385},{3... | collective-permute-start | bytes 405512 | tf_op jit(solution)/shard_map/ppermute | solution.py:271
  72.2 0.0 copy-start.1
  72.2 3.2 %collective-permute-start.20 = (f32[264,128]{1,0:T(8,128)S(1)}, f32[264,128]{1,0:T(8,128)S(1)}, u32[]{:S(2)}, u32[]{:S(2)}) collective-permute-start(f32[264,128]{1,0:T(8,128)S(1)} %get-tuple-element.50), channel_id=1, source_target_pairs={{0,256},{128,384},{256,0},{384,128},{1,257},{129,385},{257,1},{385... | collective-permute-start | bytes 405512 | tf_op jit(solution)/shard_map/ppermute | solution.py:271
  75.4 3.8 %collective-permute-start.21 = (f32[264,128]{1,0:T(8,128)S(1)}, f32[264,128]{1,0:T(8,128)S(1)}, u32[]{:S(2)}, u32[]{:S(2)}) collective-permute-start(f32[264,128]{1,0:T(8,128)S(1)} %get-tuple-element.51), channel_id=1, source_target_pairs={{0,384},{128,0},{256,128},{384,256},{1,385},{129,1},{257,129},{385... | collective-permute-start | bytes 405512 | tf_op jit(solution)/shard_map/ppermute | solution.py:271
  79.3 0.1 copy.12.frequency
  79.4 0.0 collective-permute-done.19.packs_and_out_1_
  79.4 5.9 %collective-permute-done.20.packs_and_out_2_ = f32[264,128]{1,0:T(8,128)S(1)} collective-permute-done((f32[264,128]{1,0:T(8,128)S(1)}, f32[264,128]{1,0:T(8,128)S(1)}, u32[]{:S(2)}, u32[]{:S(2)}) %collective-permute-start.20) | collective-permute-done | bytes 135200 | tf_op jit(solution)/shard_map/ppermute | solution.py:271
  85.3 0.0 collective-permute-done.21.packs_and_out_3_
  85.3 0.0 all-to-all-done.2
  85.3 1.8 %shard_map.112 = f32[16,1,128]{2,1,0:T(1,128)S(1)} custom-call(f32[4,2]{1,0:T(4,128)S(1)} %copy.12.frequency, f32[1024,128]{1,0:T(8,128)S(1)} %bitcast.10, f32[264,128]{1,0:T(8,128)S(1)} %get-tuple-element.48.packs_and_out_0_, f32[264,128]{1,0:T(8,128)S(1)} %collective-permute-done.19.packs_and_out_1_, ...), custom_call_target="tpu_custom_call" | custom-call | flops 134217728 | bytes 1048576 | tf_op jit(solution)/shard_map/pallas_call | solution.py:342
  87.1 22.1 %all_to_all.21.terms = f32[16,1,128]{2,1,0:T(1,128)S(1)} all-to-all(f32[16,1,128]{2,1,0:T(1,128)S(1)} %shard_map.112), channel_id=1, replica_groups=mesh['z'=4,'y'=4,'x'=4,'core'=2,'pb'=4] {'z','pb'}, dimensions={0} | all-to-all | bytes 16384 | tf_op jit(solution)/shard_map/all_to_all | solution.py:345
  109.1 0.6 shard_map.113
  (6 shorter events, 0.0 us)
Async XLA Ops:
  2.6 6.6 %copy-start = (f32[2,64,128]{2,1,0:T(8,128)S(1)}, f32[2,64,128]{2,1,0:T(8,128)}, u32[]{:S(2)}) copy-start(f32[2,64,128]{2,1,0:T(8,128)} %gauge.1) | copy-start | bytes 196612
  2.6 41.2 %all-to-all-start = ((f32[4,2,2,64,128]{4,3,2,1,0:T(8,128)}), f32[4,2,2,64,128]{4,3,2,1,0:T(8,128)S(1)}, u32[]{:S(2)}, u32[]{:S(2)}) async-start(f32[4,2,2,64,128]{4,3,2,1,0:T(8,128)} %get-tuple-element.47), calls=%async_computation | async-start | bytes 1048576 | tf_op jit(solution)/shard_map/all_to_all | solution.py:264
  9.1 18.6 %collective-permute-start.15 = (f32[2,64,128]{2,1,0:T(8,128)S(1)}, f32[2,64,128]{2,1,0:T(8,128)S(1)}, u32[]{:S(2)}, u32[]{:S(2)}) collective-permute-start(f32[2,64,128]{2,1,0:T(8,128)S(1)} %copy-done), channel_id=1, source_target_pairs={{128,0},{256,128},{384,256},{1,384},{129,1},{257,129},{385,257},{2... | collective-permute-start | bytes 196616 | tf_op jit(solution)/shard_map/ppermute | solution.py:296
  19.7 8.0 %collective-permute-start.16 = (f32[2,64,128]{2,1,0:T(8,128)S(1)}, f32[2,64,128]{2,1,0:T(8,128)S(1)}, u32[]{:S(2)}, u32[]{:S(2)}) collective-permute-start(f32[2,64,128]{2,1,0:T(8,128)S(1)} %copy-done), channel_id=1, source_target_pairs={{256,0},{384,128},{1,256},{129,384},{257,1},{385,129},{2,257},{130... | collective-permute-start | bytes 196616 | tf_op jit(solution)/shard_map/ppermute | solution.py:296
  21.9 6.4 %collective-permute-start.17 = (f32[2,64,128]{2,1,0:T(8,128)S(1)}, f32[2,64,128]{2,1,0:T(8,128)S(1)}, u32[]{:S(2)}, u32[]{:S(2)}) collective-permute-start(f32[2,64,128]{2,1,0:T(8,128)S(1)} %copy-done), channel_id=1, source_target_pairs={{387,0},{0,128},{128,256},{256,384},{384,1},{1,129},{129,257},{257... | collective-permute-start | bytes 196616 | tf_op jit(solution)/shard_map/ppermute | solution.py:296
  25.0 0.7 copy-start.2
  28.3 9.0 %collective-permute-start.1 = (f32[4,2,64,128]{3,2,1,0:T(8,128)S(1)}, f32[4,2,64,128]{3,2,1,0:T(8,128)S(1)}, u32[]{:S(2)}, u32[]{:S(2)}) collective-permute-start(f32[4,2,64,128]{3,2,1,0:T(8,128)S(1)} %param.2), channel_id=1, source_target_pairs={{16,0},{24,8},{32,16},{40,24},{48,32},{56,40},{0,48},{8,56},{80,64... | collective-permute-start | bytes 786440 | tf_op jit(solution)/shard_map/cond/branch_2_fun/ppermute | solution.py:77
  37.3 6.4 %collective-permute-start.18 = (f32[4,2,64,128]{3,2,1,0:T(8,128)S(1)}, f32[4,2,64,128]{3,2,1,0:T(8,128)S(1)}, u32[]{:S(2)}, u32[]{:S(2)}) collective-permute-start(f32[4,2,64,128]{3,2,1,0:T(8,128)S(1)} %get-tuple-element.54.kept), channel_id=1, source_target_pairs={{0,4},{4,0},{1,5},{5,1},{2,6},{6,2},{3,7},{7,3},{8,12},{12,8},{9,1... | collective-permute-start | bytes 786440 | tf_op jit(solution)/shard_map/ppermute | solution.py:324
  66.3 19.0 %all-to-all-start.2 = ((f32[32,32,128]{2,1,0:T(8,128)}), f32[32,32,128]{2,1,0:T(8,128)S(1)}, u32[]{:S(2)}, u32[]{:S(2)}) async-start(f32[32,32,128]{2,1,0:T(8,128)} %bitcast.8), calls=%async_computation.2 | async-start | bytes 1048576 | tf_op jit(solution)/shard_map/all_to_all | solution.py:339
  70.2 9.1 %collective-permute-start.19 = (f32[264,128]{1,0:T(8,128)S(1)}, f32[264,128]{1,0:T(8,128)S(1)}, u32[]{:S(2)}, u32[]{:S(2)}) collective-permute-start(f32[264,128]{1,0:T(8,128)S(1)} %get-tuple-element.49), channel_id=1, source_target_pairs={{0,128},{128,256},{256,384},{384,0},{1,129},{129,257},{257,385},{3... | collective-permute-start | bytes 405512 | tf_op jit(solution)/shard_map/ppermute | solution.py:271
  72.2 7.1 %copy-start.1 = (f32[4,2]{0,1:T(2,128)S(1)}, f32[4,2]{0,1:T(2,128)}, u32[]{:S(2)}) copy-start(f32[4,2]{0,1:T(2,128)} %param.36) | copy-start | bytes 100
  72.2 13.1 %collective-permute-start.20 = (f32[264,128]{1,0:T(8,128)S(1)}, f32[264,128]{1,0:T(8,128)S(1)}, u32[]{:S(2)}, u32[]{:S(2)}) collective-permute-start(f32[264,128]{1,0:T(8,128)S(1)} %get-tuple-element.50), channel_id=1, source_target_pairs={{0,256},{128,384},{256,0},{384,128},{1,257},{129,385},{257,1},{385... | collective-permute-start | bytes 405512 | tf_op jit(solution)/shard_map/ppermute | solution.py:271
  75.4 9.9 %collective-permute-start.21 = (f32[264,128]{1,0:T(8,128)S(1)}, f32[264,128]{1,0:T(8,128)S(1)}, u32[]{:S(2)}, u32[]{:S(2)}) collective-permute-start(f32[264,128]{1,0:T(8,128)S(1)} %get-tuple-element.51), channel_id=1, source_target_pairs={{0,384},{128,0},{256,128},{384,256},{1,385},{129,1},{257,129},{385... | collective-permute-start | bytes 405512 | tf_op jit(solution)/shard_map/ppermute | solution.py:271

commit v8 on v6

--- a/solution.py
+++ b/solution.py
@@ -50,12 +50,12 @@
     return jnp.where(lane < W, first, -first)
 
 
-def apply_left(left, right_pair):
-    both = product(halves(left), halves(right_pair), (0, 0))
+def apply_left(left, right):
+    both = product(halves(left), halves(right), (0, 0))
     sign = signs(1.0)
     return [
         both[:W, at : at + LANES] + sign * pltpu.roll(both[W:, at : at + LANES], W, 1)
-        for at in (0, LANES)
+        for at in range(0, right.shape[1], LANES)
     ]
 
 
@@ -81,9 +81,9 @@
     for k in range(2):
         block = right_block(gauge[k])
         rows = coupling[k].reshape(-1, LANES)
-        result = product(halves(rows), block, (1, 0)).reshape(4, 2, W, LANES)
-        for q in range(4):
-            out[q, k] = result[q]
+        result = product(halves(rows), block, (1, 0)).reshape(8, W, LANES)
+        for column in range(8):
+            out[column, k] = result[column]
 
 
 def pack_kernel(position, eig_left, eig_right, energy_k, energy_kq, occupied, *outs):
@@ -104,19 +104,18 @@
     first = (target >> 5) - 2 * position[0] - (position[1] >> 1)
     carry = ((position[1] >> 1) + (first & 7)) >> 1
     wanniers = []
-    for l in range(2):
-        third = (target + l) & 3
+    for place in range(4):
+        third = (target - 2 * core + place) & 3
         mine = (third >> 1) == core
         for z in range(4):
             plane = (z + carry) & 3
             gauge = jnp.where(mine, kept[plane, third & 1], swapped[plane, third & 1])
-            pair = jnp.concatenate([products[z, l, 0], products[z, l, 1]], -1)
-            wanniers.append((l, z, apply_left(gauge, pair)))
-    for l, z, both in wanniers:
-        for b, wannier in enumerate(both):
-            for part in range(2):
-                start = (part * 2 + b) * 8 + z * 2 + l
-                out[pl.ds(start, 32, stride=32), :] = wannier[part * 32 : part * 32 + 32]
+            wannier = apply_left(gauge, products[z * 2 + place // 2, place % 2])[0]
+            wanniers.append((z * 4 + place, wannier))
+    for start, wannier in wanniers:
+        for part in range(4):
+            rows = wannier[part * 16 : part * 16 + 16]
+            out[pl.ds(part * 16 + start, 16, stride=64), :] = rows
 
 
 def phase_kernel(coords, tables, high, low):
@@ -146,7 +145,7 @@
 
 
 def fourier_kernel(high, low, columns, out):
-    parts = [columns[:, at : at + 8, :].reshape(NK, LANES) for at in (0, 8)]
+    parts = [columns[:, at : at + 16, :].reshape(NK, LANES) for at in (0, 16)]
     result = product((high[...], low[...]), halves(jnp.concatenate(parts, -1)), (1, 0))
     sign = signs(-1.0)
     for c in range(2):
@@ -170,9 +169,9 @@
         plane = (position[0] - shift + 4) & 3
         for f in range(2):
             rows = [
-                arrived[pl.ds((part * 2 + b) * 8 + plane * 2 + f, 32, stride=32), :]
+                arrived[pl.ds(b * 32 + part * 8 + plane * 2 + f, 16, stride=64), :]
                 for b in range(2)
-                for part in range(2)
+                for part in range(4)
             ]
             eig_right = pack[LANES + f * W : LANES + f * W + W]
             half = product(halves(jnp.concatenate(rows, 0)), right_block(eig_right), (1, 0))
@@ -213,9 +212,9 @@
 
 def phase_tables():
     column = np.arange(NK)
-    source, z, l = column // 8, column // 2 % 4, column % 2
-    y, x, core = source // 8, source // 2 % 4, source % 2
-    coordinates = (2 * z + y // 2, (y % 2) * 4 + x, 2 * core + l)
+    source, z, place = column // 16, column // 4 % 4, column % 4
+    y, x = source // 4, source % 4
+    coordinates = (2 * z + y // 2, (y % 2) * 4 + x, place)
     tables = np.zeros((3, 2, FG, NK), np.float64)
     for axis, (size, where) in enumerate(zip((8, 8, 4), coordinates)):
         steps = np.arange(FG)[:, None] - (FG // size) * where[None, :]
@@ -246,8 +245,8 @@
     return jax.ShapeDtypeStruct(shape, jnp.float32)
 
 
-def spread(value):
-    return lax.all_to_all(value, "z", 0, 0, tiled=True)
+def spread(value, axes):
+    return lax.all_to_all(value, axes, 0, 0, tiled=True)
 
 
 def shifted(values):
@@ -276,9 +275,11 @@
         (((target >> 5) - (along_y >> 1)) & 1) << 3
     )
     position = jnp.stack([along_z, along_y, along_x, core, target, number])
-    planes = spread(jnp.broadcast_to(gauge[None], (4, 2, W, LANES)))
-    products = call(right_kernel, f32(4, 2, 2, W, LANES), [VMEM, VMEM], 1 << 27)(coupling, gauge)
-    products = spread(products)
+    planes = spread(jnp.broadcast_to(gauge[None], (4, 2, W, LANES)), "z")
+    products = call(right_kernel, f32(8, 2, W, LANES), [VMEM, VMEM], 1 << 27)(
+        coupling, gauge
+    )
+    products = spread(products, ("z", "core"))
     packs = call(pack_kernel, [f32(264, LANES)] * 4, [SMEM] + [VMEM] * 5, 1 << 20)(
         position, eig_left, eig_right, energy_k, energy_kq, occupied
     )
@@ -288,7 +289,9 @@
     pieces = call(left_kernel, f32(1024, LANES), [SMEM] + [VMEM] * 3, 1 << 27)(
         position, kept, swapped, products
     )
-    columns = lax.all_to_all(pieces.reshape(32, 32, LANES), ("y", "x", "core"), 0, 0, tiled=True)
+    columns = lax.all_to_all(
+        pieces.reshape(16, 64, LANES), ("y", "x"), 0, 0, tiled=True
+    )
     packs = shifted(packs)
     coords = fine_coords.reshape(3, 4, 32, 2).transpose(0, 2, 1, 3).reshape(3, NK)
     high, low = call(
@@ -301,7 +304,7 @@
     fine = call(
         fourier_kernel,
         f32(32, 4, 8, LANES),
-        [fixed, fixed, pl.BlockSpec((32, 16, LANES), lambda i: (0, i, 0))],
+        [fixed, fixed, pl.BlockSpec((16, 32, LANES), lambda i: (0, i, 0))],
         1 << 28,
         grid=(2,),
         out_specs=pl.BlockSpec((32, 2, 8, LANES), lambda i: (0, i, 0, 0)),

time: 110 us -> 112 us (1.018)
  waiting for transfers between devices: 25.7 us -> 28 us
    all_to_all x3, starting transfers between devices: 17.9 us -> 22 us  [the longest x2 14.9 us: spread(): return lax.all_to_all(value, axes, 0, 0, tiled=True)]
    ppermute x1, waiting for transfers between devices: 3.29 us -> 6.24 us  [translated(): return lax.ppermute(value, ('y', 'x'), pairs)]
    ppermute x1, starting transfers between devices: 5.7 us -> 2.85 us  [shards(): swapped = lax.ppermute(kept, 'core', [(0, 1), (1, 0)])]
    ppermute x1, starting transfers between devices: 7.6 us -> 4.93 us  [translated(): return lax.ppermute(value, ('y', 'x'), pairs)]
    all_to_all x1, starting transfers between devices: 4.08 us -> 5.44 us  [shards(): lax.all_to_all(fine.reshape(32, 32, LANES), ('y', 'x', 'core'), 0, 0, til...]
where the time goes in v8:
time: 112 us; the launch traced here: 110 us
  starting transfers between devices  44.9 us (40%)
  waiting for transfers between devices  28 us (25%)
  blocking collectives  22.3 us (20%)
  Pallas kernels  8.51 us (8%)
  local copies, waits for them, and re-layouts  4.22 us (4%)
  between operations  1.46 us (1%)
    all_to_all x1, blocking collectives, shards(): terms = lax.all_to_all(terms, ('z', 'pb'), 0, 0, tiled=True)  22.3 us
    all_to_all x2, starting transfers between devices, spread(): return lax.all_to_all(value, axes, 0, 0, tiled=True)  14.9 us
    ppermute x3, starting transfers between devices, shifted(): arrived.append(lax.ppermute(values[shift], 'z', pairs))  9.68 us
    all_to_all x1, waiting for transfers between devices, shards(): lax.all_to_all(pieces.reshape(16, 64, LANES), ('y', 'x'), 0, 0, tiled=True)  9.13 us
    ppermute x3, waiting for transfers between devices, shifted(): arrived.append(lax.ppermute(values[shift], 'z', pairs))  7.7 us
    all_to_all x1, starting transfers between devices, shards(): lax.all_to_all(pieces.reshape(16, 64, LANES), ('y', 'x'), 0, 0, tiled=True)  7.06 us
    ppermute x1, waiting for transfers between devices, translated(): return lax.ppermute(value, ('y', 'x'), pairs)  6.24 us
    all_to_all x1, starting transfers between devices, shards(): lax.all_to_all(fine.reshape(32, 32, LANES), ('y', 'x', 'core'), 0, 0, til...  5.44 us
  transfers between devices with their start and end apart: 9, of which 6 were waited for; matrix products, arithmetic and copies ran while one was open for 2% of the time, Pallas kernels for 2%

profile of v8, /device:TPU:1, one launch (start us, length us, event | category | flops | bytes accessed | tf_op | source)
XLA Modules:
  0.0 110.0 jit_solution(11365503976572383695)
XLA Ops:
  0.0 1.6 %broadcast_in_dim.2 = f32[4,2,64,128]{3,2,1,0:T(8,128)} broadcast(f32[2,64,128]{2,1,0:T(8,128)} %gauge.1), dimensions={1,2,3} | broadcast | bytes 327680 | tf_op jit(solution)/shard_map/broadcast_in_dim | solution.py:278
  1.6 6.6 %all-to-all-start = ((f32[4,2,64,128]{3,2,1,0:T(8,128)}), f32[4,2,64,128]{3,2,1,0:T(8,128)S(1)}, u32[]{:S(2)}, u32[]{:S(2)}) async-start(f32[4,2,64,128]{3,2,1,0:T(8,128)} %broadcast_in_dim.2), calls=%async_computation | async-start | bytes 524288 | tf_op jit(solution)/shard_map/all_to_all | solution.py:249
  8.2 1.2 %shard_map.110 = f32[8,2,64,128]{3,2,1,0:T(8,128)} custom-call(f32[2,4,2,64,128]{4,3,2,1,0:T(8,128)S(1)} %copy-done, f32[2,64,128]{2,1,0:T(8,128)S(1)} %copy-done.1), custom_call_target="tpu_custom_call" | custom-call | flops 134217728 | bytes 1048576 | tf_op jit(solution)/shard_map/pallas_call | solution.py:279
  9.4 4.4 %all-to-all-done = f32[4,2,64,128]{3,2,1,0:T(8,128)S(1)} async-done(((f32[4,2,64,128]{3,2,1,0:T(8,128)}), f32[4,2,64,128]{3,2,1,0:T(8,128)S(1)}, u32[]{:S(2)}, u32[]{:S(2)}) %all-to-all-start) | async-done | bytes 262176 | tf_op jit(solution)/shard_map/all_to_all | solution.py:249
  13.8 8.4 %all-to-all-start.1 = ((f32[8,2,64,128]{3,2,1,0:T(8,128)}), f32[8,2,64,128]{3,2,1,0:T(8,128)S(1)}, u32[]{:S(2)}, u32[]{:S(2)}) async-start(f32[8,2,64,128]{3,2,1,0:T(8,128)} %shard_map.110), calls=%async_computation.1 | async-start | bytes 1048576 | tf_op jit(solution)/shard_map/all_to_all | solution.py:249
  22.2 0.7 copy-done.10
  22.9 0.7 fusion
  24.8 11.2 %conditional.1 = (f32[4,2,64,128]{3,2,1,0:T(8,128)S(1)}) conditional(s32[]{:T(128)} %clamp.3, f32[4,2,64,128]{3,2,1,0:T(8,128)S(1)} %all-to-all-done, f32[4,2,64,128]{3,2,1,0:T(8,128)S(1)} %all-to-all-done, f32[4,2,64,128]{3,2,1,0:T(8,128)S(1)} %all-to-all-done, f32[4,2,64,128]{3,2,1,0:T(8,128)S(1)} %all-to-all-done, ...), branch_computations={%region_0.0_spmd, %region_1.0_spmd, %region_2.0_spmd, %region_3.0_... | conditional | bytes 1572912 | solution.py:287
  24.8 4.9 %collective-permute-start.1 = (f32[4,2,64,128]{3,2,1,0:T(8,128)S(1)}, f32[4,2,64,128]{3,2,1,0:T(8,128)S(1)}, u32[]{:S(2)}, u32[]{:S(2)}) collective-permute-start(f32[4,2,64,128]{3,2,1,0:T(8,128)S(1)} %param.2), channel_id=1, source_target_pairs={{16,0},{24,8},{32,16},{40,24},{48,32},{56,40},{0,48},{8,56},{80,64... | collective-permute-start | bytes 786440 | tf_op jit(solution)/shard_map/cond/branch_2_fun/ppermute | solution.py:77
  29.8 6.2 %collective-permute-done.1 = f32[4,2,64,128]{3,2,1,0:T(8,128)S(1)} collective-permute-done((f32[4,2,64,128]{3,2,1,0:T(8,128)S(1)}, f32[4,2,64,128]{3,2,1,0:T(8,128)S(1)}, u32[]{:S(2)}, u32[]{:S(2)}) %collective-permute-start.1) | collective-permute-done | bytes 262176 | tf_op jit(solution)/shard_map/cond/branch_2_fun/ppermute | solution.py:77
  36.1 2.9 %collective-permute-start.15 = (f32[4,2,64,128]{3,2,1,0:T(8,128)S(1)}, f32[4,2,64,128]{3,2,1,0:T(8,128)S(1)}, u32[]{:S(2)}, u32[]{:S(2)}) collective-permute-start(f32[4,2,64,128]{3,2,1,0:T(8,128)S(1)} %get-tuple-element.52.kept), channel_id=1, source_target_pairs={{0,4},{4,0},{1,5},{5,1},{2,6},{6,2},{3,7},{7,3},{8,12},{12,8},{9,1... | collective-permute-start | bytes 786440 | tf_op jit(solution)/shard_map/ppermute | solution.py:288
  38.9 0.6 stack.23.position
  39.6 0.5 collective-permute-done.15.swapped
  40.1 2.2 %shard_map.111 = f32[1024,128]{1,0:T(8,128)} custom-call(s32[6]{0:T(128)S(1)} %stack.23.position, f32[4,2,64,128]{3,2,1,0:T(8,128)S(1)} %get-tuple-element.52.kept, f32[4,2,64,128]{3,2,1,0:T(8,128)S(1)} %collective-permute-done.15.swapped, f32[8,2,64,128]{3,2,1,0:T(8,128)S(1)} %all-to-all-done.1.products), custom_call_target="tpu_custom_call" | custom-call | flops 134217728 | bytes 1048576 | tf_op jit(solution)/shard_map/pallas_call | solution.py:289
  42.2 7.1 %all-to-all-start.2 = ((f32[16,64,128]{2,1,0:T(8,128)}), f32[16,64,128]{2,1,0:T(8,128)S(1)}, u32[]{:S(2)}, u32[]{:S(2)}) async-start(f32[16,64,128]{2,1,0:T(8,128)} %bitcast.9), calls=%async_computation.2 | async-start | bytes 1048576 | tf_op jit(solution)/shard_map/all_to_all | solution.py:292
  49.3 0.2 reshape.20
  49.5 0.1 copy.14
  49.6 0.2 reshape.21.coords
  49.8 0.6 copy-done.7
  50.4 0.4 shard_map.109
  50.9 9.1 %all-to-all-done.2.columns = f32[16,64,128]{2,1,0:T(8,128)S(1)} async-done(((f32[16,64,128]{2,1,0:T(8,128)}), f32[16,64,128]{2,1,0:T(8,128)S(1)}, u32[]{:S(2)}, u32[]{:S(2)}) %all-to-all-start.2) | async-done | bytes 524320 | tf_op jit(solution)/shard_map/all_to_all | solution.py:292
  60.0 1.7 %shard_map.112 = f32[32,4,8,128]{3,2,1,0:T(8,128)} custom-call(bf16[512,256]{1,0:T(8,128)(2,1)S(1)} %get-tuple-element.44.high, bf16[512,256]{1,0:T(8,128)(2,1)S(1)} %get-tuple-element.45.low, f32[16,64,128]{2,1,0:T(8,128)S(1)} %all-to-all-done.2.columns), custom_call_target="tpu_custom_call" | custom-call | flops 268435456 | bytes 1048576 | tf_op jit(solution)/shard_map/pallas_call | solution.py:304
  61.7 5.4 %all-to-all-start.3 = ((f32[32,32,128]{2,1,0:T(8,128)}), f32[32,32,128]{2,1,0:T(8,128)S(1)}, u32[]{:S(2)}, u32[]{:S(2)}) async-start(f32[32,32,128]{2,1,0:T(8,128)} %bitcast.10), calls=%async_computation.3 | async-start | bytes 1048576 | tf_op jit(solution)/shard_map/all_to_all | solution.py:312
  67.2 0.6 shard_map.113
  67.9 2.7 %collective-permute-start.16 = (f32[264,128]{1,0:T(8,128)S(1)}, f32[264,128]{1,0:T(8,128)S(1)}, u32[]{:S(2)}, u32[]{:S(2)}) collective-permute-start(f32[264,128]{1,0:T(8,128)S(1)} %get-tuple-element.47), channel_id=1, source_target_pairs={{0,128},{128,256},{256,384},{384,0},{1,129},{129,257},{257,385},{3... | collective-permute-start | bytes 405512 | tf_op jit(solution)/shard_map/ppermute | solution.py:256
  70.6 5.0 %collective-permute-start.17 = (f32[264,128]{1,0:T(8,128)S(1)}, f32[264,128]{1,0:T(8,128)S(1)}, u32[]{:S(2)}, u32[]{:S(2)}) collective-permute-start(f32[264,128]{1,0:T(8,128)S(1)} %get-tuple-element.48), channel_id=1, source_target_pairs={{0,256},{128,384},{256,0},{384,128},{1,257},{129,385},{257,1},{385... | collective-permute-start | bytes 405512 | tf_op jit(solution)/shard_map/ppermute | solution.py:256
  75.6 1.9 %collective-permute-start.18 = (f32[264,128]{1,0:T(8,128)S(1)}, f32[264,128]{1,0:T(8,128)S(1)}, u32[]{:S(2)}, u32[]{:S(2)}) collective-permute-start(f32[264,128]{1,0:T(8,128)S(1)} %get-tuple-element.49), channel_id=1, source_target_pairs={{0,384},{128,0},{256,128},{384,256},{1,385},{129,1},{257,129},{385... | collective-permute-start | bytes 405512 | tf_op jit(solution)/shard_map/ppermute | solution.py:256
  77.7 5.6 %collective-permute-done.17.packs_and_out_2_ = f32[264,128]{1,0:T(8,128)S(1)} collective-permute-done((f32[264,128]{1,0:T(8,128)S(1)}, f32[264,128]{1,0:T(8,128)S(1)}, u32[]{:S(2)}, u32[]{:S(2)}) %collective-permute-start.17) | collective-permute-done | bytes 135200 | tf_op jit(solution)/shard_map/ppermute | solution.py:256
  83.3 2.1 %collective-permute-done.18.packs_and_out_3_ = f32[264,128]{1,0:T(8,128)S(1)} collective-permute-done((f32[264,128]{1,0:T(8,128)S(1)}, f32[264,128]{1,0:T(8,128)S(1)}, u32[]{:S(2)}, u32[]{:S(2)}) %collective-permute-start.18) | collective-permute-done | bytes 135200 | tf_op jit(solution)/shard_map/ppermute | solution.py:256
  85.4 1.8 %shard_map.114 = f32[16,1,128]{2,1,0:T(1,128)S(1)} custom-call(s32[6]{0:T(128)S(1)} %stack.23.position, f32[4,2]{1,0:T(4,128)S(1)} %copy.15.frequency, f32[1024,128]{1,0:T(8,128)S(1)} %bitcast.12, f32[264,128]{1,0:T(8,128)S(1)} %get-tuple-element.46.packs_and_out_0_, f32[264,128]{1,0:T(8,128)S(1)} %collective-permute-done.16.packs_and_out_1_, ...), custom_call_target="tpu_custom_call" | custom-call | flops 134217728 | bytes 1048576 | tf_op jit(solution)/shard_map/pallas_call | solution.py:315
  87.1 22.3 %all_to_all.73.terms = f32[16,1,128]{2,1,0:T(1,128)S(1)} all-to-all(f32[16,1,128]{2,1,0:T(1,128)S(1)} %shard_map.114), channel_id=1, replica_groups=mesh['z'=4,'y'=4,'x'=4,'core'=2,'pb'=4] {'z','pb'}, dimensions={0} | all-to-all | bytes 16384 | tf_op jit(solution)/shard_map/all_to_all | solution.py:318
  109.4 0.6 shard_map.115
  (25 shorter events, 0.2 us)
Async XLA Ops:
  0.0 8.2 %copy-start = (f32[2,4,2,64,128]{4,3,2,1,0:T(8,128)S(1)}, f32[2,4,2,64,128]{4,3,2,1,0:T(8,128)}, u32[]{:S(2)}) copy-start(f32[2,4,2,64,128]{4,3,2,1,0:T(8,128)} %coupling.1) | copy-start | bytes 1572868
  1.6 6.6 %copy-start.1 = (f32[2,64,128]{2,1,0:T(8,128)S(1)}, f32[2,64,128]{2,1,0:T(8,128)}, u32[]{:S(2)}) copy-start(f32[2,64,128]{2,1,0:T(8,128)} %gauge.1) | copy-start | bytes 196612
  1.6 12.2 %all-to-all-start = ((f32[4,2,64,128]{3,2,1,0:T(8,128)}), f32[4,2,64,128]{3,2,1,0:T(8,128)S(1)}, u32[]{:S(2)}, u32[]{:S(2)}) async-start(f32[4,2,64,128]{3,2,1,0:T(8,128)} %broadcast_in_dim.2), calls=%async_computation | async-start | bytes 524288 | tf_op jit(solution)/shard_map/all_to_all | solution.py:249
  13.8 26.2 %all-to-all-start.1 = ((f32[8,2,64,128]{3,2,1,0:T(8,128)}), f32[8,2,64,128]{3,2,1,0:T(8,128)S(1)}, u32[]{:S(2)}, u32[]{:S(2)}) async-start(f32[8,2,64,128]{3,2,1,0:T(8,128)} %shard_map.110), calls=%async_computation.1 | async-start | bytes 1048576 | tf_op jit(solution)/shard_map/all_to_all | solution.py:249
  22.2 0.7 copy-start.10
  24.8 11.2 %collective-permute-start.1 = (f32[4,2,64,128]{3,2,1,0:T(8,128)S(1)}, f32[4,2,64,128]{3,2,1,0:T(8,128)S(1)}, u32[]{:S(2)}, u32[]{:S(2)}) collective-permute-start(f32[4,2,64,128]{3,2,1,0:T(8,128)S(1)} %param.2), channel_id=1, source_target_pairs={{16,0},{24,8},{32,16},{40,24},{48,32},{56,40},{0,48},{8,56},{80,64... | collective-permute-start | bytes 786440 | tf_op jit(solution)/shard_map/cond/branch_2_fun/ppermute | solution.py:77
  36.1 4.0 %collective-permute-start.15 = (f32[4,2,64,128]{3,2,1,0:T(8,128)S(1)}, f32[4,2,64,128]{3,2,1,0:T(8,128)S(1)}, u32[]{:S(2)}, u32[]{:S(2)}) collective-permute-start(f32[4,2,64,128]{3,2,1,0:T(8,128)S(1)} %get-tuple-element.52.kept), channel_id=1, source_target_pairs={{0,4},{4,0},{1,5},{5,1},{2,6},{6,2},{3,7},{7,3},{8,12},{12,8},{9,1... | collective-permute-start | bytes 786440 | tf_op jit(solution)/shard_map/ppermute | solution.py:288
  42.2 7.1 %copy-start.8 = (s32[3,256]{1,0:T(4,128)S(1)}, s32[3,256]{1,0:T(4,128)}, u32[]{:S(2)}) copy-start(s32[3,256]{1,0:T(4,128)} %param.30) | copy-start | bytes 9220
  42.2 17.8 %all-to-all-start.2 = ((f32[16,64,128]{2,1,0:T(8,128)}), f32[16,64,128]{2,1,0:T(8,128)S(1)}, u32[]{:S(2)}, u32[]{:S(2)}) async-start(f32[16,64,128]{2,1,0:T(8,128)} %bitcast.9), calls=%async_computation.2 | async-start | bytes 1048576 | tf_op jit(solution)/shard_map/all_to_all | solution.py:292
  49.5 1.0 copy-start.7
  61.7 5.5 %copy-start.2 = (f32[2,4,64,128]{3,2,1,0:T(8,128)S(1)}, f32[2,4,64,128]{3,2,1,0:T(8,128)}, u32[]{:S(2)}) copy-start(f32[2,4,64,128]{3,2,1,0:T(8,128)} %eig_left.1) | copy-start | bytes 786436
  61.7 5.5 %copy-start.3 = (f32[2,64,128]{2,1,0:T(8,128)S(1)}, f32[2,64,128]{2,1,0:T(8,128)}, u32[]{:S(2)}) copy-start(f32[2,64,128]{2,1,0:T(8,128)} %eig_right.1) | copy-start | bytes 196612
  61.7 5.5 %copy-start.4 = (f32[2,4,64]{2,1,0:T(4,128)S(1)}, f32[2,4,64]{2,1,0:T(4,128)}, u32[]{:S(2)}) copy-start(f32[2,4,64]{2,1,0:T(4,128)} %energy_kq.1) | copy-start | bytes 6148
  61.7 5.5 %copy-start.5 = (s32[2,4,64]{2,1,0:T(4,128)S(1)}, s32[2,4,64]{2,1,0:T(4,128)}, u32[]{:S(2)}) copy-start(s32[2,4,64]{2,1,0:T(4,128)} %occupied.1) | copy-start | bytes 6148
  61.7 5.5 %copy-start.6 = (f32[2,64]{1,0:T(2,128)S(1)}, f32[2,64]{1,0:T(2,128)}, u32[]{:S(2)}) copy-start(f32[2,64]{1,0:T(2,128)} %energy_k.1) | copy-start | bytes 1540
  61.7 23.7 %all-to-all-start.3 = ((f32[32,32,128]{2,1,0:T(8,128)}), f32[32,32,128]{2,1,0:T(8,128)S(1)}, u32[]{:S(2)}, u32[]{:S(2)}) async-start(f32[32,32,128]{2,1,0:T(8,128)} %bitcast.10), calls=%async_computation.3 | async-start | bytes 1048576 | tf_op jit(solution)/shard_map/all_to_all | solution.py:312
  67.9 9.8 %collective-permute-start.16 = (f32[264,128]{1,0:T(8,128)S(1)}, f32[264,128]{1,0:T(8,128)S(1)}, u32[]{:S(2)}, u32[]{:S(2)}) collective-permute-start(f32[264,128]{1,0:T(8,128)S(1)} %get-tuple-element.47), channel_id=1, source_target_pairs={{0,128},{128,256},{256,384},{384,0},{1,129},{129,257},{257,385},{3... | collective-permute-start | bytes 405512 | tf_op jit(solution)/shard_map/ppermute | solution.py:256
  70.6 7.0 %copy-start.9 = (f32[4,2]{0,1:T(2,128)S(1)}, f32[4,2]{0,1:T(2,128)}, u32[]{:S(2)}) copy-start(f32[4,2]{0,1:T(2,128)} %param.36) | copy-start | bytes 100
  70.6 12.7 %collective-permute-start.17 = (f32[264,128]{1,0:T(8,128)S(1)}, f32[264,128]{1,0:T(8,128)S(1)}, u32[]{:S(2)}, u32[]{:S(2)}) collective-permute-start(f32[264,128]{1,0:T(8,128)S(1)} %get-tuple-element.48), channel_id=1, source_target_pairs={{0,256},{128,384},{256,0},{384,128},{1,257},{129,385},{257,1},{385... | collective-permute-start | bytes 405512 | tf_op jit(solution)/shard_map/ppermute | solution.py:256
  75.6 9.7 %collective-permute-start.18 = (f32[264,128]{1,0:T(8,128)S(1)}, f32[264,128]{1,0:T(8,128)S(1)}, u32[]{:S(2)}, u32[]{:S(2)}) collective-permute-start(f32[264,128]{1,0:T(8,128)S(1)} %get-tuple-element.49), channel_id=1, source_target_pairs={{0,384},{128,0},{256,128},{384,256},{1,385},{129,1},{257,129},{385... | collective-permute-start | bytes 405512 | tf_op jit(solution)/shard_map/ppermute | solution.py:256

commit v9 on v7

--- a/solution.py
+++ b/solution.py
@@ -77,20 +77,25 @@
     return lax.ppermute(value, ("y", "x"), pairs)
 
 
-def prepare_kernel(
-    coupling, gauge, coords, tables, eig_left, eig_right, energy_k, energy_kq, occupied, *outs
-):
-    right_part(coupling, gauge, outs[0])
-    pack_part(eig_left, eig_right, energy_k, energy_kq, occupied, outs[3:])
-    phase_part(coords, tables, outs[1], outs[2])
-
-
-def right_part(coupling, gauge, out):
+def right_kernel(coupling, gauge, kq, out, number, target):
+    along_z, along_y, along_x, pb = (lax.axis_index(name) for name in ("z", "y", "x", "pb"))
+    point = kq[0, pb * 4 + along_z]
+    target[0] = point
+    number[0] = (((point >> 2) - (along_y * 4 + along_x)) & 7) + (
+        (((point >> 5) - (along_y >> 1)) & 1) << 3
+    )
     for k in range(2):
         rows = coupling[k].reshape(-1, LANES)
         result = product(halves(rows), right_block(gauge[k]), (1, 0)).reshape(4, 2, W, LANES)
         for q in range(4):
             out[q, k] = result[q]
+
+
+def owners_kernel(
+    coords, tables, eig_left, eig_right, energy_k, energy_kq, occupied, high, low, *outs
+):
+    pack_part(eig_left, eig_right, energy_k, energy_kq, occupied, outs)
+    phase_part(coords, tables, high, low)
 
 
 def pack_part(eig_left, eig_right, energy_k, energy_kq, occupied, outs):
@@ -264,6 +269,10 @@
     return lax.all_to_all(value, "z", 0, 0, tiled=True)
 
 
+def in_hbm(value):
+    return pltpu.with_memory_space_constraint(value, pltpu.HBM)
+
+
 def shifted(values):
     arrived = [values[0]]
     for shift in (1, 2, 3):
@@ -284,30 +293,33 @@
     occupied,
     frequency,
 ):
-    along_z, along_y, along_x, _ = (lax.axis_index(name) for name in KA)
-    target = kq_index[lax.axis_index("pb") * 4 + along_z, 0]
-    number = (((target >> 2) - (along_y * 4 + along_x)) & 7) + (
-        (((target >> 5) - (along_y >> 1)) & 1) << 3
-    )
+    along_z, along_y, along_x, core = (lax.axis_index(name) for name in KA)
     planes = [gauge]
     for ahead in (1, 2, 15):
         ring = [place % 4 * 4 + place // 4 for place in range(16)]
         pairs = [(ring[(place + ahead) % 16], ring[place]) for place in range(16)]
         planes.append(lax.ppermute(gauge, ("z", "pb"), pairs))
     planes = jnp.stack(planes)
-    products, high, low, *packs = call(
-        prepare_kernel,
-        [f32(4, 2, 2, W, LANES)]
-        + [jax.ShapeDtypeStruct((2 * NK, NK), jnp.bfloat16)] * 2
-        + [f32(264, LANES)] * 4,
-        [VMEM] * 9,
+    products, number, target = call(
+        right_kernel,
+        [f32(4, 2, 2, W, LANES)] + [jax.ShapeDtypeStruct((1,), jnp.int32)] * 2,
+        [VMEM, VMEM, SMEM],
         1 << 27,
+        out_specs=[VMEM, SMEM, SMEM],
+    )(in_hbm(coupling), in_hbm(gauge), kq_index.T)
+    products = spread(products)
+    branches = [functools.partial(translated, number=number) for number in range(16)]
+    kept = lax.switch(number[0], branches, planes)
+    swapped = lax.ppermute(kept, "core", [(0, 1), (1, 0)])
+    high, low, *packs = call(
+        owners_kernel,
+        [jax.ShapeDtypeStruct((2 * NK, NK), jnp.bfloat16)] * 2 + [f32(264, LANES)] * 4,
+        [VMEM] * 7,
+        1 << 20,
     )(
         *(
-            pltpu.with_memory_space_constraint(value, pltpu.HBM)
+            in_hbm(value)
             for value in (
-                coupling,
-                gauge,
                 fine_coords,
                 jnp.asarray(phase_tables()),
                 eig_left,
@@ -318,12 +330,8 @@
             )
         )
     )
-    products = spread(products)
-    branches = [functools.partial(translated, number=number) for number in range(16)]
-    kept = lax.switch(number, branches, planes)
-    swapped = lax.ppermute(kept, "core", [(0, 1), (1, 0)])
     pieces = call(left_kernel, f32(1024, LANES), [SMEM] + [VMEM] * 3, 1 << 27)(
-        target.reshape(1), kept, swapped, products
+        target, kept, swapped, products
     )
     columns = lax.all_to_all(pieces.reshape(32, 32, LANES), ("y", "x", "core"), 0, 0, tiled=True)
     packs = shifted(packs)

time: 111 us -> 112 us (level)
  blocking collectives: 41.6 us -> 22 us
  waiting for transfers between devices: 10.9 us -> 22.6 us
  starting transfers between devices: 46.3 us -> 54.6 us
  Pallas kernels: 7.98 us -> 10.2 us
    all_to_all x1 -> x0, blocking collectives: 19.5 us -> none  [shards(): lax.all_to_all(pieces.reshape(32, 32, LANES), ('y', 'x', 'core'), 0, 0, t...]
    all_to_all x0 -> x1, waiting for transfers between devices: none -> 9.66 us  [shards(): lax.all_to_all(pieces.reshape(32, 32, LANES), ('y', 'x', 'core'), 0, 0, t...]
    all_to_all x0 -> x1, starting transfers between devices: none -> 8.31 us  [shards(): lax.all_to_all(pieces.reshape(32, 32, LANES), ('y', 'x', 'core'), 0, 0, t...]
    ppermute x3, waiting for transfers between devices: 0.53 us -> 2.6 us  [shards(): planes.append(lax.ppermute(gauge, ('z', 'pb'), pairs))]
    pallas_call x1 -> x2, Pallas kernels: 2.55 us -> 4.04 us  [the longest x1 2.28 us: shards(): call(right_kernel, [f32(4, 2, 2, W, LANES)] + [jax.ShapeDtypeStruct((1,),...]
  transfers between devices with their start and end apart: 10 -> 11, of which waited for: 4 -> 6; matrix products, arithmetic and copies ran while one was open for 1% -> 0% of each run, Pallas kernels for 0% -> 2%
where the time goes in v9:
time: 112 us; the launch traced here: 111 us
  starting transfers between devices  54.6 us (49%)
  waiting for transfers between devices  22.6 us (20%)
  blocking collectives  22 us (20%)
  Pallas kernels  10.2 us (9%)
    all_to_all x1, blocking collectives, shards(): terms = lax.all_to_all(terms, ('z', 'pb'), 0, 0, tiled=True)  22 us
    ppermute x3, starting transfers between devices, shards(): planes.append(lax.ppermute(gauge, ('z', 'pb'), pairs))  15.8 us
    all_to_all x1, waiting for transfers between devices, shards(): lax.all_to_all(pieces.reshape(32, 32, LANES), ('y', 'x', 'core'), 0, 0, t...  9.66 us
    ppermute x3, starting transfers between devices, shifted(): arrived.append(lax.ppermute(values[shift], 'z', pairs))  9 us
    all_to_all x1, starting transfers between devices, shards(): lax.all_to_all(pieces.reshape(32, 32, LANES), ('y', 'x', 'core'), 0, 0, t...  8.31 us
    all_to_all x1, starting transfers between devices, spread(): return lax.all_to_all(value, 'z', 0, 0, tiled=True)  6.57 us
    ppermute x3, waiting for transfers between devices, shifted(): arrived.append(lax.ppermute(values[shift], 'z', pairs))  5.92 us
    ppermute x1, starting transfers between devices, translated(): return lax.ppermute(value, ('y', 'x'), pairs)  5.67 us
  transfers between devices with their start and end apart: 11, of which 6 were waited for; matrix products, arithmetic and copies ran while one was open for 0% of the time, Pallas kernels for 2%

profile of v9, /device:TPU:1, one launch (start us, length us, event | category | flops | bytes accessed | tf_op | source)
XLA Modules:
  0.0 111.2 jit_solution(6291795354108542590)
XLA Ops:
  0.0 0.7 copy-done
  0.7 2.3 %shard_map.110 = (f32[4,2,2,64,128]{4,3,2,1,0:T(8,128)}, s32[1]{0:T(128)}, s32[1]{0:T(128)}) custom-call(f32[2,4,2,64,128]{4,3,2,1,0:T(8,128)} %coupling.1, f32[2,64,128]{2,1,0:T(8,128)} %gauge.1, s32[2,16]{1,0:T(2,128)S(1)} %bitcast.10), custom_call_target="tpu_custom_call" | custom-call | flops 134217728 | bytes 1048576 | tf_op jit(solution)/shard_map/pallas_call | solution.py:303
  3.0 0.0 copy-start.1
  3.0 6.6 %all-to-all-start = ((f32[4,2,2,64,128]{4,3,2,1,0:T(8,128)}), f32[4,2,2,64,128]{4,3,2,1,0:T(8,128)S(1)}, u32[]{:S(2)}, u32[]{:S(2)}) async-start(f32[4,2,2,64,128]{4,3,2,1,0:T(8,128)} %get-tuple-element.51), calls=%async_computation | async-start | bytes 1048576 | tf_op jit(solution)/shard_map/all_to_all | solution.py:269
  9.6 10.6 %collective-permute-start.15 = (f32[2,64,128]{2,1,0:T(8,128)S(1)}, f32[2,64,128]{2,1,0:T(8,128)S(1)}, u32[]{:S(2)}, u32[]{:S(2)}) collective-permute-start(f32[2,64,128]{2,1,0:T(8,128)S(1)} %copy-done.1), channel_id=1, source_target_pairs={{128,0},{256,128},{384,256},{1,384},{129,1},{257,129},{385,257},{2... | collective-permute-start | bytes 196616 | tf_op jit(solution)/shard_map/ppermute | solution.py:301
  20.1 2.2 %collective-permute-start.16 = (f32[2,64,128]{2,1,0:T(8,128)S(1)}, f32[2,64,128]{2,1,0:T(8,128)S(1)}, u32[]{:S(2)}, u32[]{:S(2)}) collective-permute-start(f32[2,64,128]{2,1,0:T(8,128)S(1)} %copy-done.1), channel_id=1, source_target_pairs={{256,0},{384,128},{1,256},{129,384},{257,1},{385,129},{2,257},{130... | collective-permute-start | bytes 196616 | tf_op jit(solution)/shard_map/ppermute | solution.py:301
  22.3 3.1 %collective-permute-start.17 = (f32[2,64,128]{2,1,0:T(8,128)S(1)}, f32[2,64,128]{2,1,0:T(8,128)S(1)}, u32[]{:S(2)}, u32[]{:S(2)}) collective-permute-start(f32[2,64,128]{2,1,0:T(8,128)S(1)} %copy-done.1), channel_id=1, source_target_pairs={{387,0},{0,128},{128,256},{256,384},{384,1},{1,129},{129,257},{257... | collective-permute-start | bytes 196616 | tf_op jit(solution)/shard_map/ppermute | solution.py:301
  26.1 1.4 %collective-permute-done.16 = f32[2,64,128]{2,1,0:T(8,128)S(1)} collective-permute-done((f32[2,64,128]{2,1,0:T(8,128)S(1)}, f32[2,64,128]{2,1,0:T(8,128)S(1)}, u32[]{:S(2)}, u32[]{:S(2)}) %collective-permute-start.16) | collective-permute-done | bytes 65568 | tf_op jit(solution)/shard_map/ppermute | solution.py:301
  27.5 1.2 %collective-permute-done.17 = f32[2,64,128]{2,1,0:T(8,128)S(1)} collective-permute-done((f32[2,64,128]{2,1,0:T(8,128)S(1)}, f32[2,64,128]{2,1,0:T(8,128)S(1)}, u32[]{:S(2)}, u32[]{:S(2)}) %collective-permute-start.17) | collective-permute-done | bytes 65568 | tf_op jit(solution)/shard_map/ppermute | solution.py:301
  28.7 9.0 %conditional.1 = (f32[4,2,64,128]{3,2,1,0:T(8,128)S(1)}) conditional(s32[]{:T(128)} %bitcast.1, f32[4,2,64,128]{3,2,1,0:T(8,128)S(1)} %pad_maximum_fusion, f32[4,2,64,128]{3,2,1,0:T(8,128)S(1)} %pad_maximum_fusion, f32[4,2,64,128]{3,2,1,0:T(8,128)S(1)} %pad_maximum_fusion, ...), branch_computations={%region_0.0_spmd, %region_1.0_spmd, %region_2.0_spmd, %region_3.0_... | conditional | bytes 1572912 | solution.py:312
  28.7 5.7 %collective-permute-start.1 = (f32[4,2,64,128]{3,2,1,0:T(8,128)S(1)}, f32[4,2,64,128]{3,2,1,0:T(8,128)S(1)}, u32[]{:S(2)}, u32[]{:S(2)}) collective-permute-start(f32[4,2,64,128]{3,2,1,0:T(8,128)S(1)} %param.2), channel_id=1, source_target_pairs={{16,0},{24,8},{32,16},{40,24},{48,32},{56,40},{0,48},{8,56},{80,64... | collective-permute-start | bytes 786440 | tf_op jit(solution)/shard_map/cond/branch_2_fun/ppermute | solution.py:77
  34.4 3.3 %collective-permute-done.1 = f32[4,2,64,128]{3,2,1,0:T(8,128)S(1)} collective-permute-done((f32[4,2,64,128]{3,2,1,0:T(8,128)S(1)}, f32[4,2,64,128]{3,2,1,0:T(8,128)S(1)}, u32[]{:S(2)}, u32[]{:S(2)}) %collective-permute-start.1) | collective-permute-done | bytes 262176 | tf_op jit(solution)/shard_map/cond/branch_2_fun/ppermute | solution.py:77
  37.7 5.3 %collective-permute-start.18 = (f32[4,2,64,128]{3,2,1,0:T(8,128)S(1)}, f32[4,2,64,128]{3,2,1,0:T(8,128)S(1)}, u32[]{:S(2)}, u32[]{:S(2)}) collective-permute-start(f32[4,2,64,128]{3,2,1,0:T(8,128)S(1)} %get-tuple-element.56.kept), channel_id=1, source_target_pairs={{0,4},{4,0},{1,5},{5,1},{2,6},{6,2},{3,7},{7,3},{8,12},{12,8},{9,1... | collective-permute-start | bytes 786440 | tf_op jit(solution)/shard_map/ppermute | solution.py:313
  43.0 1.1 %collective-permute-done.18.swapped = f32[4,2,64,128]{3,2,1,0:T(8,128)S(1)} collective-permute-done((f32[4,2,64,128]{3,2,1,0:T(8,128)S(1)}, f32[4,2,64,128]{3,2,1,0:T(8,128)S(1)}, u32[]{:S(2)}, u32[]{:S(2)}) %collective-permute-start.18) | collective-permute-done | bytes 262176 | tf_op jit(solution)/shard_map/ppermute | solution.py:313
  44.2 0.0 all-to-all-done.products
  44.2 2.1 %shard_map.111 = f32[1024,128]{1,0:T(8,128)} custom-call(s32[1]{0:T(128)} %get-tuple-element.49.target, f32[4,2,64,128]{3,2,1,0:T(8,128)S(1)} %get-tuple-element.56.kept, f32[4,2,64,128]{3,2,1,0:T(8,128)S(1)} %collective-permute-done.18.swapped, f32[4,2,2,64,128]{4,3,2,1,0:T(8,128)S(1)} %all-to-all-done.products), custom_call_target="tpu_custom_call" | custom-call | flops 134217728 | bytes 1048576 | tf_op jit(solution)/shard_map/pallas_call | solution.py:333
  46.3 8.3 %all-to-all-start.1 = ((f32[32,32,128]{2,1,0:T(8,128)}), f32[32,32,128]{2,1,0:T(8,128)S(1)}, u32[]{:S(2)}, u32[]{:S(2)}) async-start(f32[32,32,128]{2,1,0:T(8,128)} %bitcast.6), calls=%async_computation.1 | async-start | bytes 1048576 | tf_op jit(solution)/shard_map/all_to_all | solution.py:336
  54.6 1.8 %shard_map.109 = (bf16[512,256]{1,0:T(8,128)(2,1)S(1)}, bf16[512,256]{1,0:T(8,128)(2,1)S(1)}, f32[264,128]{1,0:T(8,128)S(1)}, f32[264,128]{1,0:T(8,128)S(1)}, f3...) custom-call(s32[3,256]{1,0:T(4,128)} %coords.1, bf16[3,96,512]{2,1,0:T(8,128)(2,1)} %constant.8.clone.tables, ...), custom_call_target="tpu_custom_call" | custom-call | flops 1048576 | bytes 1048576 | tf_op jit(solution)/shard_map/pallas_call | solution.py:314
  56.3 9.7 %all-to-all-done.1.columns = f32[32,32,128]{2,1,0:T(8,128)S(1)} async-done(((f32[32,32,128]{2,1,0:T(8,128)}), f32[32,32,128]{2,1,0:T(8,128)S(1)}, u32[]{:S(2)}, u32[]{:S(2)}) %all-to-all-start.1) | async-done | bytes 524320 | tf_op jit(solution)/shard_map/all_to_all | solution.py:336
  66.0 1.7 %shard_map.112 = f32[32,4,8,128]{3,2,1,0:T(8,128)} custom-call(bf16[512,256]{1,0:T(8,128)(2,1)S(1)} %get-tuple-element.47.high, bf16[512,256]{1,0:T(8,128)(2,1)S(1)} %get-tuple-element.48.low, f32[32,32,128]{2,1,0:T(8,128)S(1)} %all-to-all-done.1.columns), custom_call_target="tpu_custom_call" | custom-call | flops 268435456 | bytes 1048576 | tf_op jit(solution)/shard_map/pallas_call | solution.py:339
  67.7 3.9 %all-to-all-start.2 = ((f32[32,32,128]{2,1,0:T(8,128)}), f32[32,32,128]{2,1,0:T(8,128)S(1)}, u32[]{:S(2)}, u32[]{:S(2)}) async-start(f32[32,32,128]{2,1,0:T(8,128)} %bitcast.7), calls=%async_computation.2 | async-start | bytes 1048576 | tf_op jit(solution)/shard_map/all_to_all | solution.py:347
  71.6 1.9 %collective-permute-start.19 = (f32[264,128]{1,0:T(8,128)S(1)}, f32[264,128]{1,0:T(8,128)S(1)}, u32[]{:S(2)}, u32[]{:S(2)}) collective-permute-start(f32[264,128]{1,0:T(8,128)S(1)} %get-tuple-element.53), channel_id=1, source_target_pairs={{0,128},{128,256},{256,384},{384,0},{1,129},{129,257},{257,385},{3... | collective-permute-start | bytes 405512 | tf_op jit(solution)/shard_map/ppermute | solution.py:280
  73.5 0.0 copy-start.2
  73.6 3.2 %collective-permute-start.20 = (f32[264,128]{1,0:T(8,128)S(1)}, f32[264,128]{1,0:T(8,128)S(1)}, u32[]{:S(2)}, u32[]{:S(2)}) collective-permute-start(f32[264,128]{1,0:T(8,128)S(1)} %get-tuple-element.54), channel_id=1, source_target_pairs={{0,256},{128,384},{256,0},{384,128},{1,257},{129,385},{257,1},{385... | collective-permute-start | bytes 405512 | tf_op jit(solution)/shard_map/ppermute | solution.py:280
  76.8 3.8 %collective-permute-start.21 = (f32[264,128]{1,0:T(8,128)S(1)}, f32[264,128]{1,0:T(8,128)S(1)}, u32[]{:S(2)}, u32[]{:S(2)}) collective-permute-start(f32[264,128]{1,0:T(8,128)S(1)} %get-tuple-element.55), channel_id=1, source_target_pairs={{0,384},{128,0},{256,128},{384,256},{1,385},{129,1},{257,129},{385... | collective-permute-start | bytes 405512 | tf_op jit(solution)/shard_map/ppermute | solution.py:280
  80.7 0.1 copy.12.frequency
  80.8 0.0 collective-permute-done.19.packs_and_out_1_
  80.8 5.9 %collective-permute-done.20.packs_and_out_2_ = f32[264,128]{1,0:T(8,128)S(1)} collective-permute-done((f32[264,128]{1,0:T(8,128)S(1)}, f32[264,128]{1,0:T(8,128)S(1)}, u32[]{:S(2)}, u32[]{:S(2)}) %collective-permute-start.20) | collective-permute-done | bytes 135200 | tf_op jit(solution)/shard_map/ppermute | solution.py:280
  86.7 0.0 collective-permute-done.21.packs_and_out_3_
  86.7 1.8 %shard_map.113 = f32[16,1,128]{2,1,0:T(1,128)S(1)} custom-call(f32[4,2]{1,0:T(4,128)S(1)} %copy.12.frequency, f32[1024,128]{1,0:T(8,128)S(1)} %bitcast.9, f32[264,128]{1,0:T(8,128)S(1)} %get-tuple-element.52.packs_and_out_0_, f32[264,128]{1,0:T(8,128)S(1)} %collective-permute-done.19.packs_and_out_1_, ...), custom_call_target="tpu_custom_call" | custom-call | flops 134217728 | bytes 1048576 | tf_op jit(solution)/shard_map/pallas_call | solution.py:350
  88.5 22.0 %all_to_all.20.terms = f32[16,1,128]{2,1,0:T(1,128)S(1)} all-to-all(f32[16,1,128]{2,1,0:T(1,128)S(1)} %shard_map.113), channel_id=1, replica_groups=mesh['z'=4,'y'=4,'x'=4,'core'=2,'pb'=4] {'z','pb'}, dimensions={0} | all-to-all | bytes 16384 | tf_op jit(solution)/shard_map/all_to_all | solution.py:353
  110.5 0.6 shard_map.114
  (7 shorter events, 0.0 us)
Async XLA Ops:
  0.0 0.7 copy-start
  3.0 6.6 %copy-start.1 = (f32[2,64,128]{2,1,0:T(8,128)S(1)}, f32[2,64,128]{2,1,0:T(8,128)}, u32[]{:S(2)}) copy-start(f32[2,64,128]{2,1,0:T(8,128)} %gauge.1) | copy-start | bytes 196612
  3.0 41.2 %all-to-all-start = ((f32[4,2,2,64,128]{4,3,2,1,0:T(8,128)}), f32[4,2,2,64,128]{4,3,2,1,0:T(8,128)S(1)}, u32[]{:S(2)}, u32[]{:S(2)}) async-start(f32[4,2,2,64,128]{4,3,2,1,0:T(8,128)} %get-tuple-element.51), calls=%async_computation | async-start | bytes 1048576 | tf_op jit(solution)/shard_map/all_to_all | solution.py:269
  9.6 16.5 %collective-permute-start.15 = (f32[2,64,128]{2,1,0:T(8,128)S(1)}, f32[2,64,128]{2,1,0:T(8,128)S(1)}, u32[]{:S(2)}, u32[]{:S(2)}) collective-permute-start(f32[2,64,128]{2,1,0:T(8,128)S(1)} %copy-done.1), channel_id=1, source_target_pairs={{128,0},{256,128},{384,256},{1,384},{129,1},{257,129},{385,257},{2... | collective-permute-start | bytes 196616 | tf_op jit(solution)/shard_map/ppermute | solution.py:301
  20.1 7.4 %collective-permute-start.16 = (f32[2,64,128]{2,1,0:T(8,128)S(1)}, f32[2,64,128]{2,1,0:T(8,128)S(1)}, u32[]{:S(2)}, u32[]{:S(2)}) collective-permute-start(f32[2,64,128]{2,1,0:T(8,128)S(1)} %copy-done.1), channel_id=1, source_target_pairs={{256,0},{384,128},{1,256},{129,384},{257,1},{385,129},{2,257},{130... | collective-permute-start | bytes 196616 | tf_op jit(solution)/shard_map/ppermute | solution.py:301
  22.3 6.4 %collective-permute-start.17 = (f32[2,64,128]{2,1,0:T(8,128)S(1)}, f32[2,64,128]{2,1,0:T(8,128)S(1)}, u32[]{:S(2)}, u32[]{:S(2)}) collective-permute-start(f32[2,64,128]{2,1,0:T(8,128)S(1)} %copy-done.1), channel_id=1, source_target_pairs={{387,0},{0,128},{128,256},{256,384},{384,1},{1,129},{129,257},{257... | collective-permute-start | bytes 196616 | tf_op jit(solution)/shard_map/ppermute | solution.py:301
  28.7 9.0 %collective-permute-start.1 = (f32[4,2,64,128]{3,2,1,0:T(8,128)S(1)}, f32[4,2,64,128]{3,2,1,0:T(8,128)S(1)}, u32[]{:S(2)}, u32[]{:S(2)}) collective-permute-start(f32[4,2,64,128]{3,2,1,0:T(8,128)S(1)} %param.2), channel_id=1, source_target_pairs={{16,0},{24,8},{32,16},{40,24},{48,32},{56,40},{0,48},{8,56},{80,64... | collective-permute-start | bytes 786440 | tf_op jit(solution)/shard_map/cond/branch_2_fun/ppermute | solution.py:77
  37.7 6.4 %collective-permute-start.18 = (f32[4,2,64,128]{3,2,1,0:T(8,128)S(1)}, f32[4,2,64,128]{3,2,1,0:T(8,128)S(1)}, u32[]{:S(2)}, u32[]{:S(2)}) collective-permute-start(f32[4,2,64,128]{3,2,1,0:T(8,128)S(1)} %get-tuple-element.56.kept), channel_id=1, source_target_pairs={{0,4},{4,0},{1,5},{5,1},{2,6},{6,2},{3,7},{7,3},{8,12},{12,8},{9,1... | collective-permute-start | bytes 786440 | tf_op jit(solution)/shard_map/ppermute | solution.py:313
  46.3 19.7 %all-to-all-start.1 = ((f32[32,32,128]{2,1,0:T(8,128)}), f32[32,32,128]{2,1,0:T(8,128)S(1)}, u32[]{:S(2)}, u32[]{:S(2)}) async-start(f32[32,32,128]{2,1,0:T(8,128)} %bitcast.6), calls=%async_computation.1 | async-start | bytes 1048576 | tf_op jit(solution)/shard_map/all_to_all | solution.py:336
  67.7 19.0 %all-to-all-start.2 = ((f32[32,32,128]{2,1,0:T(8,128)}), f32[32,32,128]{2,1,0:T(8,128)S(1)}, u32[]{:S(2)}, u32[]{:S(2)}) async-start(f32[32,32,128]{2,1,0:T(8,128)} %bitcast.7), calls=%async_computation.2 | async-start | bytes 1048576 | tf_op jit(solution)/shard_map/all_to_all | solution.py:347
  71.6 9.1 %collective-permute-start.19 = (f32[264,128]{1,0:T(8,128)S(1)}, f32[264,128]{1,0:T(8,128)S(1)}, u32[]{:S(2)}, u32[]{:S(2)}) collective-permute-start(f32[264,128]{1,0:T(8,128)S(1)} %get-tuple-element.53), channel_id=1, source_target_pairs={{0,128},{128,256},{256,384},{384,0},{1,129},{129,257},{257,385},{3... | collective-permute-start | bytes 405512 | tf_op jit(solution)/shard_map/ppermute | solution.py:280
  73.5 7.1 %copy-start.2 = (f32[4,2]{0,1:T(2,128)S(1)}, f32[4,2]{0,1:T(2,128)}, u32[]{:S(2)}) copy-start(f32[4,2]{0,1:T(2,128)} %param.36) | copy-start | bytes 100
  73.6 13.1 %collective-permute-start.20 = (f32[264,128]{1,0:T(8,128)S(1)}, f32[264,128]{1,0:T(8,128)S(1)}, u32[]{:S(2)}, u32[]{:S(2)}) collective-permute-start(f32[264,128]{1,0:T(8,128)S(1)} %get-tuple-element.54), channel_id=1, source_target_pairs={{0,256},{128,384},{256,0},{384,128},{1,257},{129,385},{257,1},{385... | collective-permute-start | bytes 405512 | tf_op jit(solution)/shard_map/ppermute | solution.py:280
  76.8 9.9 %collective-permute-start.21 = (f32[264,128]{1,0:T(8,128)S(1)}, f32[264,128]{1,0:T(8,128)S(1)}, u32[]{:S(2)}, u32[]{:S(2)}) collective-permute-start(f32[264,128]{1,0:T(8,128)S(1)} %get-tuple-element.55), channel_id=1, source_target_pairs={{0,384},{128,0},{256,128},{384,256},{1,385},{129,1},{257,129},{385... | collective-permute-start | bytes 405512 | tf_op jit(solution)/shard_map/ppermute | solution.py:280

commit v10 on v9

--- a/solution.py
+++ b/solution.py
@@ -84,11 +84,9 @@
     number[0] = (((point >> 2) - (along_y * 4 + along_x)) & 7) + (
         (((point >> 5) - (along_y >> 1)) & 1) << 3
     )
-    for k in range(2):
-        rows = coupling[k].reshape(-1, LANES)
-        result = product(halves(rows), right_block(gauge[k]), (1, 0)).reshape(4, 2, W, LANES)
-        for q in range(4):
-            out[q, k] = result[q]
+    rows = coupling[0].reshape(-1, LANES)
+    result = product(halves(rows), right_block(gauge[0]), (1, 0)).reshape(4, 2, W, LANES)
+    out[:, 0] = result
 
 
 def owners_kernel(
@@ -221,7 +219,7 @@
         summed = jnp.sum(total, axis=0, keepdims=True) * (1.0 / 1024.0)
         plane = (lax.axis_index("z") - shift + 4) & 3
         for group in range(4):
-            out[plane * 4 + group] = summed
+            out[group * 4 + plane] = summed
 
 
 def sum_kernel(terms, out):
@@ -303,9 +301,18 @@
     products, number, target = call(
         right_kernel,
         [f32(4, 2, 2, W, LANES)] + [jax.ShapeDtypeStruct((1,), jnp.int32)] * 2,
-        [VMEM, VMEM, SMEM],
+        [
+            pl.BlockSpec((1, 4, 2, W, LANES), lambda k: (k, 0, 0, 0, 0)),
+            pl.BlockSpec((1, W, LANES), lambda k: (k, 0, 0)),
+            SMEM,
+        ],
         1 << 27,
-        out_specs=[VMEM, SMEM, SMEM],
+        grid=(2,),
+        out_specs=[
+            pl.BlockSpec((4, 1, 2, W, LANES), lambda k: (0, k, 0, 0, 0)),
+            SMEM,
+            SMEM,
+        ],
     )(in_hbm(coupling), in_hbm(gauge), kq_index.T)
     products = spread(products)
     branches = [functools.partial(translated, number=number) for number in range(16)]
@@ -350,7 +357,7 @@
     terms = call(bloch_kernel, f32(16, 1, LANES), [SMEM] + [VMEM] * 5, 1 << 27)(
         frequency, blocks.reshape(1024, LANES), *packs
     )
-    terms = lax.all_to_all(terms, ("z", "pb"), 0, 0, tiled=True)
+    terms = lax.all_to_all(terms, ("pb", "z"), 0, 0, tiled=True)
     return call(sum_kernel, f32(2, W), [VMEM], 1 << 12)(terms)
 
 

time: 112 us -> 113 us (level)
  no operation moved by 1% of the time
where the time goes in v10:
time: 113 us; the launch traced here: 111 us
  starting transfers between devices  54.6 us (48%)
  waiting for transfers between devices  22.6 us (20%)
  blocking collectives  22.1 us (20%)
  Pallas kernels  10.3 us (9%)
    all_to_all x1, blocking collectives, shards(): terms = lax.all_to_all(terms, ('pb', 'z'), 0, 0, tiled=True)  22.1 us
    ppermute x3, starting transfers between devices, shards(): planes.append(lax.ppermute(gauge, ('z', 'pb'), pairs))  15.8 us
    all_to_all x1, waiting for transfers between devices, shards(): lax.all_to_all(pieces.reshape(32, 32, LANES), ('y', 'x', 'core'), 0, 0, t...  9.66 us
    ppermute x3, starting transfers between devices, shifted(): arrived.append(lax.ppermute(values[shift], 'z', pairs))  9 us
    all_to_all x1, starting transfers between devices, shards(): lax.all_to_all(pieces.reshape(32, 32, LANES), ('y', 'x', 'core'), 0, 0, t...  8.3 us
    all_to_all x1, starting transfers between devices, spread(): return lax.all_to_all(value, 'z', 0, 0, tiled=True)  6.57 us
    ppermute x3, waiting for transfers between devices, shifted(): arrived.append(lax.ppermute(values[shift], 'z', pairs))  5.92 us
    ppermute x1, starting transfers between devices, translated(): return lax.ppermute(value, ('y', 'x'), pairs)  5.66 us
  transfers between devices with their start and end apart: 11, of which 6 were waited for; matrix products, arithmetic and copies ran while one was open for 0% of the time, Pallas kernels for 2%

profile of v10, /device:TPU:1, one launch (start us, length us, event | category | flops | bytes accessed | tf_op | source)
XLA Modules:
  0.0 111.3 jit_solution(15699125645040333069)
XLA Ops:
  0.0 0.7 copy-done
  0.7 2.4 %shard_map.110 = (f32[4,2,2,64,128]{4,3,2,1,0:T(8,128)}, s32[1]{0:T(128)}, s32[1]{0:T(128)}) custom-call(f32[2,4,2,64,128]{4,3,2,1,0:T(8,128)} %coupling.1, f32[2,64,128]{2,1,0:T(8,128)} %gauge.1, s32[2,16]{1,0:T(2,128)S(1)} %bitcast.10), custom_call_target="tpu_custom_call" | custom-call | flops 134217728 | bytes 1048576 | tf_op jit(solution)/shard_map/pallas_call | solution.py:301
  3.0 6.6 %all-to-all-start = ((f32[4,2,2,64,128]{4,3,2,1,0:T(8,128)}), f32[4,2,2,64,128]{4,3,2,1,0:T(8,128)S(1)}, u32[]{:S(2)}, u32[]{:S(2)}) async-start(f32[4,2,2,64,128]{4,3,2,1,0:T(8,128)} %get-tuple-element.51), calls=%async_computation | async-start | bytes 1048576 | tf_op jit(solution)/shard_map/all_to_all | solution.py:267
  9.6 10.6 %collective-permute-start.15 = (f32[2,64,128]{2,1,0:T(8,128)S(1)}, f32[2,64,128]{2,1,0:T(8,128)S(1)}, u32[]{:S(2)}, u32[]{:S(2)}) collective-permute-start(f32[2,64,128]{2,1,0:T(8,128)S(1)} %copy-done.1), channel_id=1, source_target_pairs={{128,0},{256,128},{384,256},{1,384},{129,1},{257,129},{385,257},{2... | collective-permute-start | bytes 196616 | tf_op jit(solution)/shard_map/ppermute | solution.py:299
  20.2 2.2 %collective-permute-start.16 = (f32[2,64,128]{2,1,0:T(8,128)S(1)}, f32[2,64,128]{2,1,0:T(8,128)S(1)}, u32[]{:S(2)}, u32[]{:S(2)}) collective-permute-start(f32[2,64,128]{2,1,0:T(8,128)S(1)} %copy-done.1), channel_id=1, source_target_pairs={{256,0},{384,128},{1,256},{129,384},{257,1},{385,129},{2,257},{130... | collective-permute-start | bytes 196616 | tf_op jit(solution)/shard_map/ppermute | solution.py:299
  22.4 3.1 %collective-permute-start.17 = (f32[2,64,128]{2,1,0:T(8,128)S(1)}, f32[2,64,128]{2,1,0:T(8,128)S(1)}, u32[]{:S(2)}, u32[]{:S(2)}) collective-permute-start(f32[2,64,128]{2,1,0:T(8,128)S(1)} %copy-done.1), channel_id=1, source_target_pairs={{387,0},{0,128},{128,256},{256,384},{384,1},{1,129},{129,257},{257... | collective-permute-start | bytes 196616 | tf_op jit(solution)/shard_map/ppermute | solution.py:299
  26.1 0.0 collective-permute-done.15
  26.1 1.4 %collective-permute-done.16 = f32[2,64,128]{2,1,0:T(8,128)S(1)} collective-permute-done((f32[2,64,128]{2,1,0:T(8,128)S(1)}, f32[2,64,128]{2,1,0:T(8,128)S(1)}, u32[]{:S(2)}, u32[]{:S(2)}) %collective-permute-start.16) | collective-permute-done | bytes 65568 | tf_op jit(solution)/shard_map/ppermute | solution.py:299
  27.5 1.2 %collective-permute-done.17 = f32[2,64,128]{2,1,0:T(8,128)S(1)} collective-permute-done((f32[2,64,128]{2,1,0:T(8,128)S(1)}, f32[2,64,128]{2,1,0:T(8,128)S(1)}, u32[]{:S(2)}, u32[]{:S(2)}) %collective-permute-start.17) | collective-permute-done | bytes 65568 | tf_op jit(solution)/shard_map/ppermute | solution.py:299
  28.8 9.0 %conditional.1 = (f32[4,2,64,128]{3,2,1,0:T(8,128)S(1)}) conditional(s32[]{:T(128)} %bitcast.1, f32[4,2,64,128]{3,2,1,0:T(8,128)S(1)} %pad_maximum_fusion, f32[4,2,64,128]{3,2,1,0:T(8,128)S(1)} %pad_maximum_fusion, f32[4,2,64,128]{3,2,1,0:T(8,128)S(1)} %pad_maximum_fusion, ...), branch_computations={%region_0.0_spmd, %region_1.0_spmd, %region_2.0_spmd, %region_3.0_... | conditional | bytes 1572912 | solution.py:319
  28.8 5.7 %collective-permute-start.1 = (f32[4,2,64,128]{3,2,1,0:T(8,128)S(1)}, f32[4,2,64,128]{3,2,1,0:T(8,128)S(1)}, u32[]{:S(2)}, u32[]{:S(2)}) collective-permute-start(f32[4,2,64,128]{3,2,1,0:T(8,128)S(1)} %param.2), channel_id=1, source_target_pairs={{16,0},{24,8},{32,16},{40,24},{48,32},{56,40},{0,48},{8,56},{80,64... | collective-permute-start | bytes 786440 | tf_op jit(solution)/shard_map/cond/branch_2_fun/ppermute | solution.py:77
  34.5 3.3 %collective-permute-done.1 = f32[4,2,64,128]{3,2,1,0:T(8,128)S(1)} collective-permute-done((f32[4,2,64,128]{3,2,1,0:T(8,128)S(1)}, f32[4,2,64,128]{3,2,1,0:T(8,128)S(1)}, u32[]{:S(2)}, u32[]{:S(2)}) %collective-permute-start.1) | collective-permute-done | bytes 262176 | tf_op jit(solution)/shard_map/cond/branch_2_fun/ppermute | solution.py:77
  37.8 5.3 %collective-permute-start.18 = (f32[4,2,64,128]{3,2,1,0:T(8,128)S(1)}, f32[4,2,64,128]{3,2,1,0:T(8,128)S(1)}, u32[]{:S(2)}, u32[]{:S(2)}) collective-permute-start(f32[4,2,64,128]{3,2,1,0:T(8,128)S(1)} %get-tuple-element.56.kept), channel_id=1, source_target_pairs={{0,4},{4,0},{1,5},{5,1},{2,6},{6,2},{3,7},{7,3},{8,12},{12,8},{9,1... | collective-permute-start | bytes 786440 | tf_op jit(solution)/shard_map/ppermute | solution.py:320
  43.1 1.1 %collective-permute-done.18.swapped = f32[4,2,64,128]{3,2,1,0:T(8,128)S(1)} collective-permute-done((f32[4,2,64,128]{3,2,1,0:T(8,128)S(1)}, f32[4,2,64,128]{3,2,1,0:T(8,128)S(1)}, u32[]{:S(2)}, u32[]{:S(2)}) %collective-permute-start.18) | collective-permute-done | bytes 262176 | tf_op jit(solution)/shard_map/ppermute | solution.py:320
  44.2 0.0 all-to-all-done.products
  44.2 2.1 %shard_map.111 = f32[1024,128]{1,0:T(8,128)} custom-call(s32[1]{0:T(128)} %get-tuple-element.49.target, f32[4,2,64,128]{3,2,1,0:T(8,128)S(1)} %get-tuple-element.56.kept, f32[4,2,64,128]{3,2,1,0:T(8,128)S(1)} %collective-permute-done.18.swapped, f32[4,2,2,64,128]{4,3,2,1,0:T(8,128)S(1)} %all-to-all-done.products), custom_call_target="tpu_custom_call" | custom-call | flops 134217728 | bytes 1048576 | tf_op jit(solution)/shard_map/pallas_call | solution.py:340
  46.3 8.3 %all-to-all-start.1 = ((f32[32,32,128]{2,1,0:T(8,128)}), f32[32,32,128]{2,1,0:T(8,128)S(1)}, u32[]{:S(2)}, u32[]{:S(2)}) async-start(f32[32,32,128]{2,1,0:T(8,128)} %bitcast.6), calls=%async_computation.1 | async-start | bytes 1048576 | tf_op jit(solution)/shard_map/all_to_all | solution.py:343
  54.6 1.8 %shard_map.109 = (bf16[512,256]{1,0:T(8,128)(2,1)S(1)}, bf16[512,256]{1,0:T(8,128)(2,1)S(1)}, f32[264,128]{1,0:T(8,128)S(1)}, f32[264,128]{1,0:T(8,128)S(1)}, f3...) custom-call(s32[3,256]{1,0:T(4,128)} %coords.1, bf16[3,96,512]{2,1,0:T(8,128)(2,1)} %constant.8.clone.tables, ...), custom_call_target="tpu_custom_call" | custom-call | flops 1048576 | bytes 1048576 | tf_op jit(solution)/shard_map/pallas_call | solution.py:321
  56.4 9.7 %all-to-all-done.1.columns = f32[32,32,128]{2,1,0:T(8,128)S(1)} async-done(((f32[32,32,128]{2,1,0:T(8,128)}), f32[32,32,128]{2,1,0:T(8,128)S(1)}, u32[]{:S(2)}, u32[]{:S(2)}) %all-to-all-start.1) | async-done | bytes 524320 | tf_op jit(solution)/shard_map/all_to_all | solution.py:343
  66.1 1.7 %shard_map.112 = f32[32,4,8,128]{3,2,1,0:T(8,128)} custom-call(bf16[512,256]{1,0:T(8,128)(2,1)S(1)} %get-tuple-element.47.high, bf16[512,256]{1,0:T(8,128)(2,1)S(1)} %get-tuple-element.48.low, f32[32,32,128]{2,1,0:T(8,128)S(1)} %all-to-all-done.1.columns), custom_call_target="tpu_custom_call" | custom-call | flops 268435456 | bytes 1048576 | tf_op jit(solution)/shard_map/pallas_call | solution.py:346
  67.7 3.9 %all-to-all-start.2 = ((f32[32,32,128]{2,1,0:T(8,128)}), f32[32,32,128]{2,1,0:T(8,128)S(1)}, u32[]{:S(2)}, u32[]{:S(2)}) async-start(f32[32,32,128]{2,1,0:T(8,128)} %bitcast.7), calls=%async_computation.2 | async-start | bytes 1048576 | tf_op jit(solution)/shard_map/all_to_all | solution.py:354
  71.7 1.9 %collective-permute-start.19 = (f32[264,128]{1,0:T(8,128)S(1)}, f32[264,128]{1,0:T(8,128)S(1)}, u32[]{:S(2)}, u32[]{:S(2)}) collective-permute-start(f32[264,128]{1,0:T(8,128)S(1)} %get-tuple-element.53), channel_id=1, source_target_pairs={{0,128},{128,256},{256,384},{384,0},{1,129},{129,257},{257,385},{3... | collective-permute-start | bytes 405512 | tf_op jit(solution)/shard_map/ppermute | solution.py:278
  73.6 0.0 copy-start.2
  73.6 3.2 %collective-permute-start.20 = (f32[264,128]{1,0:T(8,128)S(1)}, f32[264,128]{1,0:T(8,128)S(1)}, u32[]{:S(2)}, u32[]{:S(2)}) collective-permute-start(f32[264,128]{1,0:T(8,128)S(1)} %get-tuple-element.54), channel_id=1, source_target_pairs={{0,256},{128,384},{256,0},{384,128},{1,257},{129,385},{257,1},{385... | collective-permute-start | bytes 405512 | tf_op jit(solution)/shard_map/ppermute | solution.py:278
  76.9 3.8 %collective-permute-start.21 = (f32[264,128]{1,0:T(8,128)S(1)}, f32[264,128]{1,0:T(8,128)S(1)}, u32[]{:S(2)}, u32[]{:S(2)}) collective-permute-start(f32[264,128]{1,0:T(8,128)S(1)} %get-tuple-element.55), channel_id=1, source_target_pairs={{0,384},{128,0},{256,128},{384,256},{1,385},{129,1},{257,129},{385... | collective-permute-start | bytes 405512 | tf_op jit(solution)/shard_map/ppermute | solution.py:278
  80.7 0.1 copy.12.frequency
  80.8 0.0 collective-permute-done.19.packs_and_out_1_
  80.8 5.9 %collective-permute-done.20.packs_and_out_2_ = f32[264,128]{1,0:T(8,128)S(1)} collective-permute-done((f32[264,128]{1,0:T(8,128)S(1)}, f32[264,128]{1,0:T(8,128)S(1)}, u32[]{:S(2)}, u32[]{:S(2)}) %collective-permute-start.20) | collective-permute-done | bytes 135200 | tf_op jit(solution)/shard_map/ppermute | solution.py:278
  86.7 0.0 collective-permute-done.21.packs_and_out_3_
  86.7 1.8 %shard_map.113 = f32[16,1,128]{2,1,0:T(1,128)S(1)} custom-call(f32[4,2]{1,0:T(4,128)S(1)} %copy.12.frequency, f32[1024,128]{1,0:T(8,128)S(1)} %bitcast.9, f32[264,128]{1,0:T(8,128)S(1)} %get-tuple-element.52.packs_and_out_0_, f32[264,128]{1,0:T(8,128)S(1)} %collective-permute-done.19.packs_and_out_1_, ...), custom_call_target="tpu_custom_call" | custom-call | flops 134217728 | bytes 1048576 | tf_op jit(solution)/shard_map/pallas_call | solution.py:357
  88.5 22.1 %all_to_all.20.terms = f32[16,1,128]{2,1,0:T(1,128)S(1)} all-to-all(f32[16,1,128]{2,1,0:T(1,128)S(1)} %shard_map.113), channel_id=1, replica_groups=mesh['z'=4,'y'=4,'x'=4,'core'=2,'pb'=4] {'pb','z'}, dimensions={0} | all-to-all | bytes 16384 | tf_op jit(solution)/shard_map/all_to_all | solution.py:360
  110.6 0.6 shard_map.114
  (7 shorter events, 0.0 us)
Async XLA Ops:
  0.0 0.7 copy-start
  3.0 6.6 %copy-start.1 = (f32[2,64,128]{2,1,0:T(8,128)S(1)}, f32[2,64,128]{2,1,0:T(8,128)}, u32[]{:S(2)}) copy-start(f32[2,64,128]{2,1,0:T(8,128)} %gauge.1) | copy-start | bytes 196612
  3.0 41.2 %all-to-all-start = ((f32[4,2,2,64,128]{4,3,2,1,0:T(8,128)}), f32[4,2,2,64,128]{4,3,2,1,0:T(8,128)S(1)}, u32[]{:S(2)}, u32[]{:S(2)}) async-start(f32[4,2,2,64,128]{4,3,2,1,0:T(8,128)} %get-tuple-element.51), calls=%async_computation | async-start | bytes 1048576 | tf_op jit(solution)/shard_map/all_to_all | solution.py:267
  9.6 16.5 %collective-permute-start.15 = (f32[2,64,128]{2,1,0:T(8,128)S(1)}, f32[2,64,128]{2,1,0:T(8,128)S(1)}, u32[]{:S(2)}, u32[]{:S(2)}) collective-permute-start(f32[2,64,128]{2,1,0:T(8,128)S(1)} %copy-done.1), channel_id=1, source_target_pairs={{128,0},{256,128},{384,256},{1,384},{129,1},{257,129},{385,257},{2... | collective-permute-start | bytes 196616 | tf_op jit(solution)/shard_map/ppermute | solution.py:299
  20.2 7.4 %collective-permute-start.16 = (f32[2,64,128]{2,1,0:T(8,128)S(1)}, f32[2,64,128]{2,1,0:T(8,128)S(1)}, u32[]{:S(2)}, u32[]{:S(2)}) collective-permute-start(f32[2,64,128]{2,1,0:T(8,128)S(1)} %copy-done.1), channel_id=1, source_target_pairs={{256,0},{384,128},{1,256},{129,384},{257,1},{385,129},{2,257},{130... | collective-permute-start | bytes 196616 | tf_op jit(solution)/shard_map/ppermute | solution.py:299
  22.4 6.4 %collective-permute-start.17 = (f32[2,64,128]{2,1,0:T(8,128)S(1)}, f32[2,64,128]{2,1,0:T(8,128)S(1)}, u32[]{:S(2)}, u32[]{:S(2)}) collective-permute-start(f32[2,64,128]{2,1,0:T(8,128)S(1)} %copy-done.1), channel_id=1, source_target_pairs={{387,0},{0,128},{128,256},{256,384},{384,1},{1,129},{129,257},{257... | collective-permute-start | bytes 196616 | tf_op jit(solution)/shard_map/ppermute | solution.py:299
  28.8 9.0 %collective-permute-start.1 = (f32[4,2,64,128]{3,2,1,0:T(8,128)S(1)}, f32[4,2,64,128]{3,2,1,0:T(8,128)S(1)}, u32[]{:S(2)}, u32[]{:S(2)}) collective-permute-start(f32[4,2,64,128]{3,2,1,0:T(8,128)S(1)} %param.2), channel_id=1, source_target_pairs={{16,0},{24,8},{32,16},{40,24},{48,32},{56,40},{0,48},{8,56},{80,64... | collective-permute-start | bytes 786440 | tf_op jit(solution)/shard_map/cond/branch_2_fun/ppermute | solution.py:77
  37.8 6.4 %collective-permute-start.18 = (f32[4,2,64,128]{3,2,1,0:T(8,128)S(1)}, f32[4,2,64,128]{3,2,1,0:T(8,128)S(1)}, u32[]{:S(2)}, u32[]{:S(2)}) collective-permute-start(f32[4,2,64,128]{3,2,1,0:T(8,128)S(1)} %get-tuple-element.56.kept), channel_id=1, source_target_pairs={{0,4},{4,0},{1,5},{5,1},{2,6},{6,2},{3,7},{7,3},{8,12},{12,8},{9,1... | collective-permute-start | bytes 786440 | tf_op jit(solution)/shard_map/ppermute | solution.py:320
  46.3 19.7 %all-to-all-start.1 = ((f32[32,32,128]{2,1,0:T(8,128)}), f32[32,32,128]{2,1,0:T(8,128)S(1)}, u32[]{:S(2)}, u32[]{:S(2)}) async-start(f32[32,32,128]{2,1,0:T(8,128)} %bitcast.6), calls=%async_computation.1 | async-start | bytes 1048576 | tf_op jit(solution)/shard_map/all_to_all | solution.py:343
  67.7 19.0 %all-to-all-start.2 = ((f32[32,32,128]{2,1,0:T(8,128)}), f32[32,32,128]{2,1,0:T(8,128)S(1)}, u32[]{:S(2)}, u32[]{:S(2)}) async-start(f32[32,32,128]{2,1,0:T(8,128)} %bitcast.7), calls=%async_computation.2 | async-start | bytes 1048576 | tf_op jit(solution)/shard_map/all_to_all | solution.py:354
  71.7 9.1 %collective-permute-start.19 = (f32[264,128]{1,0:T(8,128)S(1)}, f32[264,128]{1,0:T(8,128)S(1)}, u32[]{:S(2)}, u32[]{:S(2)}) collective-permute-start(f32[264,128]{1,0:T(8,128)S(1)} %get-tuple-element.53), channel_id=1, source_target_pairs={{0,128},{128,256},{256,384},{384,0},{1,129},{129,257},{257,385},{3... | collective-permute-start | bytes 405512 | tf_op jit(solution)/shard_map/ppermute | solution.py:278
  73.6 7.1 %copy-start.2 = (f32[4,2]{0,1:T(2,128)S(1)}, f32[4,2]{0,1:T(2,128)}, u32[]{:S(2)}) copy-start(f32[4,2]{0,1:T(2,128)} %param.36) | copy-start | bytes 100
  73.6 13.1 %collective-permute-start.20 = (f32[264,128]{1,0:T(8,128)S(1)}, f32[264,128]{1,0:T(8,128)S(1)}, u32[]{:S(2)}, u32[]{:S(2)}) collective-permute-start(f32[264,128]{1,0:T(8,128)S(1)} %get-tuple-element.54), channel_id=1, source_target_pairs={{0,256},{128,384},{256,0},{384,128},{1,257},{129,385},{257,1},{385... | collective-permute-start | bytes 405512 | tf_op jit(solution)/shard_map/ppermute | solution.py:278
  76.9 9.9 %collective-permute-start.21 = (f32[264,128]{1,0:T(8,128)S(1)}, f32[264,128]{1,0:T(8,128)S(1)}, u32[]{:S(2)}, u32[]{:S(2)}) collective-permute-start(f32[264,128]{1,0:T(8,128)S(1)} %get-tuple-element.55), channel_id=1, source_target_pairs={{0,384},{128,0},{256,128},{384,256},{1,385},{129,1},{257,129},{385... | collective-permute-start | bytes 405512 | tf_op jit(solution)/shard_map/ppermute | solution.py:278

commit v11 on v9

--- a/solution.py
+++ b/solution.py
@@ -269,6 +269,12 @@
     return lax.all_to_all(value, "z", 0, 0, tiled=True)
 
 
+def from_ring(value, ahead):
+    ring = [place % 4 * 4 + place // 4 for place in range(16)]
+    pairs = [(ring[(place + ahead) % 16], ring[place]) for place in range(16)]
+    return lax.ppermute(value, ("z", "pb"), pairs)
+
+
 def in_hbm(value):
     return pltpu.with_memory_space_constraint(value, pltpu.HBM)
 
@@ -294,11 +300,9 @@
     frequency,
 ):
     along_z, along_y, along_x, core = (lax.axis_index(name) for name in KA)
-    planes = [gauge]
-    for ahead in (1, 2, 15):
-        ring = [place % 4 * 4 + place // 4 for place in range(16)]
-        pairs = [(ring[(place + ahead) % 16], ring[place]) for place in range(16)]
-        planes.append(lax.ppermute(gauge, ("z", "pb"), pairs))
+    after = from_ring(gauge, 1)
+    before = from_ring(gauge, 15)
+    planes = [gauge, after, from_ring(after, 1), before]
     planes = jnp.stack(planes)
     products, number, target = call(
         right_kernel,

time: 112 us -> 115 us (1.027)
  starting transfers between devices: 54.6 us -> 58.6 us
  waiting for transfers between devices: 22.6 us -> 20.7 us
    ppermute x3, starting transfers between devices: 15.8 us -> 20 us  [from_ring(): return lax.ppermute(value, ('z', 'pb'), pairs)]
    ppermute x3, waiting for transfers between devices: 2.6 us -> 0.66 us  [from_ring(): return lax.ppermute(value, ('z', 'pb'), pairs)]
  transfers between devices with their start and end apart: 11 -> 11, of which waited for: 6 -> 5; matrix products, arithmetic and copies ran while one was open for 0% -> 0% of each run, Pallas kernels for 2% -> 2%
where the time goes in v11:
time: 115 us; the launch traced here: 113 us
  starting transfers between devices  58.6 us (51%)
  blocking collectives  22.1 us (19%)
  waiting for transfers between devices  20.7 us (18%)
  Pallas kernels  10.2 us (9%)
    all_to_all x1, blocking collectives, shards(): terms = lax.all_to_all(terms, ('z', 'pb'), 0, 0, tiled=True)  22.1 us
    ppermute x3, starting transfers between devices, from_ring(): return lax.ppermute(value, ('z', 'pb'), pairs)  20 us
    all_to_all x1, waiting for transfers between devices, shards(): lax.all_to_all(pieces.reshape(32, 32, LANES), ('y', 'x', 'core'), 0, 0, t...  9.66 us
    ppermute x3, starting transfers between devices, shifted(): arrived.append(lax.ppermute(values[shift], 'z', pairs))  9 us
    all_to_all x1, starting transfers between devices, shards(): lax.all_to_all(pieces.reshape(32, 32, LANES), ('y', 'x', 'core'), 0, 0, t...  8.31 us
    all_to_all x1, starting transfers between devices, spread(): return lax.all_to_all(value, 'z', 0, 0, tiled=True)  6.57 us
    ppermute x3, waiting for transfers between devices, shifted(): arrived.append(lax.ppermute(values[shift], 'z', pairs))  5.92 us
    ppermute x1, starting transfers between devices, translated(): return lax.ppermute(value, ('y', 'x'), pairs)  5.67 us
  transfers between devices with their start and end apart: 11, of which 5 were waited for; matrix products, arithmetic and copies ran while one was open for 0% of the time, Pallas kernels for 2%

profile of v11, /device:TPU:1, one launch (start us, length us, event | category | flops | bytes accessed | tf_op | source)
XLA Modules:
  0.0 113.3 jit_solution(3124612830300513050)
XLA Ops:
  0.0 0.7 copy-done
  0.7 2.3 %shard_map.110 = (f32[4,2,2,64,128]{4,3,2,1,0:T(8,128)}, s32[1]{0:T(128)}, s32[1]{0:T(128)}) custom-call(f32[2,4,2,64,128]{4,3,2,1,0:T(8,128)} %coupling.1, f32[2,64,128]{2,1,0:T(8,128)} %gauge.1, s32[2,16]{1,0:T(2,128)S(1)} %bitcast.10), custom_call_target="tpu_custom_call" | custom-call | flops 134217728 | bytes 1048576 | tf_op jit(solution)/shard_map/pallas_call | solution.py:307
  3.0 0.0 copy-start.1
  3.0 6.6 %all-to-all-start = ((f32[4,2,2,64,128]{4,3,2,1,0:T(8,128)}), f32[4,2,2,64,128]{4,3,2,1,0:T(8,128)S(1)}, u32[]{:S(2)}, u32[]{:S(2)}) async-start(f32[4,2,2,64,128]{4,3,2,1,0:T(8,128)} %get-tuple-element.51), calls=%async_computation | async-start | bytes 1048576 | tf_op jit(solution)/shard_map/all_to_all | solution.py:269
  9.6 10.6 %collective-permute-start.15 = (f32[2,64,128]{2,1,0:T(8,128)S(1)}, f32[2,64,128]{2,1,0:T(8,128)S(1)}, u32[]{:S(2)}, u32[]{:S(2)}) collective-permute-start(f32[2,64,128]{2,1,0:T(8,128)S(1)} %copy-done.1), channel_id=1, source_target_pairs={{128,0},{256,128},{384,256},{1,384},{129,1},{257,129},{385,257},{2... | collective-permute-start | bytes 196616 | tf_op jit(solution)/shard_map/ppermute | solution.py:275
  20.1 1.9 %collective-permute-start.17 = (f32[2,64,128]{2,1,0:T(8,128)S(1)}, f32[2,64,128]{2,1,0:T(8,128)S(1)}, u32[]{:S(2)}, u32[]{:S(2)}) collective-permute-start(f32[2,64,128]{2,1,0:T(8,128)S(1)} %copy-done.1), channel_id=1, source_target_pairs={{387,0},{0,128},{128,256},{256,384},{384,1},{1,129},{129,257},{257... | collective-permute-start | bytes 196616 | tf_op jit(solution)/shard_map/ppermute | solution.py:275
  22.0 0.0 collective-permute-done.15
  22.1 7.6 %collective-permute-start.16 = (f32[2,64,128]{2,1,0:T(8,128)S(1)}, f32[2,64,128]{2,1,0:T(8,128)S(1)}, u32[]{:S(2)}, u32[]{:S(2)}) collective-permute-start(f32[2,64,128]{2,1,0:T(8,128)S(1)} %collective-permute-done.15), channel_id=1, source_target_pairs={{128,0},{256,128},{384,256},{1,384},{129,1},{257,129},{385,257},{2... | collective-permute-start | bytes 196616 | tf_op jit(solution)/shard_map/ppermute | solution.py:275
  30.3 0.0 collective-permute-done.17
  30.3 0.7 collective-permute-done.16
  30.9 9.0 %conditional.1 = (f32[4,2,64,128]{3,2,1,0:T(8,128)S(1)}) conditional(s32[]{:T(128)} %bitcast.1, f32[4,2,64,128]{3,2,1,0:T(8,128)S(1)} %pad_maximum_fusion, f32[4,2,64,128]{3,2,1,0:T(8,128)S(1)} %pad_maximum_fusion, f32[4,2,64,128]{3,2,1,0:T(8,128)S(1)} %pad_maximum_fusion, ...), branch_computations={%region_0.0_spmd, %region_1.0_spmd, %region_2.0_spmd, %region_3.0_... | conditional | bytes 1572912 | solution.py:316
  31.0 5.7 %collective-permute-start.1 = (f32[4,2,64,128]{3,2,1,0:T(8,128)S(1)}, f32[4,2,64,128]{3,2,1,0:T(8,128)S(1)}, u32[]{:S(2)}, u32[]{:S(2)}) collective-permute-start(f32[4,2,64,128]{3,2,1,0:T(8,128)S(1)} %param.2), channel_id=1, source_target_pairs={{16,0},{24,8},{32,16},{40,24},{48,32},{56,40},{0,48},{8,56},{80,64... | collective-permute-start | bytes 786440 | tf_op jit(solution)/shard_map/cond/branch_2_fun/ppermute | solution.py:77
  36.7 3.3 %collective-permute-done.1 = f32[4,2,64,128]{3,2,1,0:T(8,128)S(1)} collective-permute-done((f32[4,2,64,128]{3,2,1,0:T(8,128)S(1)}, f32[4,2,64,128]{3,2,1,0:T(8,128)S(1)}, u32[]{:S(2)}, u32[]{:S(2)}) %collective-permute-start.1) | collective-permute-done | bytes 262176 | tf_op jit(solution)/shard_map/cond/branch_2_fun/ppermute | solution.py:77
  40.0 5.1 %collective-permute-start.18 = (f32[4,2,64,128]{3,2,1,0:T(8,128)S(1)}, f32[4,2,64,128]{3,2,1,0:T(8,128)S(1)}, u32[]{:S(2)}, u32[]{:S(2)}) collective-permute-start(f32[4,2,64,128]{3,2,1,0:T(8,128)S(1)} %get-tuple-element.56.kept), channel_id=1, source_target_pairs={{0,4},{4,0},{1,5},{5,1},{2,6},{6,2},{3,7},{7,3},{8,12},{12,8},{9,1... | collective-permute-start | bytes 786440 | tf_op jit(solution)/shard_map/ppermute | solution.py:317
  45.1 1.1 %collective-permute-done.18.swapped = f32[4,2,64,128]{3,2,1,0:T(8,128)S(1)} collective-permute-done((f32[4,2,64,128]{3,2,1,0:T(8,128)S(1)}, f32[4,2,64,128]{3,2,1,0:T(8,128)S(1)}, u32[]{:S(2)}, u32[]{:S(2)}) %collective-permute-start.18) | collective-permute-done | bytes 262176 | tf_op jit(solution)/shard_map/ppermute | solution.py:317
  46.3 0.0 all-to-all-done.products
  46.3 2.1 %shard_map.111 = f32[1024,128]{1,0:T(8,128)} custom-call(s32[1]{0:T(128)} %get-tuple-element.49.target, f32[4,2,64,128]{3,2,1,0:T(8,128)S(1)} %get-tuple-element.56.kept, f32[4,2,64,128]{3,2,1,0:T(8,128)S(1)} %collective-permute-done.18.swapped, f32[4,2,2,64,128]{4,3,2,1,0:T(8,128)S(1)} %all-to-all-done.products), custom_call_target="tpu_custom_call" | custom-call | flops 134217728 | bytes 1048576 | tf_op jit(solution)/shard_map/pallas_call | solution.py:337
  48.3 8.3 %all-to-all-start.1 = ((f32[32,32,128]{2,1,0:T(8,128)}), f32[32,32,128]{2,1,0:T(8,128)S(1)}, u32[]{:S(2)}, u32[]{:S(2)}) async-start(f32[32,32,128]{2,1,0:T(8,128)} %bitcast.6), calls=%async_computation.1 | async-start | bytes 1048576 | tf_op jit(solution)/shard_map/all_to_all | solution.py:340
  56.6 1.8 %shard_map.109 = (bf16[512,256]{1,0:T(8,128)(2,1)S(1)}, bf16[512,256]{1,0:T(8,128)(2,1)S(1)}, f32[264,128]{1,0:T(8,128)S(1)}, f32[264,128]{1,0:T(8,128)S(1)}, f3...) custom-call(s32[3,256]{1,0:T(4,128)} %coords.1, bf16[3,96,512]{2,1,0:T(8,128)(2,1)} %constant.8.clone.tables, ...), custom_call_target="tpu_custom_call" | custom-call | flops 1048576 | bytes 1048576 | tf_op jit(solution)/shard_map/pallas_call | solution.py:318
  58.4 9.7 %all-to-all-done.1.columns = f32[32,32,128]{2,1,0:T(8,128)S(1)} async-done(((f32[32,32,128]{2,1,0:T(8,128)}), f32[32,32,128]{2,1,0:T(8,128)S(1)}, u32[]{:S(2)}, u32[]{:S(2)}) %all-to-all-start.1) | async-done | bytes 524320 | tf_op jit(solution)/shard_map/all_to_all | solution.py:340
  68.1 1.7 %shard_map.112 = f32[32,4,8,128]{3,2,1,0:T(8,128)} custom-call(bf16[512,256]{1,0:T(8,128)(2,1)S(1)} %get-tuple-element.47.high, bf16[512,256]{1,0:T(8,128)(2,1)S(1)} %get-tuple-element.48.low, f32[32,32,128]{2,1,0:T(8,128)S(1)} %all-to-all-done.1.columns), custom_call_target="tpu_custom_call" | custom-call | flops 268435456 | bytes 1048576 | tf_op jit(solution)/shard_map/pallas_call | solution.py:343
  69.8 3.9 %all-to-all-start.2 = ((f32[32,32,128]{2,1,0:T(8,128)}), f32[32,32,128]{2,1,0:T(8,128)S(1)}, u32[]{:S(2)}, u32[]{:S(2)}) async-start(f32[32,32,128]{2,1,0:T(8,128)} %bitcast.7), calls=%async_computation.2 | async-start | bytes 1048576 | tf_op jit(solution)/shard_map/all_to_all | solution.py:351
  73.7 1.9 %collective-permute-start.19 = (f32[264,128]{1,0:T(8,128)S(1)}, f32[264,128]{1,0:T(8,128)S(1)}, u32[]{:S(2)}, u32[]{:S(2)}) collective-permute-start(f32[264,128]{1,0:T(8,128)S(1)} %get-tuple-element.53), channel_id=1, source_target_pairs={{0,128},{128,256},{256,384},{384,0},{1,129},{129,257},{257,385},{3... | collective-permute-start | bytes 405512 | tf_op jit(solution)/shard_map/ppermute | solution.py:286
  75.6 0.0 copy-start.2
  75.6 1.9 %collective-permute-start.20 = (f32[264,128]{1,0:T(8,128)S(1)}, f32[264,128]{1,0:T(8,128)S(1)}, u32[]{:S(2)}, u32[]{:S(2)}) collective-permute-start(f32[264,128]{1,0:T(8,128)S(1)} %get-tuple-element.54), channel_id=1, source_target_pairs={{0,256},{128,384},{256,0},{384,128},{1,257},{129,385},{257,1},{385... | collective-permute-start | bytes 405512 | tf_op jit(solution)/shard_map/ppermute | solution.py:286
  77.6 5.2 %collective-permute-start.21 = (f32[264,128]{1,0:T(8,128)S(1)}, f32[264,128]{1,0:T(8,128)S(1)}, u32[]{:S(2)}, u32[]{:S(2)}) collective-permute-start(f32[264,128]{1,0:T(8,128)S(1)} %get-tuple-element.55), channel_id=1, source_target_pairs={{0,384},{128,0},{256,128},{384,256},{1,385},{129,1},{257,129},{385... | collective-permute-start | bytes 405512 | tf_op jit(solution)/shard_map/ppermute | solution.py:286
  82.7 0.1 copy.12.frequency
  82.8 5.9 %collective-permute-done.20.packs_and_out_2_ = f32[264,128]{1,0:T(8,128)S(1)} collective-permute-done((f32[264,128]{1,0:T(8,128)S(1)}, f32[264,128]{1,0:T(8,128)S(1)}, u32[]{:S(2)}, u32[]{:S(2)}) %collective-permute-start.20) | collective-permute-done | bytes 135200 | tf_op jit(solution)/shard_map/ppermute | solution.py:286
  88.8 0.0 collective-permute-done.21.packs_and_out_3_
  88.8 1.8 %shard_map.113 = f32[16,1,128]{2,1,0:T(1,128)S(1)} custom-call(f32[4,2]{1,0:T(4,128)S(1)} %copy.12.frequency, f32[1024,128]{1,0:T(8,128)S(1)} %bitcast.9, f32[264,128]{1,0:T(8,128)S(1)} %get-tuple-element.52.packs_and_out_0_, f32[264,128]{1,0:T(8,128)S(1)} %collective-permute-done.19.packs_and_out_1_, ...), custom_call_target="tpu_custom_call" | custom-call | flops 134217728 | bytes 1048576 | tf_op jit(solution)/shard_map/pallas_call | solution.py:354
  90.6 22.1 %all_to_all.20.terms = f32[16,1,128]{2,1,0:T(1,128)S(1)} all-to-all(f32[16,1,128]{2,1,0:T(1,128)S(1)} %shard_map.113), channel_id=1, replica_groups=mesh['z'=4,'y'=4,'x'=4,'core'=2,'pb'=4] {'z','pb'}, dimensions={0} | all-to-all | bytes 16384 | tf_op jit(solution)/shard_map/all_to_all | solution.py:357
  112.6 0.6 shard_map.114
  (7 shorter events, 0.0 us)
Async XLA Ops:
  0.0 0.7 copy-start
  3.0 6.6 %copy-start.1 = (f32[2,64,128]{2,1,0:T(8,128)S(1)}, f32[2,64,128]{2,1,0:T(8,128)}, u32[]{:S(2)}) copy-start(f32[2,64,128]{2,1,0:T(8,128)} %gauge.1) | copy-start | bytes 196612
  3.0 43.3 %all-to-all-start = ((f32[4,2,2,64,128]{4,3,2,1,0:T(8,128)}), f32[4,2,2,64,128]{4,3,2,1,0:T(8,128)S(1)}, u32[]{:S(2)}, u32[]{:S(2)}) async-start(f32[4,2,2,64,128]{4,3,2,1,0:T(8,128)} %get-tuple-element.51), calls=%async_computation | async-start | bytes 1048576 | tf_op jit(solution)/shard_map/all_to_all | solution.py:269
  9.6 12.5 %collective-permute-start.15 = (f32[2,64,128]{2,1,0:T(8,128)S(1)}, f32[2,64,128]{2,1,0:T(8,128)S(1)}, u32[]{:S(2)}, u32[]{:S(2)}) collective-permute-start(f32[2,64,128]{2,1,0:T(8,128)S(1)} %copy-done.1), channel_id=1, source_target_pairs={{128,0},{256,128},{384,256},{1,384},{129,1},{257,129},{385,257},{2... | collective-permute-start | bytes 196616 | tf_op jit(solution)/shard_map/ppermute | solution.py:275
  20.1 10.2 %collective-permute-start.17 = (f32[2,64,128]{2,1,0:T(8,128)S(1)}, f32[2,64,128]{2,1,0:T(8,128)S(1)}, u32[]{:S(2)}, u32[]{:S(2)}) collective-permute-start(f32[2,64,128]{2,1,0:T(8,128)S(1)} %copy-done.1), channel_id=1, source_target_pairs={{387,0},{0,128},{128,256},{256,384},{384,1},{1,129},{129,257},{257... | collective-permute-start | bytes 196616 | tf_op jit(solution)/shard_map/ppermute | solution.py:275
  22.1 8.9 %collective-permute-start.16 = (f32[2,64,128]{2,1,0:T(8,128)S(1)}, f32[2,64,128]{2,1,0:T(8,128)S(1)}, u32[]{:S(2)}, u32[]{:S(2)}) collective-permute-start(f32[2,64,128]{2,1,0:T(8,128)S(1)} %collective-permute-done.15), channel_id=1, source_target_pairs={{128,0},{256,128},{384,256},{1,384},{129,1},{257,129},{385,257},{2... | collective-permute-start | bytes 196616 | tf_op jit(solution)/shard_map/ppermute | solution.py:275
  31.0 9.0 %collective-permute-start.1 = (f32[4,2,64,128]{3,2,1,0:T(8,128)S(1)}, f32[4,2,64,128]{3,2,1,0:T(8,128)S(1)}, u32[]{:S(2)}, u32[]{:S(2)}) collective-permute-start(f32[4,2,64,128]{3,2,1,0:T(8,128)S(1)} %param.2), channel_id=1, source_target_pairs={{16,0},{24,8},{32,16},{40,24},{48,32},{56,40},{0,48},{8,56},{80,64... | collective-permute-start | bytes 786440 | tf_op jit(solution)/shard_map/cond/branch_2_fun/ppermute | solution.py:77
  40.0 6.3 %collective-permute-start.18 = (f32[4,2,64,128]{3,2,1,0:T(8,128)S(1)}, f32[4,2,64,128]{3,2,1,0:T(8,128)S(1)}, u32[]{:S(2)}, u32[]{:S(2)}) collective-permute-start(f32[4,2,64,128]{3,2,1,0:T(8,128)S(1)} %get-tuple-element.56.kept), channel_id=1, source_target_pairs={{0,4},{4,0},{1,5},{5,1},{2,6},{6,2},{3,7},{7,3},{8,12},{12,8},{9,1... | collective-permute-start | bytes 786440 | tf_op jit(solution)/shard_map/ppermute | solution.py:317
  48.3 19.7 %all-to-all-start.1 = ((f32[32,32,128]{2,1,0:T(8,128)}), f32[32,32,128]{2,1,0:T(8,128)S(1)}, u32[]{:S(2)}, u32[]{:S(2)}) async-start(f32[32,32,128]{2,1,0:T(8,128)} %bitcast.6), calls=%async_computation.1 | async-start | bytes 1048576 | tf_op jit(solution)/shard_map/all_to_all | solution.py:340
  69.8 19.0 %all-to-all-start.2 = ((f32[32,32,128]{2,1,0:T(8,128)}), f32[32,32,128]{2,1,0:T(8,128)S(1)}, u32[]{:S(2)}, u32[]{:S(2)}) async-start(f32[32,32,128]{2,1,0:T(8,128)} %bitcast.7), calls=%async_computation.2 | async-start | bytes 1048576 | tf_op jit(solution)/shard_map/all_to_all | solution.py:351
  73.7 9.1 %collective-permute-start.19 = (f32[264,128]{1,0:T(8,128)S(1)}, f32[264,128]{1,0:T(8,128)S(1)}, u32[]{:S(2)}, u32[]{:S(2)}) collective-permute-start(f32[264,128]{1,0:T(8,128)S(1)} %get-tuple-element.53), channel_id=1, source_target_pairs={{0,128},{128,256},{256,384},{384,0},{1,129},{129,257},{257,385},{3... | collective-permute-start | bytes 405512 | tf_op jit(solution)/shard_map/ppermute | solution.py:286
  75.6 7.1 %copy-start.2 = (f32[4,2]{0,1:T(2,128)S(1)}, f32[4,2]{0,1:T(2,128)}, u32[]{:S(2)}) copy-start(f32[4,2]{0,1:T(2,128)} %param.36) | copy-start | bytes 100
  75.6 13.1 %collective-permute-start.20 = (f32[264,128]{1,0:T(8,128)S(1)}, f32[264,128]{1,0:T(8,128)S(1)}, u32[]{:S(2)}, u32[]{:S(2)}) collective-permute-start(f32[264,128]{1,0:T(8,128)S(1)} %get-tuple-element.54), channel_id=1, source_target_pairs={{0,256},{128,384},{256,0},{384,128},{1,257},{129,385},{257,1},{385... | collective-permute-start | bytes 405512 | tf_op jit(solution)/shard_map/ppermute | solution.py:286
  77.6 11.2 %collective-permute-start.21 = (f32[264,128]{1,0:T(8,128)S(1)}, f32[264,128]{1,0:T(8,128)S(1)}, u32[]{:S(2)}, u32[]{:S(2)}) collective-permute-start(f32[264,128]{1,0:T(8,128)S(1)} %get-tuple-element.55), channel_id=1, source_target_pairs={{0,384},{128,0},{256,128},{384,256},{1,385},{129,1},{257,129},{385... | collective-permute-start | bytes 405512 | tf_op jit(solution)/shard_map/ppermute | solution.py:286
